TPU v7x, 32 devices: a whole 2x2x4 slice. The times are simulated.
32 devices in a mesh: ens: 4 (over x, core), lat: 8 (over z, y).
Axes of the slice: x: 2, y: 2, z: 4, core: 2. Of those that a mesh axis runs over, the one named last changes fastest.
Arguments:
- fields: bfloat16 [8, 24, 48, 1440], P('ens', None, 'lat'), may hold values from -6 to 6
- depth_kernel: float32 [24, 7, 7], replicated, may hold values from -0.875 to 0.875
- mix_weight: bfloat16 [24, 24], replicated, may hold values from -1.25 to 1.25
- legendre: bfloat16 [48, 160, 160], P('lat'), may hold values from -1.25 to 1.25
- truth: bfloat16 [24, 2, 160, 160], replicated, may hold values from -6 to 6
- degree_order: int32 [160], replicated, may hold values from 0 to 159, each once
Outputs:
- grad_fields: bfloat16 [8, 24, 48, 1440], P('ens', None, 'lat')
- score_grad: float32 [8, 24, 2, 160, 160], P('ens', None, None, None, 'lat')
Inputs may be any that keep to these rules, and one draw needn't show every extreme that they name: `degree_order`: each degree appears once.
All inputs are finite; a program needn't handle non-finite values.
Results may differ from a plain program's by a relative error of at most 0.02.
Values may be sent and summed in bfloat16 or wider, within the bound.
No kernel may reach another device: no remote copies, remote signals or barrier semaphores. Data moves between devices by JAX's collectives and lax.ppermute only.
A program may use at most 128 MiB of HBM per device.

v0:
```python
import functools
import math

import jax
import jax.numpy as jnp
import numpy as np
from jax import lax
from jax.experimental import pallas as pl
from jax.experimental.pallas import tpu as pltpu
from jax.sharding import PartitionSpec as P

smooth_width = 0.5
LEAD = 8
F32 = jnp.float32
BF16 = jnp.bfloat16


def up(value, step):
    return -(-value // step) * step


def full(shape):
    return pl.BlockSpec(shape, lambda *_: (0,) * len(shape), memory_space=pltpu.VMEM)


def wave_table(nlon, orders, groups, order_pad):
    share = orders // groups
    columns = np.arange(nlon, dtype=np.int64)
    number = np.arange(orders, dtype=np.int64)
    angles = (columns[:, None] * number[None, :] % nlon) * (2.0 * math.pi / nlon)
    table = np.zeros((nlon, 2, groups, order_pad), np.float32)
    for part, values in enumerate((np.cos(angles), -np.sin(angles))):
        table[:, part, :, :share] = (values / math.sqrt(nlon)).reshape(nlon, groups, share)
    return table.reshape(nlon, 2 * groups * order_pad).astype(jnp.bfloat16)


def neighbours(block, width):
    count = lax.axis_size("lat")
    forward = [(i, i + 1) for i in range(count - 1)]
    backward = [(target, source) for source, target in forward]
    low = lax.ppermute(block[:, block.shape[1] - width :], "lat", forward)
    high = lax.ppermute(block[:, :width], "lat", backward)
    return low, high


def convolve(own, low, high, taps, padded, emit):
    members, rows, chans, nlon = own.shape
    wide = padded.shape[-1]
    pad = low.shape[1]

    def fill(row, value):
        value = value.astype(F32)
        ext = jnp.concatenate(
            [value[:, nlon - LEAD :], value, value[:, : wide - nlon - LEAD]], axis=-1
        )
        padded[row] = ext

    @pl.loop(0, members)
    def _(b):
        for row in range(pad):
            fill(row, low[b, row])
            fill(row + pad + rows, high[b, row])
        for row in range(rows):
            fill(row + pad, own[b, row])

        @pl.loop(0, chans // 8)
        def _(ct):
            c0 = pl.multiple_of(ct * 8, 8)

            @pl.loop(0, rows)
            def _(i):
                total = None
                for q in range(7):
                    part = None
                    for p in range(7):
                        weight = jnp.tile(taps[p * 7 + q, pl.ds(c0, 8), :], (1, wide // 128))
                        term = weight * padded[i + p, pl.ds(c0, 8), :]
                        part = term if part is None else part + term
                    if q != 3:
                        part = pltpu.roll(part, (3 - q) % wide, 1)
                    total = part if total is None else total + part
                emit(b, i, c0, total[:, LEAD : LEAD + nlon])


def gelu_pair(x):
    scale = math.sqrt(2.0 / math.pi)
    square = x * x
    t = jnp.tanh(scale * x * (1.0 + 0.044715 * square))
    half = 0.5 * (1.0 + t)
    slope = half + 0.5 * x * (1.0 - t * t) * (scale * (1.0 + 3 * 0.044715 * square))
    return x * half, slope


def forward_kernel(own, low, high, taps, table, mixer, out, slope, padded, act):
    members, rows, chans, nlon = own.shape
    owners, groups, order_pad, lanes = out.shape

    def emit(b, i, c0, value):
        value, grad = gelu_pair(value)
        act[b, i, pl.ds(c0, 8), :] = value
        slope[b, i, pl.ds(c0, 8), :] = grad

    convolve(own, low, high, taps, padded, emit)
    rows_all = members * rows * chans
    flat = act[...].reshape(rows_all, nlon).astype(BF16)
    spectral = jnp.dot(flat, table[...], preferred_element_type=F32).astype(BF16)
    half = groups * order_pad
    mixed = None
    for r in range(2):
        part = lax.dot_general(
            spectral[:, r * half : (r + 1) * half],
            mixer[r],
            (((0,), (0,)), ((), ())),
            preferred_element_type=F32,
        )
        mixed = part if mixed is None else mixed + part
    for e in range(owners):
        out[e] = mixed[:, e * lanes : (e + 1) * lanes].reshape(groups, order_pad, lanes).astype(BF16)


def soft_sign(gaps):
    return gaps * lax.rsqrt(gaps * gaps + smooth_width * smooth_width)


def score_kernel(rows, got, legendre, target, order, back, grads, spread, gather):
    owners, groups, order_pad, lanes = got.shape
    orders, nlat, degrees = legendre.shape
    slots = target.shape[1]
    ens = spread.shape[1] // slots
    local = ens // owners
    width = local * slots
    for t in range(groups):
        for i in range(rows):
            pieces = [got[e, t, :, i * width : (i + 1) * width] for e in range(owners)]
            at = (t * rows + i) * order_pad
            spread[at : at + order_pad, :] = jnp.concatenate(pieces, axis=-1).astype(F32)
    gather[...] = jnp.zeros(gather.shape, F32)

    @pl.loop(0, orders)
    def _(m):
        block = spread[pl.ds(m, nlat, stride=order_pad), :].astype(BF16)
        leg = legendre[m]
        coeff = lax.dot_general(
            block, leg, (((0,), (0,)), ((), ())), preferred_element_type=F32
        )
        own = [coeff[k * slots : (k + 1) * slots] for k in range(ens)]
        truth = target[m].astype(F32)
        sums = [None] * ens
        for k in range(ens):
            for n in range(k + 1, ens):
                sign = soft_sign(own[k] - own[n])
                sums[k] = sign if sums[k] is None else sums[k] + sign
                sums[n] = -sign if sums[n] is None else sums[n] - sign
        grad = jnp.concatenate(
            [
                soft_sign(own[k] - truth) * (1.0 / ens) - sums[k] * (1.0 / (ens * (ens - 1)))
                for k in range(ens)
            ],
            axis=0,
        ).astype(BF16)
        spec = lax.dot_general(
            leg, grad, (((1,), (1,)), ((), ())), preferred_element_type=F32
        )
        gather[pl.ds(m, nlat, stride=order_pad), :] = spec
        grads[m] = jnp.dot(grad, order[...], preferred_element_type=F32).astype(BF16)

    for t in range(groups):
        for e in range(owners):
            pieces = []
            for i in range(rows):
                at = (t * rows + i) * order_pad
                pieces.append(gather[at : at + order_pad, e * width : (e + 1) * width])
            if lanes > rows * width:
                pieces.append(jnp.zeros((order_pad, lanes - rows * width), F32))
            back[e, t] = jnp.concatenate(pieces, axis=-1).astype(BF16)


def backward_kernel(got, mixer, table, slope, out, flat):
    owners, groups, order_pad, lanes = got.shape
    members, rows, chans, nlon = slope.shape
    half = groups * order_pad
    spectra = jnp.concatenate(
        [got[e].reshape(half, lanes) for e in range(owners)], axis=-1
    )
    parts = []
    for r in range(2):
        parts.append(
            lax.dot_general(
                mixer[r], spectra, (((1,), (1,)), ((), ())), preferred_element_type=F32
            ).astype(BF16)
        )
    unmixed = jnp.concatenate(parts, axis=-1)
    flat[...] = lax.dot_general(
        unmixed, table[...], (((1,), (1,)), ((), ())), preferred_element_type=F32
    ).reshape(flat.shape)
    for b in range(members):
        for i in range(rows):
            out[b, i] = (flat[b, i] * slope[b, i]).astype(BF16)


def convolve_kernel(own, low, high, taps, out, padded, stage):
    members, rows, chans, nlon = own.shape

    def emit(b, i, c0, value):
        stage[b, i, pl.ds(c0, 8), :] = value

    convolve(own, low, high, taps, padded, emit)
    out[...] = stage[...].astype(BF16)


def tap_planes(kernel):
    chans, size, _ = kernel.shape
    planes = kernel.transpose(1, 2, 0).reshape(size * size, chans)
    planes = planes.at[(size * size) // 2].add(1.0)
    return jnp.broadcast_to(planes[:, :, None], (size * size, chans, 128))


def local(fields, depth_kernel, mix_weight, legendre, truth, degree_order):
    ens_parts, groups = lax.axis_size("ens"), lax.axis_size("lat")
    ens_at, lat_at = lax.axis_index("ens"), lax.axis_index("lat")
    members, chans, rows, nlon = fields.shape
    _, orders, degrees = legendre.shape
    ens = members * ens_parts
    nlat = rows * groups
    share, per_owner, chan_share = orders // groups, degrees // groups, chans // ens_parts
    order_pad = up(share, 8)
    slots = up(2 * chan_share, 8)
    lanes = up(rows * members * slots, 128)
    wide = up(nlon + 2 * LEAD, 128)
    halo = depth_kernel.shape[1] // 2

    table = jnp.asarray(wave_table(nlon, orders, groups, order_pad))
    own = fields.transpose(0, 2, 1, 3)
    low, high = neighbours(own, halo)

    picked = mix_weight.reshape(ens_parts, chan_share, chans)
    slotted = jnp.stack(
        [
            jnp.pad(picked, ((0, 0), (r * chan_share, slots - (r + 1) * chan_share), (0, 0)))
            for r in range(2)
        ]
    )
    same_row = jnp.asarray(np.eye(rows), BF16)
    same_member = jnp.asarray(np.eye(members), BF16)
    mixer = jnp.einsum("reoc,ij,bd->rbicejdo", slotted, same_row, same_member)
    mixer = mixer.reshape(2, members * rows * chans, ens_parts, rows * members * slots)
    mixer = jnp.pad(mixer, ((0, 0), (0, 0), (0, 0), (0, lanes - rows * members * slots)))
    mixer = mixer.reshape(2, members * rows * chans, ens_parts * lanes).astype(BF16)

    order_legendre = lax.all_to_all(legendre, "lat", split_axis=1, concat_axis=0, tiled=True)
    order_legendre = order_legendre.transpose(1, 0, 2)
    target = lax.dynamic_slice(
        truth, (ens_at * chan_share, 0, lat_at * share, 0), (chan_share, 2, share, degrees)
    )
    target = target.transpose(2, 1, 0, 3).reshape(share, 2 * chan_share, degrees)
    target = jnp.pad(target, ((0, 0), (0, slots - 2 * chan_share), (0, 0)))
    reorder = (jnp.arange(degrees)[:, None] == degree_order[None, :]).astype(BF16)

    vmem = pltpu.CompilerParams(vmem_limit_bytes=60 * 1024 * 1024)
    grid_shape = (members, rows, chans, nlon)
    chunk = jax.ShapeDtypeStruct((ens_parts, groups, order_pad, lanes), BF16)
    sent, slope = pl.pallas_call(
        forward_kernel,
        out_shape=(chunk, jax.ShapeDtypeStruct(grid_shape, F32)),
        scratch_shapes=[
            pltpu.VMEM((rows + 2 * halo, chans, wide), F32),
            pltpu.VMEM(grid_shape, F32),
        ],
        compiler_params=vmem,
        name="forward",
    )(own, low, high, tap_planes(depth_kernel), table, mixer)

    def swap(x):
        flat = x.reshape((ens_parts * groups,) + x.shape[2:])
        flat = lax.all_to_all(flat, ("ens", "lat"), split_axis=0, concat_axis=0, tiled=True)
        return flat.reshape(x.shape)

    got = swap(sent)
    back, grads = pl.pallas_call(
        functools.partial(score_kernel, rows),
        out_shape=(chunk, jax.ShapeDtypeStruct((share, ens * slots, degrees), BF16)),
        scratch_shapes=[
            pltpu.VMEM((nlat * order_pad, ens * slots), F32),
            pltpu.VMEM((nlat * order_pad, ens * slots), F32),
        ],
        compiler_params=vmem,
        name="score",
    )(got, order_legendre, target, reorder)
    returned = swap(back)

    hid_grad = pl.pallas_call(
        backward_kernel,
        out_shape=jax.ShapeDtypeStruct(grid_shape, BF16),
        scratch_shapes=[pltpu.VMEM(grid_shape, F32)],
        compiler_params=vmem,
        name="backward",
    )(returned, mixer, table, slope)
    low, high = neighbours(hid_grad, halo)
    grad_fields = pl.pallas_call(
        convolve_kernel,
        out_shape=jax.ShapeDtypeStruct(grid_shape, BF16),
        scratch_shapes=[
            pltpu.VMEM((rows + 2 * halo, chans, wide), F32),
            pltpu.VMEM(grid_shape, F32),
        ],
        compiler_params=vmem,
        name="convolve",
    )(hid_grad, low, high, tap_planes(depth_kernel[:, ::-1, ::-1]))

    grads = grads.reshape(share, ens_parts, members, slots, groups, per_owner)
    grads = grads[:, :, :, : 2 * chan_share].transpose(1, 4, 2, 0, 3, 5)
    grads = grads.reshape(ens_parts, groups, members * share, 2 * chan_share * per_owner)
    grads = swap(grads).reshape(
        ens_parts, groups, members, share, 2, chan_share, per_owner
    )
    score_grad = grads.transpose(2, 0, 5, 4, 1, 3, 6).reshape(
        members, chans, 2, orders, per_owner
    )
    return grad_fields.transpose(0, 2, 1, 3), score_grad.astype(F32)


def solution(mesh):
    placed = (P("ens", None, "lat", None), P(), P(), P("lat", None, None), P(), P())
    return jax.shard_map(
        local,
        mesh=mesh,
        in_specs=placed,
        out_specs=(P("ens", None, "lat", None), P("ens", None, None, None, "lat")),
        check_vma=False,
    )
```

profile of v0, /device:TPU:0, one launch (start us, length us, event | category | flops | bytes accessed | tf_op | source)
XLA Modules:
  0.0 187.6 jit_solution(16562202637177647259)
XLA Ops:
  3.5 7.3 %all-to-all-start.1 = ((bf16[8,2,9600]{2,1,0:T(2,128)(2,1)}), bf16[8,2,9600]{2,1,0:T(2,128)(2,1)S(1)}, u32[]{:S(2)}, u32[]{:S(2)}) async-start(bf16[8,2,9600]{2,1,0:T(2,128)(2,1)} %reshape.106), calls=%async_computation.1 | async-start | bytes 614400 | tf_op jit(solution)/shard_map/all_to_all | solution.py:250
  10.8 2.0 %fusion.2 = (bf16[2,3,24,1440]{3,2,1,0:T(8,128)(2,1)}, bf16[2,3,24,1440]{3,2,1,0:T(8,128)(2,1)S(1)}) fusion(bf16[2,6,24,1440]{3,2,1,0:T(8,128)(2,1)} %bitcast.41), kind=kLoop, calls=%fused_computation.13 | loop fusion | bytes 1658880 | tf_op jit(solution)/shard_map/slice | solution.py:42
  14.1 5.4 %collective-permute-start = (bf16[2,3,24,1440]{3,2,1,0:T(8,128)(2,1)S(1)}, bf16[2,3,24,1440]{3,2,1,0:T(8,128)(2,1)}, u32[]{:S(2)}, u32[]{:S(2)}) collective-permute-start(bf16[2,3,24,1440]{3,2,1,0:T(8,128)(2,1)S(1)} %get-tuple-element.41), channel_id=1, source_target_pairs={{0,1},{1,2},{2,3},{3,4},{4,5},{5,6},{6,7},{8,9},{9,10},{10,11},{11... | collective-permute-start | bytes 1244168 | tf_op jit(solution)/shard_map/ppermute | solution.py:41
  19.6 3.1 %multiply_bitcast_fusion = bf16[2,2,6,24,4,6,2,16]{3,2,1,7,6,5,4,0:T(8,128)(2,1)} fusion(bf16[2,4,16,24]{3,2,1,0:T(8,128)(2,1)S(1)} %pad_maximum_fusion, bf16[2,2,6,6]{2,0,1,3:T(2,128)(2,1)S(1)} %broadcast_multiply_fusion), kind=kLoop, calls=%fused_computation | loop fusion | flops 442368 | bytes 891168 | tf_op jit(solution)/shard_map/reoc,ij,bd->rbicejdo/transpose | solution.py:245
  23.4 7.9 %reshape.95 = bf16[2,288,4,192]{1,3,2,0:T(8,128)(2,1)S(1)} reshape(bf16[2,2,6,24,4,6,2,16]{3,2,1,7,6,5,4,0:T(8,128)(2,1)} %multiply_bitcast_fusion) | data formatting | bytes 1769472 | tf_op jit(solution)/shard_map/reshape | solution.py:246
  34.9 1.9 %collective-permute-done.low = bf16[2,3,24,1440]{3,2,1,0:T(8,128)(2,1)} collective-permute-done((bf16[2,3,24,1440]{3,2,1,0:T(8,128)(2,1)S(1)}, bf16[2,3,24,1440]{3,2,1,0:T(8,128)(2,1)}, u32[]{:S(2)}, u32[]{:S(2)}) %collective-permute-start) | collective-permute-done | bytes 414752 | tf_op jit(solution)/shard_map/ppermute | solution.py:41
  38.6 16.1 %forward.1 = (bf16[4,8,24,256]{3,2,1,0:T(8,128)(2,1)}, f32[2,6,24,1440]{3,2,1,0:T(8,128)}) custom-call(bf16[2,6,24,1440]{3,2,1,0:T(8,128)(2,1)} %bitcast.42, bf16[2,3,24,1440]{3,2,1,0:T(8,128)(2,1)} %collective-permute-done.low, bf16[2,3,24,1440]{3,2,1,0:T(8,128)(2,1)} %collective-permute-done.1.high, f32[49,24,128]{2,1,0:T(8,128)} %broadcast_in_dim.9.taps, ...), custom_call_target="tpu_custom_call" | custom-call | tf_op jit(solution)/shard_map/forward/pallas_call | solution.py:262
  54.7 5.1 %all-to-all-start = ((bf16[32,24,256]{2,1,0:T(8,128)(2,1)}), bf16[32,24,256]{2,1,0:T(8,128)(2,1)S(1)}, u32[]{:S(2)}, u32[]{:S(2)}) async-start(bf16[32,24,256]{2,1,0:T(8,128)(2,1)} %bitcast.51), calls=%async_computation | async-start | bytes 786432 | tf_op jit(solution)/shard_map/all_to_all | solution.py:275
  63.9 9.3 %all-to-all-done = bf16[32,24,256]{2,1,0:T(8,128)(2,1)S(1)} async-done(((bf16[32,24,256]{2,1,0:T(8,128)(2,1)}), bf16[32,24,256]{2,1,0:T(8,128)(2,1)S(1)}, u32[]{:S(2)}, u32[]{:S(2)}) %all-to-all-start) | async-done | bytes 393248 | tf_op jit(solution)/shard_map/all_to_all | solution.py:275
  73.9 12.0 %score.1 = (bf16[4,8,24,256]{3,2,1,0:T(8,128)(2,1)}, bf16[20,128,160]{2,1,0:T(8,128)(2,1)}) custom-call(bf16[4,8,24,256]{3,2,1,0:T(8,128)(2,1)} %bitcast.47, bf16[20,48,160]{2,1,0:T(8,128)(2,1)} %bitcast.46, bf16[20,16,160]{2,1,0:T(8,128)(2,1)} %pad.23.target, bf16[160,160]{1,0:T(8,128)(2,1)} %fusion.order), custom_call_target="tpu_custom_call" | custom-call | tf_op jit(solution)/shard_map/score/pallas_call | solution.py:279
  85.9 2.6 %all-to-all-start.2 = ((bf16[32,24,256]{2,1,0:T(8,128)(2,1)}), bf16[32,24,256]{2,1,0:T(8,128)(2,1)S(1)}, u32[]{:S(2)}, u32[]{:S(2)}) async-start(bf16[32,24,256]{2,1,0:T(8,128)(2,1)} %bitcast.52), calls=%async_computation.2 | async-start | bytes 786432 | tf_op jit(solution)/shard_map/all_to_all | solution.py:275
  88.5 7.2 %reshape.102 = bf16[20,4,2,16,8,20]{5,4,3,2,1,0:T(8,128)(2,1)} reshape(bf16[20,128,160]{2,1,0:T(8,128)(2,1)} %get-tuple-element.33) | data formatting | bytes 1638400 | tf_op jit(solution)/shard_map/reshape | solution.py:310
  95.7 3.1 %slice_bitcast_fusion = bf16[4,8,2,20,12,20]{5,1,4,2,0,3:T(8,128)(2,1)S(1)} fusion(bf16[20,4,2,16,8,20]{5,4,3,2,1,0:T(8,128)(2,1)} %reshape.102), kind=kLoop, calls=%fused_computation.1 | loop fusion | bytes 1228800 | tf_op jit(solution)/shard_map/transpose | solution.py:311
  98.8 3.7 %copy.35 = bf16[4,8,2,20,12,20]{5,4,3,2,1,0:T(8,128)(2,1)} copy(bf16[4,8,2,20,12,20]{5,1,4,2,0,3:T(8,128)(2,1)S(1)} %slice_bitcast_fusion) | data formatting | bytes 1228800 | tf_op jit(solution)/shard_map/transpose | solution.py:311
  102.5 7.1 %reshape_reshape.4 = bf16[32,40,240]{2,1,0:T(8,128)(2,1)} reshape(bf16[4,8,2,20,12,20]{5,4,3,2,1,0:T(8,128)(2,1)} %copy.35) | data formatting | bytes 1228800 | tf_op jit(solution)/shard_map/reshape;reshape | solution.py:274
  109.7 5.8 %all-to-all-start.3 = ((bf16[32,40,240]{2,1,0:T(8,128)(2,1)}), bf16[32,40,240]{2,1,0:T(8,128)(2,1)S(1)}, u32[]{:S(2)}, u32[]{:S(2)}) async-start(bf16[32,40,240]{2,1,0:T(8,128)(2,1)} %reshape_reshape.4), calls=%async_computation.3 | async-start | bytes 1310720 | tf_op jit(solution)/shard_map/all_to_all | solution.py:275
  115.5 4.3 %backward.1.own = bf16[2,6,24,1440]{3,2,1,0:T(8,128)(2,1)} custom-call(bf16[4,8,24,256]{3,2,1,0:T(8,128)(2,1)} %bitcast.48, bf16[2,288,1024]{2,1,0:T(8,128)(2,1)} %copy.38.mixer, bf16[1440,384]{1,0:T(8,128)(2,1)} %constant.79.clone.table, f32[2,6,24,1440]{3,2,1,0:T(8,128)} %get-tuple-element.32.slope), custom_call_target="tpu_custom_call" | custom-call | tf_op jit(solution)/shard_map/backward/pallas_call | solution.py:291
  122.6 4.6 %collective-permute-start.2 = (bf16[2,3,24,1440]{3,2,1,0:T(8,128)(2,1)S(1)}, bf16[2,3,24,1440]{3,2,1,0:T(8,128)(2,1)S(1)}, u32[]{:S(2)}, u32[]{:S(2)}) collective-permute-start(bf16[2,3,24,1440]{3,2,1,0:T(8,128)(2,1)S(1)} %get-tuple-element.39), channel_id=1, source_target_pairs={{0,1},{1,2},{2,3},{3,4},{4,5},{5,6},{6,7},{8,9},{9,10},{10,11},{11... | collective-permute-start | bytes 1244168 | tf_op jit(solution)/shard_map/ppermute | solution.py:41
  127.2 9.6 %collective-permute-done.3.high = bf16[2,3,24,1440]{3,2,1,0:T(8,128)(2,1)S(1)} collective-permute-done((bf16[2,3,24,1440]{3,2,1,0:T(8,128)(2,1)S(1)}, bf16[2,3,24,1440]{3,2,1,0:T(8,128)(2,1)S(1)}, u32[]{:S(2)}, u32[]{:S(2)}) %collective-permute-start.3) | collective-permute-done | bytes 414752 | tf_op jit(solution)/shard_map/ppermute | solution.py:42
  136.8 10.6 %collective-permute-done.2.low = bf16[2,3,24,1440]{3,2,1,0:T(8,128)(2,1)S(1)} collective-permute-done((bf16[2,3,24,1440]{3,2,1,0:T(8,128)(2,1)S(1)}, bf16[2,3,24,1440]{3,2,1,0:T(8,128)(2,1)S(1)}, u32[]{:S(2)}, u32[]{:S(2)}) %collective-permute-start.2) | collective-permute-done | bytes 414752 | tf_op jit(solution)/shard_map/ppermute | solution.py:41
  148.4 13.4 %convolve.1 = bf16[2,6,24,1440]{3,2,1,0:T(8,128)(2,1)} custom-call(bf16[2,6,24,1440]{3,2,1,0:T(8,128)(2,1)} %backward.1.own, bf16[2,3,24,1440]{3,2,1,0:T(8,128)(2,1)} %copy-done.3, bf16[2,3,24,1440]{3,2,1,0:T(8,128)(2,1)} %copy-done.2, f32[49,24,128]{2,1,0:T(8,128)} %broadcast_in_dim.21.taps), custom_call_target="tpu_custom_call" | custom-call | tf_op jit(solution)/shard_map/convolve/pallas_call | solution.py:299
  161.8 6.8 %reshape.104 = f32[4,8,2,20,2,6,20]{6,5,4,3,2,1,0:T(8,128)} reshape(bf16[32,40,240]{2,1,0:T(8,128)(2,1)S(1)} %all-to-all-done.3) | data formatting | bytes 1843200 | tf_op jit(solution)/shard_map/convert_element_type | solution.py:319
  168.6 11.5 %copy.41 = f32[2,4,6,2,8,20,20]{5,4,3,6,2,1,0:T(8,128)} copy(f32[2,4,6,2,8,20,20]{6,2,3,5,0,4,1:T(8,128)} %bitcast.39) | data formatting | bytes 2457600
  180.1 7.6 %reshape.105 = f32[2,24,2,160,20]{3,2,4,1,0:T(2,128)} reshape(f32[2,4,6,2,8,20,20]{5,4,3,6,2,1,0:T(8,128)} %copy.41) | data formatting | bytes 2457600
  (50 shorter events, 19.0 us)
Async XLA Ops:
  0.6 18.9 %copy-start.8 = (bf16[2,2]{0,1:T(2,128)(2,1)S(1)}, bf16[2,2]{0,1:T(2,128)(2,1)}, u32[]{:S(2)}) copy-start(bf16[2,2]{0,1:T(2,128)(2,1)} %constant.81.clone) | copy-start | bytes 28
  0.6 18.9 %copy-start.6 = (bf16[6,6]{0,1:T(8,128)(2,1)S(1)}, bf16[6,6]{0,1:T(8,128)(2,1)}, u32[]{:S(2)}) copy-start(bf16[6,6]{0,1:T(8,128)(2,1)} %constant.80.clone) | copy-start | bytes 220
  0.7 18.8 %copy-start.5 = (bf16[24,24]{1,0:T(8,128)(2,1)S(1)}, bf16[24,24]{1,0:T(8,128)(2,1)}, u32[]{:S(2)}) copy-start(bf16[24,24]{1,0:T(8,128)(2,1)} %param.15) | copy-start | bytes 3460
  3.5 51.2 %all-to-all-start.1 = ((bf16[8,2,9600]{2,1,0:T(2,128)(2,1)}), bf16[8,2,9600]{2,1,0:T(2,128)(2,1)S(1)}, u32[]{:S(2)}, u32[]{:S(2)}) async-start(bf16[8,2,9600]{2,1,0:T(2,128)(2,1)} %reshape.106), calls=%async_computation.1 | async-start | bytes 614400 | tf_op jit(solution)/shard_map/all_to_all | solution.py:250
  10.8 11.9 %copy-start.4 = (f32[24,7,7]{0,2,1:T(8,128)S(1)}, f32[24,7,7]{0,2,1:T(8,128)}, u32[]{:S(2)}) copy-start(f32[24,7,7]{0,2,1:T(8,128)} %param.14) | copy-start | bytes 14116
  12.8 22.1 %collective-permute-start.1 = (bf16[2,3,24,1440]{3,2,1,0:T(8,128)(2,1)}, bf16[2,3,24,1440]{3,2,1,0:T(8,128)(2,1)}, u32[]{:S(2)}, u32[]{:S(2)}) collective-permute-start(bf16[2,3,24,1440]{3,2,1,0:T(8,128)(2,1)} %get-tuple-element.40), channel_id=1, source_target_pairs={{1,0},{2,1},{3,2},{4,3},{5,4},{6,5},{7,6},{9,8},{10,9},{11,10},{12... | collective-permute-start | bytes 1244168 | tf_op jit(solution)/shard_map/ppermute | solution.py:42
  14.1 22.7 %collective-permute-start = (bf16[2,3,24,1440]{3,2,1,0:T(8,128)(2,1)S(1)}, bf16[2,3,24,1440]{3,2,1,0:T(8,128)(2,1)}, u32[]{:S(2)}, u32[]{:S(2)}) collective-permute-start(bf16[2,3,24,1440]{3,2,1,0:T(8,128)(2,1)S(1)} %get-tuple-element.41), channel_id=1, source_target_pairs={{0,1},{1,2},{2,3},{3,4},{4,5},{5,6},{6,7},{8,9},{9,10},{10,11},{11... | collective-permute-start | bytes 1244168 | tf_op jit(solution)/shard_map/ppermute | solution.py:41
  32.9 28.6 %copy-start.7 = (s32[160]{0:T(256)S(1)}, s32[160]{0:T(256)}, u32[]{:S(2)}) copy-start(s32[160]{0:T(256)} %param.18) | copy-start | bytes 1924
  54.7 18.5 %all-to-all-start = ((bf16[32,24,256]{2,1,0:T(8,128)(2,1)}), bf16[32,24,256]{2,1,0:T(8,128)(2,1)S(1)}, u32[]{:S(2)}, u32[]{:S(2)}) async-start(bf16[32,24,256]{2,1,0:T(8,128)(2,1)} %bitcast.51), calls=%async_computation | async-start | bytes 786432 | tf_op jit(solution)/shard_map/all_to_all | solution.py:275
  73.2 0.7 copy-start
  85.9 23.8 %all-to-all-start.2 = ((bf16[32,24,256]{2,1,0:T(8,128)(2,1)}), bf16[32,24,256]{2,1,0:T(8,128)(2,1)S(1)}, u32[]{:S(2)}, u32[]{:S(2)}) async-start(bf16[32,24,256]{2,1,0:T(8,128)(2,1)} %bitcast.52), calls=%async_computation.2 | async-start | bytes 786432 | tf_op jit(solution)/shard_map/all_to_all | solution.py:275
  109.7 5.8 %copy-start.1 = (bf16[32,24,256]{2,1,0:T(8,128)(2,1)}, bf16[32,24,256]{2,1,0:T(8,128)(2,1)S(1)}, u32[]{:S(2)}) copy-start(bf16[32,24,256]{2,1,0:T(8,128)(2,1)S(1)} %all-to-all-done.2) | copy-start | bytes 1179652
  109.7 52.1 %all-to-all-start.3 = ((bf16[32,40,240]{2,1,0:T(8,128)(2,1)}), bf16[32,40,240]{2,1,0:T(8,128)(2,1)S(1)}, u32[]{:S(2)}, u32[]{:S(2)}) async-start(bf16[32,40,240]{2,1,0:T(8,128)(2,1)} %reshape_reshape.4), calls=%async_computation.3 | async-start | bytes 1310720 | tf_op jit(solution)/shard_map/all_to_all | solution.py:275
  121.1 15.7 %collective-permute-start.3 = (bf16[2,3,24,1440]{3,2,1,0:T(8,128)(2,1)S(1)}, bf16[2,3,24,1440]{3,2,1,0:T(8,128)(2,1)S(1)}, u32[]{:S(2)}, u32[]{:S(2)}) collective-permute-start(bf16[2,3,24,1440]{3,2,1,0:T(8,128)(2,1)S(1)} %get-tuple-element.38), channel_id=1, source_target_pairs={{1,0},{2,1},{3,2},{4,3},{5,4},{6,5},{7,6},{9,8},{10,9},{11,10},{12... | collective-permute-start | bytes 1244168 | tf_op jit(solution)/shard_map/ppermute | solution.py:42
  122.6 24.8 %collective-permute-start.2 = (bf16[2,3,24,1440]{3,2,1,0:T(8,128)(2,1)S(1)}, bf16[2,3,24,1440]{3,2,1,0:T(8,128)(2,1)S(1)}, u32[]{:S(2)}, u32[]{:S(2)}) collective-permute-start(bf16[2,3,24,1440]{3,2,1,0:T(8,128)(2,1)S(1)} %get-tuple-element.39), channel_id=1, source_target_pairs={{0,1},{1,2},{2,3},{3,4},{4,5},{5,6},{6,7},{8,9},{9,10},{10,11},{11... | collective-permute-start | bytes 1244168 | tf_op jit(solution)/shard_map/ppermute | solution.py:41
  136.8 11.6 %copy-start.2 = (bf16[2,3,24,1440]{3,2,1,0:T(8,128)(2,1)}, bf16[2,3,24,1440]{3,2,1,0:T(8,128)(2,1)S(1)}, u32[]{:S(2)}) copy-start(bf16[2,3,24,1440]{3,2,1,0:T(8,128)(2,1)S(1)} %collective-permute-done.3.high) | copy-start | bytes 1244164
  147.4 1.0 copy-start.3
where the time goes:
time: 189 us; the launch traced here: 188 us
  local copies, waits for them, and re-layouts  71.6 us (38%)
  Pallas kernels  45.7 us (24%)
  starting transfers between devices  33.5 us (18%)
  waiting for transfers between devices  31.4 us (17%)
  other arithmetic  4.58 us (2%)
    unnamed x24, local copies, waits for them, and re-layouts  23.5 us
    pallas_call x1, Pallas kernels, local(): pl.pallas_call(forward_kernel, out_shape=(chunk, jax.ShapeDtypeStruct(gri...  16.1 us
    all_to_all x3, starting transfers between devices, swap(): lax.all_to_all(flat, ('ens', 'lat'), split_axis=0, concat_axis=0, tiled=T...  13.5 us
    pallas_call x1, Pallas kernels, local(): pl.pallas_call(convolve_kernel, out_shape=jax.ShapeDtypeStruct(grid_shape...  13.4 us
    ppermute x2, waiting for transfers between devices, neighbours(): low = lax.ppermute(block[:, block.shape[1] - width:], 'lat', forward)  12.5 us
    pallas_call x1, Pallas kernels, local(): pl.pallas_call(functools.partial(score_kernel, rows), out_shape=(chunk, j...  12 us
    ppermute x2, starting transfers between devices, neighbours(): low = lax.ppermute(block[:, block.shape[1] - width:], 'lat', forward)  9.94 us
    ppermute x2, waiting for transfers between devices, neighbours(): high = lax.ppermute(block[:, :width], 'lat', backward)  9.56 us
  transfers between devices with their start and end apart: 8, of which 4 were waited for; matrix products, arithmetic and copies ran while one was open for 25% of the time, Pallas kernels for 18%

commit v1 on v0

v1 whole, which is shorter than its diff:
```python
import functools
import math

import jax
import jax.numpy as jnp
import numpy as np
from jax import lax
from jax.experimental import pallas as pl
from jax.experimental.pallas import tpu as pltpu
from jax.sharding import PartitionSpec as P

smooth_width = 0.5
LEAD = 8
F32 = jnp.float32
BF16 = jnp.bfloat16


def up(value, step):
    return -(-value // step) * step


def full(shape):
    return pl.BlockSpec(shape, lambda *_: (0,) * len(shape), memory_space=pltpu.VMEM)


def wave_table(nlon, orders, groups, order_pad):
    share = orders // groups
    columns = np.arange(nlon, dtype=np.int64)
    number = np.arange(orders, dtype=np.int64)
    angles = (columns[:, None] * number[None, :] % nlon) * (2.0 * math.pi / nlon)
    table = np.zeros((nlon, 2, groups, order_pad), np.float32)
    for part, values in enumerate((np.cos(angles), -np.sin(angles))):
        table[:, part, :, :share] = (values / math.sqrt(nlon)).reshape(nlon, groups, share)
    return table.reshape(nlon, 2 * groups * order_pad).astype(jnp.bfloat16)


def edges(block, width):
    odd = lax.axis_index("lat") % 2
    last = block.shape[1] - width
    count = lax.axis_size("lat")
    near = [(i, i ^ 1) for i in range(count)]
    far = [(i, (i + (1 if i % 2 else -1)) % count) for i in range(count)]
    inner = lax.dynamic_slice_in_dim(block, (1 - odd) * last, width, 1)
    outer = lax.dynamic_slice_in_dim(block, odd * last, width, 1)
    return lax.ppermute(inner, "lat", near), lax.ppermute(outer, "lat", far)


def place():
    at, count = lax.axis_index("lat"), lax.axis_size("lat")
    return jnp.stack([at % 2, at > 0, at < count - 1]).astype(jnp.int32)


def fill_row(padded, row, value):
    nlon, wide = value.shape[-1], padded.shape[-1]
    padded[row] = jnp.concatenate(
        [value[:, nlon - LEAD :], value, value[:, : wide - nlon - LEAD]], axis=-1
    )


def tap_sum(padded, taps, c0, lines, size):
    wide = padded.shape[-1]
    total = None
    for q in range(size):
        part = None
        for row, p in lines:
            weight = jnp.tile(taps[p * size + q, pl.ds(c0, 8), :], (1, wide // 128))
            term = weight * padded[row, pl.ds(c0, 8), :]
            part = term if part is None else part + term
        shift = (size // 2 - q) % wide
        if shift:
            part = pltpu.roll(part, shift, 1)
        total = part if total is None else total + part
    return total


def spread_taps(kernel, taps, flip):
    size, _, chans = kernel.shape
    for p in range(size):
        plane = kernel[p].T
        for q in range(size):
            value = plane[:, q : q + 1]
            if p == q == size // 2:
                value = value + 1.0
            at = p * size + q
            at = size * size - 1 - at if flip else at
            taps[at] = jnp.broadcast_to(value, (chans, 128))


def own_part(own, taps, partial, padded, size):
    members, rows, chans, nlon = own.shape
    half = size // 2

    @pl.loop(0, members)
    def _(b):
        for row in range(rows):
            fill_row(padded, row, own[b, row].astype(F32))

        @pl.loop(0, chans // 8)
        def _(ct):
            c0 = pl.multiple_of(ct * 8, 8)
            for i in range(rows):
                lines = [(i + p - half, p) for p in range(size) if 0 <= i + p - half < rows]
                total = tap_sum(padded, taps, c0, lines, size)
                partial[b, i, pl.ds(c0, 8), :] = total[:, LEAD : LEAD + nlon]


def halo_part(flags, near, far, taps, partial, padded, size, emit):
    members, rows, chans, nlon = partial.shape
    half = size // 2
    odd, below, above = flags[0] == 1, flags[1] == 1, flags[2] == 1

    @pl.loop(0, members)
    def _(b):
        for row in range(half):
            one, other = near[b, row].astype(F32), far[b, row].astype(F32)
            zero = jnp.zeros_like(one)
            fill_row(padded, row, jnp.where(below, jnp.where(odd, one, other), zero))
            fill_row(padded, half + row, jnp.where(above, jnp.where(odd, other, one), zero))

        @pl.loop(0, chans // 8)
        def _(ct):
            c0 = pl.multiple_of(ct * 8, 8)
            for i in range(rows):
                lines = []
                for p in range(size):
                    at = i + p - half
                    if at < 0:
                        lines.append((at + half, p))
                    elif at >= rows:
                        lines.append((at - rows + half, p))
                value = partial[b, i, pl.ds(c0, 8), :]
                if lines:
                    total = tap_sum(padded, taps, c0, lines, size)
                    value = value + total[:, LEAD : LEAD + nlon]
                emit(b, i, c0, value)


def gelu_pair(x):
    scale = math.sqrt(2.0 / math.pi)
    square = x * x
    t = jnp.tanh(scale * x * (1.0 + 0.044715 * square))
    half = 0.5 * (1.0 + t)
    slope = half + 0.5 * x * (1.0 - t * t) * (scale * (1.0 + 3 * 0.044715 * square))
    return x * half, slope


def prepare_kernel(owners, own, kernel, weight, pick, partial, taps, mixer, padded):
    members, rows, chans, nlon = own.shape
    size = kernel.shape[0]
    spread_taps(kernel, taps, False)
    own_part(own, taps, partial, padded, size)
    lanes = mixer.shape[2] // owners
    slots = pick.shape[2] // owners
    span = owners * slots
    across = members * rows * chans
    lane = lax.broadcasted_iota(jnp.int32, (chans, mixer.shape[2]), 1)
    within = lane % lanes
    for r in range(2):
        table = lax.dot_general(
            weight[...], pick[r], (((0,), (0,)), ((), ())), preferred_element_type=F32
        )
        wide = jnp.concatenate(
            [jnp.tile(table[:, e * slots : (e + 1) * slots], (1, lanes // slots)) for e in range(owners)],
            axis=1,
        )
        for b in range(members):
            for i in range(rows):
                kept = (within // slots) == i * members + b
                at = (b * rows + i) * chans
                mixer[r, at : at + chans, :] = jnp.where(kept, wide, 0.0).astype(BF16)


def forward_kernel(flags, near, far, partial, taps, table, mixer, out, slope, padded, act):
    members, rows, chans, nlon = partial.shape
    owners, groups, order_pad, lanes = out.shape
    size = math.isqrt(taps.shape[0])

    def emit(b, i, c0, value):
        value, grad = gelu_pair(value)
        act[b, i, pl.ds(c0, 8), :] = value
        slope[b, i, pl.ds(c0, 8), :] = grad

    halo_part(flags, near, far, taps, partial, padded, size, emit)
    flat = act[...].reshape(members * rows * chans, nlon).astype(BF16)
    spectral = jnp.dot(flat, table[...], preferred_element_type=F32).astype(BF16)
    half = groups * order_pad
    mixed = None
    for r in range(2):
        part = lax.dot_general(
            spectral[:, r * half : (r + 1) * half],
            mixer[r],
            (((0,), (0,)), ((), ())),
            preferred_element_type=F32,
        )
        mixed = part if mixed is None else mixed + part
    for e in range(owners):
        out[e] = mixed[:, e * lanes : (e + 1) * lanes].reshape(groups, order_pad, lanes).astype(BF16)


def soft_sign(gaps):
    return gaps * lax.rsqrt(gaps * gaps + smooth_width * smooth_width)


def score_kernel(rows, got, legendre, target, order, back, grads, spread, gather):
    owners, groups, order_pad, lanes = got.shape
    orders, nlat, degrees = legendre.shape
    slots = target.shape[1]
    ens = spread.shape[1] // slots
    local = ens // owners
    width = local * slots
    for t in range(groups):
        for i in range(rows):
            pieces = [got[e, t, :, i * width : (i + 1) * width] for e in range(owners)]
            at = (t * rows + i) * order_pad
            spread[at : at + order_pad, :] = jnp.concatenate(pieces, axis=-1).astype(F32)
    gather[...] = jnp.zeros(gather.shape, F32)

    @pl.loop(0, orders)
    def _(m):
        block = spread[pl.ds(m, nlat, stride=order_pad), :].astype(BF16)
        leg = legendre[m]
        coeff = lax.dot_general(
            block, leg, (((0,), (0,)), ((), ())), preferred_element_type=F32
        )
        own = [coeff[k * slots : (k + 1) * slots] for k in range(ens)]
        truth = target[m].astype(F32)
        sums = [None] * ens
        for k in range(ens):
            for n in range(k + 1, ens):
                sign = soft_sign(own[k] - own[n])
                sums[k] = sign if sums[k] is None else sums[k] + sign
                sums[n] = -sign if sums[n] is None else sums[n] - sign
        grad = jnp.concatenate(
            [
                soft_sign(own[k] - truth) * (1.0 / ens) - sums[k] * (1.0 / (ens * (ens - 1)))
                for k in range(ens)
            ],
            axis=0,
        ).astype(BF16)
        spec = lax.dot_general(
            leg, grad, (((1,), (1,)), ((), ())), preferred_element_type=F32
        )
        gather[pl.ds(m, nlat, stride=order_pad), :] = spec
        at = pl.multiple_of(m * ens * slots, 8)
        ordered = jnp.dot(grad, order[...], preferred_element_type=F32)
        for j in range(grads.shape[0]):
            last = min(degrees, (j + 1) * 128)
            grads[j, pl.ds(at, ens * slots), : last - j * 128] = ordered[:, j * 128 : last]

    for t in range(groups):
        for e in range(owners):
            pieces = []
            for i in range(rows):
                at = (t * rows + i) * order_pad
                pieces.append(gather[at : at + order_pad, e * width : (e + 1) * width])
            if lanes > rows * width:
                pieces.append(jnp.zeros((order_pad, lanes - rows * width), F32))
            back[e, t] = jnp.concatenate(pieces, axis=-1).astype(BF16)


def backward_kernel(got, mixer, table, slope, out, flat):
    owners, groups, order_pad, lanes = got.shape
    members, rows, chans, nlon = slope.shape
    half = groups * order_pad
    spectra = jnp.concatenate(
        [got[e].reshape(half, lanes) for e in range(owners)], axis=-1
    )
    parts = []
    for r in range(2):
        parts.append(
            lax.dot_general(
                mixer[r], spectra, (((1,), (1,)), ((), ())), preferred_element_type=F32
            ).astype(BF16)
        )
    unmixed = jnp.concatenate(parts, axis=-1)
    flat[...] = lax.dot_general(
        unmixed, table[...], (((1,), (1,)), ((), ())), preferred_element_type=F32
    ).reshape(flat.shape)
    for b in range(members):
        for i in range(rows):
            out[b, i] = (flat[b, i] * slope[b, i]).astype(BF16)


def own_kernel(own, kernel, partial, taps, padded):
    spread_taps(kernel, taps, True)
    own_part(own, taps, partial, padded, kernel.shape[0])


def halo_kernel(flags, near, far, partial, taps, out, padded, stage):
    def emit(b, i, c0, value):
        stage[b, i, pl.ds(c0, 8), :] = value

    halo_part(flags, near, far, taps, partial, padded, math.isqrt(taps.shape[0]), emit)
    out[...] = stage[...].astype(BF16)


def pack_kernel(members, used, per_owner, grads, out):
    owners, groups, depth, lanes = out.shape
    share = depth // members
    stride = grads.shape[1] // share
    slots = stride // (owners * members)
    for e in range(owners):
        for b in range(members):
            at = (e * members + b) * slots
            planes = [
                jnp.concatenate(
                    [grads[j, pl.ds(at + s, share, stride=stride), :] for j in range(grads.shape[0])],
                    axis=1,
                )
                for s in range(used)
            ]
            for t in range(groups):
                pieces = [x[:, t * per_owner : (t + 1) * per_owner] for x in planes]
                if lanes > used * per_owner:
                    pieces.append(jnp.zeros((share, lanes - used * per_owner), F32))
                out[e, t, b * share : (b + 1) * share, :] = jnp.concatenate(pieces, axis=1).astype(BF16)


def unpack_kernel(members, got, out):
    owners, groups, depth, lanes = got.shape
    _, chans, per_owner, _, orders = out.shape
    share, chan_share = depth // members, chans // owners
    row = lax.broadcasted_iota(jnp.int32, (groups * depth, orders), 0)
    column = lax.broadcasted_iota(jnp.int32, (groups * depth, orders), 1)
    for b in range(members):
        wanted = (column // share) * depth + b * share + column % share
        picker = jnp.where(row == wanted, 1.0, 0.0).astype(BF16)
        for e in range(owners):
            block = lax.dot_general(
                got[e].reshape(groups * depth, lanes),
                picker,
                (((0,), (0,)), ((), ())),
                preferred_element_type=F32,
            )
            for c in range(chan_share):
                for r in range(2):
                    at = (r * chan_share + c) * per_owner
                    out[b, e * chan_share + c, :, r, :] = block[at : at + per_owner]


def local(fields, depth_kernel, mix_weight, legendre, truth, degree_order):
    ens_parts, groups = lax.axis_size("ens"), lax.axis_size("lat")
    ens_at, lat_at = lax.axis_index("ens"), lax.axis_index("lat")
    members, chans, rows, nlon = fields.shape
    _, orders, degrees = legendre.shape
    ens = members * ens_parts
    nlat = rows * groups
    share, per_owner, chan_share = orders // groups, degrees // groups, chans // ens_parts
    order_pad = up(share, 8)
    slots = up(2 * chan_share, 8)
    lanes = up(rows * members * slots, 128)
    wide = up(nlon + 2 * LEAD, 128)
    size = depth_kernel.shape[1]
    halo = size // 2
    used = 2 * chan_share

    table = jnp.asarray(wave_table(nlon, orders, groups, order_pad))
    kernel = depth_kernel.transpose(1, 2, 0)
    flags = place()
    own = fields.transpose(0, 2, 1, 3)
    with jax.named_scope("first"):
        near, far = edges(own, halo)

    pick = np.zeros((2, chans, ens_parts, slots), np.float32)
    for r in range(2):
        for o in range(chans):
            pick[r, o, o // chan_share, r * chan_share + o % chan_share] = 1.0
    pick = jnp.asarray(pick.reshape(2, chans, ens_parts * slots).astype(jnp.bfloat16))

    with jax.named_scope("orders"):
        order_legendre = lax.all_to_all(legendre, "lat", split_axis=1, concat_axis=0, tiled=True)
    order_legendre = order_legendre.transpose(1, 0, 2)
    target = lax.dynamic_slice(
        truth, (ens_at * chan_share, 0, lat_at * share, 0), (chan_share, 2, share, degrees)
    )
    target = target.transpose(2, 1, 0, 3).reshape(share, used, degrees)
    target = jnp.pad(target, ((0, 0), (0, slots - used), (0, 0)))
    reorder = (jnp.arange(degrees)[:, None] == degree_order[None, :]).astype(BF16)

    vmem = pltpu.CompilerParams(vmem_limit_bytes=60 * 1024 * 1024)
    scalars = pl.BlockSpec(memory_space=pltpu.SMEM)
    whole = pl.BlockSpec(memory_space=pltpu.VMEM)
    grid_shape = (members, rows, chans, nlon)
    count = members * rows * chans
    chunk = jax.ShapeDtypeStruct((ens_parts, groups, order_pad, lanes), BF16)
    partial_out = jax.ShapeDtypeStruct(grid_shape, F32)
    taps_out = jax.ShapeDtypeStruct((size * size, chans, 128), F32)
    own_rows = pltpu.VMEM((rows, chans, wide), F32)
    halo_rows = pltpu.VMEM((2 * halo, chans, wide), F32)

    def call(body, outs, scratch, name, work, *args):
        specs = [scalars if a is flags else whole for a in args]
        return pl.pallas_call(
            body,
            out_shape=outs,
            in_specs=specs,
            scratch_shapes=scratch,
            compiler_params=vmem,
            cost_estimate=pl.CostEstimate(
                flops=work, transcendentals=0, bytes_accessed=8 * count * nlon
            ),
            name=name,
        )(*args)

    work = 2 * size * size * count * nlon
    partial, taps, mixer = call(
        functools.partial(prepare_kernel, ens_parts),
        (partial_out, taps_out, jax.ShapeDtypeStruct((2, count, ens_parts * lanes), BF16)),
        [own_rows],
        "prepare",
        work,
        own,
        kernel,
        mix_weight,
        pick,
    )
    sent, slope = call(
        forward_kernel,
        (chunk, partial_out),
        [halo_rows, pltpu.VMEM(grid_shape, F32)],
        "forward",
        work,
        flags,
        near,
        far,
        partial,
        taps,
        table,
        mixer,
    )

    def swap(x):
        flat = x.reshape((ens_parts * groups,) + x.shape[2:])
        flat = lax.all_to_all(flat, ("ens", "lat"), split_axis=0, concat_axis=0, tiled=True)
        return flat.reshape(x.shape)

    got = swap(sent)
    spread = pltpu.VMEM((nlat * order_pad, ens * slots), F32)
    back, grads = call(
        functools.partial(score_kernel, rows),
        (chunk, jax.ShapeDtypeStruct((up(degrees, 128) // 128, share * ens * slots, 128), F32)),
        [spread, spread],
        "score",
        work,
        got,
        order_legendre,
        target,
        reorder,
    )
    returned = swap(back)
    packed = call(
        functools.partial(pack_kernel, members, used, per_owner),
        jax.ShapeDtypeStruct(
            (ens_parts, groups, members * share, up(used * per_owner, 128)), BF16
        ),
        [],
        "pack",
        work,
        grads,
    )
    owned = swap(packed)

    hid_grad = call(
        backward_kernel,
        jax.ShapeDtypeStruct(grid_shape, BF16),
        [pltpu.VMEM(grid_shape, F32)],
        "backward",
        work,
        returned,
        mixer,
        table,
        slope,
    )
    near, far = edges(hid_grad, halo)
    partial, taps = call(
        own_kernel, (partial_out, taps_out), [own_rows], "own", work, hid_grad, kernel
    )
    score_grad = call(
        functools.partial(unpack_kernel, members),
        jax.ShapeDtypeStruct((members, chans, per_owner, 2, orders), F32),
        [],
        "unpack",
        work,
        owned,
    )
    grad_fields = call(
        halo_kernel,
        jax.ShapeDtypeStruct(grid_shape, BF16),
        [halo_rows, pltpu.VMEM(grid_shape, F32)],
        "halo",
        work,
        flags,
        near,
        far,
        partial,
        taps,
    )
    return grad_fields.transpose(0, 2, 1, 3), score_grad.transpose(0, 1, 3, 4, 2)


def solution(mesh):
    placed = (P("ens", None, "lat", None), P(), P(), P("lat", None, None), P(), P())
    return jax.shard_map(
        local,
        mesh=mesh,
        in_specs=placed,
        out_specs=(P("ens", None, "lat", None), P("ens", None, None, None, "lat")),
        check_vma=False,
    )
```

time: 189 us -> 142 us (0.75)
  local copies, waits for them, and re-layouts: 71.6 us -> 11.1 us
  Pallas kernels: 45.7 us -> 63.3 us
  waiting for transfers between devices: 31.4 us -> 37.4 us
  starting transfers between devices: 33.5 us -> 27.6 us
  other arithmetic: 4.58 us -> 1.31 us
    pallas_call x4 -> x8, Pallas kernels: 45.7 us -> 63.3 us  [call(): pl.pallas_call(body, out_shape=outs, in_specs=specs, scratch_shapes=scrat...]
    reshape x5 -> x1, local copies, waits for them, and re-layouts: 16.6 us -> 0.03 us  [local(): target = target.transpose(2, 1, 0, 3).reshape(share, used, degrees)]
    unnamed x24 -> x22, local copies, waits for them, and re-layouts: 23.5 us -> 7.13 us
    all_to_all x3, waiting for transfers between devices: 9.29 us -> 18.5 us  [swap(): lax.all_to_all(flat, ('ens', 'lat'), split_axis=0, concat_axis=0, tiled=T...]
    another operation x2 -> x0, local copies, waits for them, and re-layouts: 7.16 us -> none  [the longest x1 7.14 us: swap(): flat = x.reshape((ens_parts * groups,) + x.shape[2:])]
    transpose x2 -> x0, local copies, waits for them, and re-layouts: 6.81 us -> none  [local(): grads = grads[:, :, :, :2 * chan_share].transpose(1, 4, 2, 0, 3, 5)]
    convert_element_type x1 -> x0, local copies, waits for them, and re-layouts: 6.78 us -> none  [local(): return (grad_fields.transpose(0, 2, 1, 3), score_grad.astype(F32))]
    all_to_all x3, starting transfers between devices: 13.5 us -> 9.95 us  [swap(): lax.all_to_all(flat, ('ens', 'lat'), split_axis=0, concat_axis=0, tiled=T...]
  transfers between devices with their start and end apart: 8 -> 8, of which waited for: 4 -> 4; matrix products, arithmetic and copies ran while one was open for 25% -> 4% of each run, Pallas kernels for 18% -> 34%
where the time goes in v1:
time: 142 us; the launch traced here: 141 us
  Pallas kernels  63.3 us (45%)
  waiting for transfers between devices  37.4 us (26%)
  starting transfers between devices  27.6 us (19%)
  local copies, waits for them, and re-layouts  11.1 us (8%)
    pallas_call x8, Pallas kernels, call(): pl.pallas_call(body, out_shape=outs, in_specs=specs, scratch_shapes=scrat...  63.3 us
    ppermute x4, waiting for transfers between devices, edges(): return (lax.ppermute(inner, 'lat', near), lax.ppermute(outer, 'lat', far))  18.9 us
    all_to_all x3, waiting for transfers between devices, swap(): lax.all_to_all(flat, ('ens', 'lat'), split_axis=0, concat_axis=0, tiled=T...  18.5 us
    ppermute x4, starting transfers between devices, edges(): return (lax.ppermute(inner, 'lat', near), lax.ppermute(outer, 'lat', far))  10.3 us
    all_to_all x3, starting transfers between devices, swap(): lax.all_to_all(flat, ('ens', 'lat'), split_axis=0, concat_axis=0, tiled=T...  9.95 us
    all_to_all x1, starting transfers between devices, local(): lax.all_to_all(legendre, 'lat', split_axis=1, concat_axis=0, tiled=True)  7.31 us
    unnamed x22, local copies, waits for them, and re-layouts  7.13 us
  transfers between devices with their start and end apart: 8, of which 4 were waited for; matrix products, arithmetic and copies ran while one was open for 4% of the time, Pallas kernels for 34%

profile of v1, /device:TPU:0, one launch (start us, length us, event | category | flops | bytes accessed | tf_op | source)
XLA Modules:
  0.0 141.5 jit_solution(7037282899139044277)
XLA Ops:
  0.6 1.4 copy.28
  2.0 1.5 %reshape.35 = bf16[8,2,9600]{2,1,0:T(2,128)(2,1)} reshape(bf16[160,6,160]{2,1,0:T(8,128)(2,1)S(1)} %bitcast.35) | data formatting | bytes 614400
  3.5 7.3 %all-to-all-start.1 = ((bf16[8,2,9600]{2,1,0:T(2,128)(2,1)}), bf16[8,2,9600]{2,1,0:T(2,128)(2,1)S(1)}, u32[]{:S(2)}, u32[]{:S(2)}) async-start(bf16[8,2,9600]{2,1,0:T(2,128)(2,1)} %reshape.35), calls=%async_computation.1 | async-start | bytes 614400 | tf_op jit(solution)/shard_map/orders/all_to_all | solution.py:371
  11.0 2.1 %collective-permute-start = (bf16[2,3,24,1440]{3,2,1,0:T(8,128)(2,1)S(1)}, bf16[2,3,24,1440]{3,2,1,0:T(8,128)(2,1)S(1)}, u32[]{:S(2)}, u32[]{:S(2)}) collective-permute-start(bf16[2,3,24,1440]{3,2,1,0:T(8,128)(2,1)S(1)} %get-tuple-element.23), channel_id=1, source_target_pairs={{0,1},{1,0},{2,3},{3,2},{4,5},{5,4},{6,7},{7,6},{8,9},{9,8},{10,11... | collective-permute-start | bytes 1244168 | tf_op jit(solution)/shard_map/first/ppermute | solution.py:45
  13.0 3.3 %collective-permute-start.1 = (bf16[2,3,24,1440]{3,2,1,0:T(8,128)(2,1)S(1)}, bf16[2,3,24,1440]{3,2,1,0:T(8,128)(2,1)S(1)}, u32[]{:S(2)}, u32[]{:S(2)}) collective-permute-start(bf16[2,3,24,1440]{3,2,1,0:T(8,128)(2,1)S(1)} %get-tuple-element.22), channel_id=1, source_target_pairs={{0,7},{1,2},{2,1},{3,4},{4,3},{5,6},{6,5},{7,0},{8,15},{9,10},{10,... | collective-permute-start | bytes 1244168 | tf_op jit(solution)/shard_map/first/ppermute | solution.py:45
  16.3 9.7 %prepare.1 = (f32[2,6,24,1440]{3,2,1,0:T(8,128)}, f32[49,24,128]{2,1,0:T(8,128)}, bf16[2,288,1024]{2,1,0:T(8,128)(2,1)}) custom-call(bf16[2,6,24,1440]{3,2,1,0:T(8,128)(2,1)} %bitcast.32, f32[7,7,24]{2,1,0:T(8,128)} %bitcast.46, bf16[24,24]{1,0:T(8,128)(2,1)} %weight.1, bf16[2,24,64]{2,1,0:T(8,128)(2,1)} %constant.46.clone.pick), custom_call_target="tpu_custom_call" | custom-call | flops 40642560 | bytes 3317760 | tf_op jit(solution)/shard_map/prepare/pallas_call | solution.py:393
  26.7 8.7 %collective-permute-done.near = bf16[2,3,24,1440]{3,2,1,0:T(8,128)(2,1)S(1)} collective-permute-done((bf16[2,3,24,1440]{3,2,1,0:T(8,128)(2,1)S(1)}, bf16[2,3,24,1440]{3,2,1,0:T(8,128)(2,1)S(1)}, u32[]{:S(2)}, u32[]{:S(2)}) %collective-permute-start) | collective-permute-done | bytes 414752 | tf_op jit(solution)/shard_map/first/ppermute | solution.py:45
  36.4 11.0 %forward.1 = (bf16[4,8,24,256]{3,2,1,0:T(8,128)(2,1)}, f32[2,6,24,1440]{3,2,1,0:T(8,128)}) custom-call(s32[3]{0:T(128)} %pad_add_fusion.flags, bf16[2,3,24,1440]{3,2,1,0:T(8,128)(2,1)} %copy-done.4, bf16[2,3,24,1440]{3,2,1,0:T(8,128)(2,1)} %copy-done.5, f32[2,6,24,1440]{3,2,1,0:T(8,128)} %get-tuple-element.11.partial, ...), custom_call_target="tpu_custom_call" | custom-call | flops 40642560 | bytes 3317760 | tf_op jit(solution)/shard_map/forward/pallas_call | solution.py:393
  47.4 4.6 %all-to-all-start = ((bf16[32,24,256]{2,1,0:T(8,128)(2,1)}), bf16[32,24,256]{2,1,0:T(8,128)(2,1)S(1)}, u32[]{:S(2)}, u32[]{:S(2)}) async-start(bf16[32,24,256]{2,1,0:T(8,128)(2,1)} %bitcast.44), calls=%async_computation | async-start | bytes 786432 | tf_op jit(solution)/shard_map/all_to_all | solution.py:434
  52.0 1.0 constant_dynamic-slice_fusion.2
  56.1 9.3 %all-to-all-done = bf16[32,24,256]{2,1,0:T(8,128)(2,1)S(1)} async-done(((bf16[32,24,256]{2,1,0:T(8,128)(2,1)}), bf16[32,24,256]{2,1,0:T(8,128)(2,1)S(1)}, u32[]{:S(2)}, u32[]{:S(2)}) %all-to-all-start) | async-done | bytes 393248 | tf_op jit(solution)/shard_map/all_to_all | solution.py:434
  66.2 12.3 %score.1 = (bf16[4,8,24,256]{3,2,1,0:T(8,128)(2,1)}, f32[2,2560,128]{2,1,0:T(8,128)}) custom-call(bf16[4,8,24,256]{3,2,1,0:T(8,128)(2,1)} %bitcast.40, bf16[20,48,160]{2,1,0:T(8,128)(2,1)} %bitcast.39, bf16[20,16,160]{2,1,0:T(8,128)(2,1)} %pad.4.target, bf16[160,160]{1,0:T(8,128)(2,1)} %fusion.order), custom_call_target="tpu_custom_call" | custom-call | flops 40642560 | bytes 3317760 | tf_op jit(solution)/shard_map/score/pallas_call | solution.py:393
  78.5 2.6 %all-to-all-start.2 = ((bf16[32,24,256]{2,1,0:T(8,128)(2,1)}), bf16[32,24,256]{2,1,0:T(8,128)(2,1)S(1)}, u32[]{:S(2)}, u32[]{:S(2)}) async-start(bf16[32,24,256]{2,1,0:T(8,128)(2,1)} %bitcast.45), calls=%async_computation.2 | async-start | bytes 786432 | tf_op jit(solution)/shard_map/all_to_all | solution.py:434
  81.1 4.2 %pack.1 = bf16[4,8,40,256]{3,2,1,0:T(8,128)(2,1)} custom-call(f32[2,2560,128]{2,1,0:T(8,128)} %get-tuple-element.19.grads), custom_call_target="tpu_custom_call" | custom-call | flops 40642560 | bytes 3317760 | tf_op jit(solution)/shard_map/pack/pallas_call | solution.py:393
  85.3 9.2 %all-to-all-done.2 = bf16[32,24,256]{2,1,0:T(8,128)(2,1)S(1)} async-done(((bf16[32,24,256]{2,1,0:T(8,128)(2,1)}), bf16[32,24,256]{2,1,0:T(8,128)(2,1)S(1)}, u32[]{:S(2)}, u32[]{:S(2)}) %all-to-all-start.2) | async-done | bytes 393248 | tf_op jit(solution)/shard_map/all_to_all | solution.py:434
  94.5 2.8 %all-to-all-start.3 = ((bf16[32,40,256]{2,1,0:T(8,128)(2,1)}), bf16[32,40,256]{2,1,0:T(8,128)(2,1)S(1)}, u32[]{:S(2)}, u32[]{:S(2)}) async-start(bf16[32,40,256]{2,1,0:T(8,128)(2,1)} %bitcast.36), calls=%async_computation.3 | async-start | bytes 1310720 | tf_op jit(solution)/shard_map/all_to_all | solution.py:434
  97.3 4.3 %backward.1.own = bf16[2,6,24,1440]{3,2,1,0:T(8,128)(2,1)} custom-call(bf16[4,8,24,256]{3,2,1,0:T(8,128)(2,1)} %bitcast.41, bf16[2,288,1024]{2,1,0:T(8,128)(2,1)} %get-tuple-element.13.mixer, bf16[1440,384]{1,0:T(8,128)(2,1)} %constant.45.clone.table, f32[2,6,24,1440]{3,2,1,0:T(8,128)} %get-tuple-element.16.slope), custom_call_target="tpu_custom_call" | custom-call | flops 40642560 | bytes 3317760 | tf_op jit(solution)/shard_map/backward/pallas_call | solution.py:393
  101.6 1.2 constant_dynamic-slice_fusion
  102.8 1.5 %collective-permute-start.2 = (bf16[2,3,24,1440]{3,2,1,0:T(8,128)(2,1)S(1)}, bf16[2,3,24,1440]{3,2,1,0:T(8,128)(2,1)S(1)}, u32[]{:S(2)}, u32[]{:S(2)}) collective-permute-start(bf16[2,3,24,1440]{3,2,1,0:T(8,128)(2,1)S(1)} %get-tuple-element.21), channel_id=1, source_target_pairs={{0,1},{1,0},{2,3},{3,2},{4,5},{5,4},{6,7},{7,6},{8,9},{9,8},{10,11... | collective-permute-start | bytes 1244168 | tf_op jit(solution)/shard_map/ppermute | solution.py:45
  104.4 3.4 %collective-permute-start.3 = (bf16[2,3,24,1440]{3,2,1,0:T(8,128)(2,1)S(1)}, bf16[2,3,24,1440]{3,2,1,0:T(8,128)(2,1)S(1)}, u32[]{:S(2)}, u32[]{:S(2)}) collective-permute-start(bf16[2,3,24,1440]{3,2,1,0:T(8,128)(2,1)S(1)} %get-tuple-element.20), channel_id=1, source_target_pairs={{0,7},{1,2},{2,1},{3,4},{4,3},{5,6},{6,5},{7,0},{8,15},{9,10},{10,... | collective-permute-start | bytes 1244168 | tf_op jit(solution)/shard_map/ppermute | solution.py:45
  107.8 9.3 %own.1 = (f32[2,6,24,1440]{3,2,1,0:T(8,128)}, f32[49,24,128]{2,1,0:T(8,128)}) custom-call(bf16[2,6,24,1440]{3,2,1,0:T(8,128)(2,1)} %backward.1.own, f32[7,7,24]{2,1,0:T(8,128)} %bitcast.47), custom_call_target="tpu_custom_call" | custom-call | flops 40642560 | bytes 3317760 | tf_op jit(solution)/shard_map/own/pallas_call | solution.py:393
  117.1 10.1 %collective-permute-done.2.near = bf16[2,3,24,1440]{3,2,1,0:T(8,128)(2,1)S(1)} collective-permute-done((bf16[2,3,24,1440]{3,2,1,0:T(8,128)(2,1)S(1)}, bf16[2,3,24,1440]{3,2,1,0:T(8,128)(2,1)S(1)}, u32[]{:S(2)}, u32[]{:S(2)}) %collective-permute-start.2) | collective-permute-done | bytes 414752 | tf_op jit(solution)/shard_map/ppermute | solution.py:45
  128.2 9.1 %halo.1 = bf16[2,6,24,1440]{3,2,1,0:T(8,128)(2,1)} custom-call(s32[3]{0:T(128)} %pad_add_fusion.flags, bf16[2,3,24,1440]{3,2,1,0:T(8,128)(2,1)} %copy-done.6, bf16[2,3,24,1440]{3,2,1,0:T(8,128)(2,1)} %copy-done.7, f32[2,6,24,1440]{3,2,1,0:T(8,128)} %get-tuple-element.17.partial, f32[49,24,128]{2,1,0:T(8,128)} %get-tuple-element.18.taps), custom_call_target="tpu_custom_call" | custom-call | flops 40642560 | bytes 3317760 | tf_op jit(solution)/shard_map/halo/pallas_call | solution.py:393
  138.1 3.4 %unpack.1 = f32[2,24,20,2,160]{4,3,2,1,0:T(2,128)} custom-call(bf16[4,8,40,256]{3,2,1,0:T(8,128)(2,1)} %bitcast.33), custom_call_target="tpu_custom_call" | custom-call | flops 40642560 | bytes 3317760 | tf_op jit(solution)/shard_map/unpack/pallas_call | solution.py:393
  (31 shorter events, 7.4 us)
Async XLA Ops:
  0.6 10.2 %copy-start = (bf16[2,24,6,1440]{3,1,2,0:T(8,128)(2,1)S(1)}, bf16[2,24,6,1440]{3,1,2,0:T(8,128)(2,1)}, u32[]{:S(2)}) copy-start(bf16[2,24,6,1440]{3,1,2,0:T(8,128)(2,1)} %param.8) | copy-start | bytes 2488324
  3.5 43.9 %all-to-all-start.1 = ((bf16[8,2,9600]{2,1,0:T(2,128)(2,1)}), bf16[8,2,9600]{2,1,0:T(2,128)(2,1)S(1)}, u32[]{:S(2)}, u32[]{:S(2)}) async-start(bf16[8,2,9600]{2,1,0:T(2,128)(2,1)} %reshape.35), calls=%async_computation.1 | async-start | bytes 614400 | tf_op jit(solution)/shard_map/orders/all_to_all | solution.py:371
  11.0 24.5 %collective-permute-start = (bf16[2,3,24,1440]{3,2,1,0:T(8,128)(2,1)S(1)}, bf16[2,3,24,1440]{3,2,1,0:T(8,128)(2,1)S(1)}, u32[]{:S(2)}, u32[]{:S(2)}) collective-permute-start(bf16[2,3,24,1440]{3,2,1,0:T(8,128)(2,1)S(1)} %get-tuple-element.23), channel_id=1, source_target_pairs={{0,1},{1,0},{2,3},{3,2},{4,5},{5,4},{6,7},{7,6},{8,9},{9,8},{10,11... | collective-permute-start | bytes 1244168 | tf_op jit(solution)/shard_map/first/ppermute | solution.py:45
  13.0 22.4 %collective-permute-start.1 = (bf16[2,3,24,1440]{3,2,1,0:T(8,128)(2,1)S(1)}, bf16[2,3,24,1440]{3,2,1,0:T(8,128)(2,1)S(1)}, u32[]{:S(2)}, u32[]{:S(2)}) collective-permute-start(bf16[2,3,24,1440]{3,2,1,0:T(8,128)(2,1)S(1)} %get-tuple-element.22), channel_id=1, source_target_pairs={{0,7},{1,2},{2,1},{3,4},{4,3},{5,6},{6,5},{7,0},{8,15},{9,10},{10,... | collective-permute-start | bytes 1244168 | tf_op jit(solution)/shard_map/first/ppermute | solution.py:45
  35.5 0.8 copy-start.4
  35.5 0.9 copy-start.5
  47.4 6.3 %copy-start.8 = (s32[160]{0:T(256)S(1)}, s32[160]{0:T(256)}, u32[]{:S(2)}) copy-start(s32[160]{0:T(256)} %param.13) | copy-start | bytes 1924
  47.4 18.0 %all-to-all-start = ((bf16[32,24,256]{2,1,0:T(8,128)(2,1)}), bf16[32,24,256]{2,1,0:T(8,128)(2,1)S(1)}, u32[]{:S(2)}, u32[]{:S(2)}) async-start(bf16[32,24,256]{2,1,0:T(8,128)(2,1)} %bitcast.44), calls=%async_computation | async-start | bytes 786432 | tf_op jit(solution)/shard_map/all_to_all | solution.py:434
  65.4 0.7 copy-start.2
  78.5 16.0 %all-to-all-start.2 = ((bf16[32,24,256]{2,1,0:T(8,128)(2,1)}), bf16[32,24,256]{2,1,0:T(8,128)(2,1)S(1)}, u32[]{:S(2)}, u32[]{:S(2)}) async-start(bf16[32,24,256]{2,1,0:T(8,128)(2,1)} %bitcast.45), calls=%async_computation.2 | async-start | bytes 786432 | tf_op jit(solution)/shard_map/all_to_all | solution.py:434
  94.5 2.8 %copy-start.3 = (bf16[32,24,256]{2,1,0:T(8,128)(2,1)}, bf16[32,24,256]{2,1,0:T(8,128)(2,1)S(1)}, u32[]{:S(2)}) copy-start(bf16[32,24,256]{2,1,0:T(8,128)(2,1)S(1)} %all-to-all-done.2) | copy-start | bytes 1179652
  94.5 42.7 %all-to-all-start.3 = ((bf16[32,40,256]{2,1,0:T(8,128)(2,1)}), bf16[32,40,256]{2,1,0:T(8,128)(2,1)S(1)}, u32[]{:S(2)}, u32[]{:S(2)}) async-start(bf16[32,40,256]{2,1,0:T(8,128)(2,1)} %bitcast.36), calls=%async_computation.3 | async-start | bytes 1310720 | tf_op jit(solution)/shard_map/all_to_all | solution.py:434
  102.8 24.4 %collective-permute-start.2 = (bf16[2,3,24,1440]{3,2,1,0:T(8,128)(2,1)S(1)}, bf16[2,3,24,1440]{3,2,1,0:T(8,128)(2,1)S(1)}, u32[]{:S(2)}, u32[]{:S(2)}) collective-permute-start(bf16[2,3,24,1440]{3,2,1,0:T(8,128)(2,1)S(1)} %get-tuple-element.21), channel_id=1, source_target_pairs={{0,1},{1,0},{2,3},{3,2},{4,5},{5,4},{6,7},{7,6},{8,9},{9,8},{10,11... | collective-permute-start | bytes 1244168 | tf_op jit(solution)/shard_map/ppermute | solution.py:45
  104.4 22.8 %collective-permute-start.3 = (bf16[2,3,24,1440]{3,2,1,0:T(8,128)(2,1)S(1)}, bf16[2,3,24,1440]{3,2,1,0:T(8,128)(2,1)S(1)}, u32[]{:S(2)}, u32[]{:S(2)}) collective-permute-start(bf16[2,3,24,1440]{3,2,1,0:T(8,128)(2,1)S(1)} %get-tuple-element.20), channel_id=1, source_target_pairs={{0,7},{1,2},{2,1},{3,4},{4,3},{5,6},{6,5},{7,0},{8,15},{9,10},{10,... | collective-permute-start | bytes 1244168 | tf_op jit(solution)/shard_map/ppermute | solution.py:45
  127.2 0.8 copy-start.6
  127.2 0.9 copy-start.7
  137.2 0.9 copy-start.1

commit v2 on v1

v2 whole, which is shorter than its diff:
```python
import functools
import math

import jax
import jax.numpy as jnp
import numpy as np
from jax import lax
from jax.experimental import pallas as pl
from jax.experimental.pallas import tpu as pltpu
from jax.sharding import PartitionSpec as P

smooth_width = 0.5
LEAD = 8
F32 = jnp.float32
BF16 = jnp.bfloat16


def up(value, step):
    return -(-value // step) * step


def full(shape):
    return pl.BlockSpec(shape, lambda *_: (0,) * len(shape), memory_space=pltpu.VMEM)


def wave_table(nlon, orders, span):
    columns = np.arange(nlon, dtype=np.int64)
    number = np.arange(orders, dtype=np.int64)
    angles = (columns[:, None] * number[None, :] % nlon) * (2.0 * math.pi / nlon)
    table = np.zeros((nlon, 2, span), np.float32)
    for part, values in enumerate((np.cos(angles), -np.sin(angles))):
        table[:, part, :orders] = values / math.sqrt(nlon)
    return table.reshape(nlon, 2 * span).astype(jnp.bfloat16)


def partners(inner, outer):
    count = lax.axis_size("lat")
    near = [(i, i ^ 1) for i in range(count)]
    far = [(i, (i + (1 if i % 2 else -1)) % count) for i in range(count)]
    return lax.ppermute(inner, "lat", near), lax.ppermute(outer, "lat", far)


def place():
    at, count = lax.axis_index("lat"), lax.axis_size("lat")
    return jnp.stack([at % 2, at > 0, at < count - 1]).astype(jnp.int32)


def fill_row(padded, row, value):
    nlon, wide = value.shape[-1], padded.shape[-1]
    padded[row] = jnp.concatenate(
        [value[:, nlon - LEAD :], value, value[:, : wide - nlon - LEAD]], axis=-1
    )


def tap_sum(padded, taps, c0, lines, size):
    wide = padded.shape[-1]
    total = None
    for q in range(size):
        part = None
        for row, p in lines:
            weight = jnp.tile(taps[p * size + q, pl.ds(c0, 8), :], (1, wide // 128))
            term = weight * padded[row, pl.ds(c0, 8), :]
            part = term if part is None else part + term
        shift = (size // 2 - q) % wide
        if shift:
            part = pltpu.roll(part, shift, 1)
        total = part if total is None else total + part
    return total


def spread_taps(kernel, taps, flip):
    size, _, chans = kernel.shape
    for p in range(size):
        plane = kernel[p].T
        for q in range(size):
            value = plane[:, q : q + 1]
            if p == q == size // 2:
                value = value + 1.0
            at = p * size + q
            at = size * size - 1 - at if flip else at
            value = jnp.broadcast_to(value, (chans, 128))
            taps[at] = jnp.concatenate([value] * (taps.shape[1] // chans), axis=0)


def own_part(taps, partial, padded, size):
    rows, depth, nlon = partial.shape
    half = size // 2

    @pl.loop(0, depth // 8)
    def _(ct):
        c0 = pl.multiple_of(ct * 8, 8)
        for i in range(rows):
            lines = [(i + p - half, p) for p in range(size) if 0 <= i + p - half < rows]
            total = tap_sum(padded, taps, c0, lines, size)
            partial[i, pl.ds(c0, 8), :] = total[:, LEAD : LEAD + nlon]


def halo_part(flags, near, far, taps, partial, padded, size, emit):
    rows, depth, nlon = partial.shape
    half = size // 2
    odd, below, above = flags[0] == 1, flags[1] == 1, flags[2] == 1
    for row in range(half):
        one, other = joined(near, row), joined(far, row)
        zero = jnp.zeros_like(one)
        fill_row(padded, row, jnp.where(below, jnp.where(odd, one, other), zero))
        fill_row(padded, half + row, jnp.where(above, jnp.where(odd, other, one), zero))

    @pl.loop(0, depth // 8)
    def _(ct):
        c0 = pl.multiple_of(ct * 8, 8)
        for i in range(rows):
            lines = []
            for p in range(size):
                at = i + p - half
                if at < 0:
                    lines.append((at + half, p))
                elif at >= rows:
                    lines.append((at - rows + half, p))
            value = partial[i, pl.ds(c0, 8), :]
            if lines:
                total = tap_sum(padded, taps, c0, lines, size)
                value = value + total[:, LEAD : LEAD + nlon]
            emit(i, c0, value)


def joined(block, row):
    return jnp.concatenate([block[b, row].astype(F32) for b in range(block.shape[0])], axis=0)


def gelu_pair(x):
    scale = math.sqrt(2.0 / math.pi)
    square = x * x
    t = jnp.tanh(scale * x * (1.0 + 0.044715 * square))
    half = 0.5 * (1.0 + t)
    slope = half + 0.5 * x * (1.0 - t * t) * (scale * (1.0 + 3 * 0.044715 * square))
    return x * half, slope


def prepare_kernel(own, kernel, weight, pick, partial, taps, mixer, padded):
    members, rows, chans, nlon = own.shape
    size = kernel.shape[0]
    spread_taps(kernel, taps, False)
    for row in range(rows):
        fill_row(padded, row, joined(own, row))
    own_part(taps, partial, padded, size)
    for r in range(2):
        lines = []
        for b in range(members):
            lines.append(jnp.dot(pick[r, b], weight[...], preferred_element_type=F32))
        mixer[r] = jnp.concatenate(lines, axis=1).astype(BF16)


def forward_kernel(share, flags, near, far, partial, taps, table, mixer, out, slope, inner, outer, padded, act):
    rows, depth, nlon = partial.shape
    owners, groups, height, lanes = out.shape
    members, width, chans, _ = inner.shape
    size = math.isqrt(taps.shape[0])
    span = table.shape[1] // 2

    def emit(i, c0, value):
        value, grad = gelu_pair(value)
        act[i, pl.ds(c0, 8), :] = value
        slope[i, pl.ds(c0, 8), :] = grad

    halo_part(flags, near, far, taps, partial, padded, size, emit)
    odd = flags[0] == 1
    for row in range(width):
        first, last = slope[row], slope[rows - width + row]
        ours, theirs = jnp.where(odd, first, last), jnp.where(odd, last, first)
        for b in range(members):
            inner[b, row] = ours[b * chans : (b + 1) * chans].astype(BF16)
            outer[b, row] = theirs[b * chans : (b + 1) * chans].astype(BF16)
    flat = act[...].reshape(rows * depth, nlon).astype(BF16)
    spectral = jnp.dot(flat, table[...], preferred_element_type=F32).astype(BF16)
    mixed = []
    for i in range(rows):
        line = spectral[i * depth : (i + 1) * depth]
        mixed.append(
            jnp.dot(mixer[0], line[:, :span], preferred_element_type=F32)
            + jnp.dot(mixer[1], line[:, span:], preferred_element_type=F32)
        )
    for t in range(groups):
        pieces = [x[:, t * share : (t + 1) * share] for x in mixed]
        if lanes > rows * share:
            pieces.append(jnp.zeros((owners * height, lanes - rows * share), F32))
        block = jnp.concatenate(pieces, axis=1)
        for e in range(owners):
            out[e, t] = block[e * height : (e + 1) * height].astype(BF16)


def soft_sign(gaps):
    return gaps * lax.rsqrt(gaps * gaps + smooth_width * smooth_width)


def score_kernel(members, used, rows, halo, got, legendre, target, order, back, grads, spread, gather):
    owners, groups, height, lanes = got.shape
    orders, nlat, degrees = legendre.shape
    slots = target.shape[1]
    ens = owners * members
    for t in range(groups):
        pieces = []
        for e in range(owners):
            block = got[e, t].astype(F32)
            for b in range(members):
                pieces.append(block[b * used : (b + 1) * used])
                if slots > used:
                    pieces.append(jnp.zeros((slots - used, lanes), F32))
        block = jnp.concatenate(pieces, axis=0).T
        at = t * rows * orders
        spread[at : at + rows * orders, :] = block[: rows * orders]
    edge = halo * orders
    gather[:edge, :] = jnp.zeros((edge, ens * slots), F32)
    gather[edge + nlat * orders :, :] = jnp.zeros((edge, ens * slots), F32)

    @pl.loop(0, orders)
    def _(m):
        block = spread[pl.ds(m, nlat, stride=orders), :].astype(BF16)
        leg = legendre[m]
        coeff = lax.dot_general(
            block, leg, (((0,), (0,)), ((), ())), preferred_element_type=F32
        )
        own = [coeff[k * slots : (k + 1) * slots] for k in range(ens)]
        truth = target[m].astype(F32)
        sums = [None] * ens
        for k in range(ens):
            for n in range(k + 1, ens):
                sign = soft_sign(own[k] - own[n])
                sums[k] = sign if sums[k] is None else sums[k] + sign
                sums[n] = -sign if sums[n] is None else sums[n] - sign
        grad = jnp.concatenate(
            [
                soft_sign(own[k] - truth) * (1.0 / ens) - sums[k] * (1.0 / (ens * (ens - 1)))
                for k in range(ens)
            ],
            axis=0,
        ).astype(BF16)
        spec = lax.dot_general(
            leg, grad, (((1,), (1,)), ((), ())), preferred_element_type=F32
        )
        gather[pl.ds(edge + m, nlat, stride=orders), :] = spec
        at = pl.multiple_of(m * ens * slots, 8)
        ordered = jnp.dot(grad, order[...], preferred_element_type=F32)
        for j in range(grads.shape[0]):
            last = min(degrees, (j + 1) * 128)
            grads[j, pl.ds(at, ens * slots), : last - j * 128] = ordered[:, j * 128 : last]

    wide = back.shape[3]
    tall = (rows + 2 * halo) * orders
    for t in range(groups):
        at = t * rows * orders
        block = gather[at : at + tall, :]
        if wide > tall:
            block = jnp.concatenate([block, jnp.zeros((wide - tall, ens * slots), F32)], axis=0)
        block = block.T
        for e in range(owners):
            pieces = []
            for b in range(members):
                at = (e * members + b) * slots
                pieces.append(block[at : at + used])
            if height > members * used:
                pieces.append(jnp.zeros((height - members * used, wide), F32))
            back[e, t] = jnp.concatenate(pieces, axis=0).astype(BF16)


def backward_kernel(share, flags, got, near, far, kernel, mixer, table, slope, out, padded, taps, flat, stage):
    owners, groups, height, lanes = got.shape
    rows, depth, nlon = slope.shape
    members, _, chans, _ = out.shape
    size = kernel.shape[0]
    half = size // 2
    span = table.shape[1] // 2
    total = rows + 2 * half
    spread_taps(kernel, taps, True)
    blocks = [
        jnp.concatenate([got[e, t].astype(F32) for e in range(owners)], axis=0) for t in range(groups)
    ]
    lines = []
    for i in range(total):
        pieces = [x[:, i * share : (i + 1) * share] for x in blocks]
        pieces.append(jnp.zeros((owners * height, span - groups * share), F32))
        line = jnp.concatenate(pieces, axis=1).astype(BF16)
        lines.append(
            jnp.concatenate(
                [
                    lax.dot_general(
                        mixer[r], line, (((0,), (0,)), ((), ())), preferred_element_type=F32
                    ).astype(BF16)
                    for r in range(2)
                ],
                axis=1,
            )
        )
    flat[...] = lax.dot_general(
        jnp.concatenate(lines, axis=0),
        table[...],
        (((1,), (1,)), ((), ())),
        preferred_element_type=F32,
    ).reshape(flat.shape)
    odd = flags[0] == 1
    for row in range(half):
        one, other = joined(near, row), joined(far, row)
        fill_row(padded, row, flat[row] * jnp.where(odd, one, other))
        at = half + rows + row
        fill_row(padded, at, flat[at] * jnp.where(odd, other, one))
    for row in range(rows):
        fill_row(padded, half + row, flat[half + row] * slope[row])

    @pl.loop(0, depth // 8)
    def _(ct):
        c0 = pl.multiple_of(ct * 8, 8)

        @pl.loop(0, rows)
        def _(i):
            value = tap_sum(padded, taps, c0, [(i + p, p) for p in range(size)], size)
            stage[i, pl.ds(c0, 8), :] = value[:, LEAD : LEAD + nlon]

    for b in range(members):
        for i in range(rows):
            out[b, i] = stage[i, b * chans : (b + 1) * chans, :].astype(BF16)


def pack_kernel(members, used, per_owner, grads, out):
    owners, groups, depth, lanes = out.shape
    share = depth // members
    stride = grads.shape[1] // share
    slots = stride // (owners * members)
    for e in range(owners):
        for b in range(members):
            at = (e * members + b) * slots
            planes = [
                jnp.concatenate(
                    [grads[j, pl.ds(at + s, share, stride=stride), :] for j in range(grads.shape[0])],
                    axis=1,
                )
                for s in range(used)
            ]
            for t in range(groups):
                pieces = [x[:, t * per_owner : (t + 1) * per_owner] for x in planes]
                if lanes > used * per_owner:
                    pieces.append(jnp.zeros((share, lanes - used * per_owner), F32))
                out[e, t, b * share : (b + 1) * share, :] = jnp.concatenate(pieces, axis=1).astype(BF16)


def unpack_kernel(members, got, out):
    owners, groups, depth, lanes = got.shape
    _, chans, per_owner, _, orders = out.shape
    share, chan_share = depth // members, chans // owners
    row = lax.broadcasted_iota(jnp.int32, (groups * depth, orders), 0)
    column = lax.broadcasted_iota(jnp.int32, (groups * depth, orders), 1)
    for b in range(members):
        wanted = (column // share) * depth + b * share + column % share
        picker = jnp.where(row == wanted, 1.0, 0.0).astype(BF16)
        for e in range(owners):
            block = lax.dot_general(
                got[e].reshape(groups * depth, lanes),
                picker,
                (((0,), (0,)), ((), ())),
                preferred_element_type=F32,
            )
            for c in range(chan_share):
                for r in range(2):
                    at = (r * chan_share + c) * per_owner
                    out[b, e * chan_share + c, :, r, :] = block[at : at + per_owner]


def local(fields, depth_kernel, mix_weight, legendre, truth, degree_order):
    ens_parts, groups = lax.axis_size("ens"), lax.axis_size("lat")
    ens_at, lat_at = lax.axis_index("ens"), lax.axis_index("lat")
    members, chans, rows, nlon = fields.shape
    _, orders, degrees = legendre.shape
    ens = members * ens_parts
    nlat = rows * groups
    share, per_owner, chan_share = orders // groups, degrees // groups, chans // ens_parts
    used = 2 * chan_share
    slots = up(used, 8)
    height = up(members * used, 8)
    wide = up(nlon + 2 * LEAD, 128)
    span = up(orders, 128)
    size = depth_kernel.shape[1]
    halo = size // 2
    depth = members * chans

    table = jnp.asarray(wave_table(nlon, orders, span))
    kernel = depth_kernel.transpose(1, 2, 0)
    flags = place()
    own = fields.transpose(0, 2, 1, 3)
    odd = lat_at % 2
    near, far = partners(
        lax.dynamic_slice_in_dim(own, (1 - odd) * (rows - halo), halo, 1),
        lax.dynamic_slice_in_dim(own, odd * (rows - halo), halo, 1),
    )

    pick = np.zeros((2, members, ens_parts, height, chans), np.float32)
    for r in range(2):
        for b in range(members):
            for o in range(chans):
                at = b * used + r * chan_share + o % chan_share
                pick[r, b, o // chan_share, at, o] = 1.0
    pick = jnp.asarray(pick.reshape(2, members, ens_parts * height, chans).astype(jnp.bfloat16))

    vmem = pltpu.CompilerParams(vmem_limit_bytes=60 * 1024 * 1024)
    scalars = pl.BlockSpec(memory_space=pltpu.SMEM)
    whole = pl.BlockSpec(memory_space=pltpu.VMEM)
    grid_shape = (members, rows, chans, nlon)
    lined = jax.ShapeDtypeStruct((rows, depth, nlon), F32)
    edge = jax.ShapeDtypeStruct((members, halo, chans, nlon), BF16)
    taps_out = jax.ShapeDtypeStruct((size * size, depth, 128), F32)

    def call(body, outs, scratch, name, work, *args):
        specs = [scalars if a is flags else whole for a in args]
        return pl.pallas_call(
            body,
            out_shape=outs,
            in_specs=specs,
            scratch_shapes=scratch,
            compiler_params=vmem,
            cost_estimate=pl.CostEstimate(
                flops=work, transcendentals=0, bytes_accessed=8 * rows * depth * nlon
            ),
            name=name,
        )(*args)

    def swap(x):
        flat = x.reshape((ens_parts * groups,) + x.shape[2:])
        flat = lax.all_to_all(flat, ("ens", "lat"), split_axis=0, concat_axis=0, tiled=True)
        return flat.reshape(x.shape)

    work = 2 * size * size * rows * depth * nlon
    partial, taps, mixer = call(
        prepare_kernel,
        (lined, taps_out, jax.ShapeDtypeStruct((2, ens_parts * height, depth), BF16)),
        [pltpu.VMEM((rows, depth, wide), F32)],
        "prepare",
        work,
        own,
        kernel,
        mix_weight,
        pick,
    )
    legendre, partial = lax.optimization_barrier((legendre, partial))
    order_legendre = lax.all_to_all(legendre, "lat", split_axis=1, concat_axis=0, tiled=True)
    order_legendre = order_legendre.transpose(1, 0, 2)
    target = lax.dynamic_slice(
        truth, (ens_at * chan_share, 0, lat_at * share, 0), (chan_share, 2, share, degrees)
    )
    target = target.transpose(2, 1, 0, 3).reshape(share, used, degrees)
    target = jnp.pad(target, ((0, 0), (0, slots - used), (0, 0)))
    reorder = (jnp.arange(degrees)[:, None] == degree_order[None, :]).astype(BF16)

    def chunk(lines):
        return jax.ShapeDtypeStruct((ens_parts, groups, height, up(lines * share, 128)), BF16)

    sent, slope, inner, outer = call(
        functools.partial(forward_kernel, share),
        (chunk(rows), lined, edge, edge),
        [pltpu.VMEM((2 * halo, depth, wide), F32), pltpu.VMEM((rows, depth, nlon), F32)],
        "forward",
        work,
        flags,
        near,
        far,
        partial,
        taps,
        table,
        mixer,
    )
    got = swap(sent)
    near, far = partners(inner, outer)
    back, grads = call(
        functools.partial(score_kernel, members, used, rows, halo),
        (
            chunk(rows + 2 * halo),
            jax.ShapeDtypeStruct((up(degrees, 128) // 128, share * ens * slots, 128), F32),
        ),
        [
            pltpu.VMEM((nlat * share, ens * slots), F32),
            pltpu.VMEM(((nlat + 2 * halo) * share, ens * slots), F32),
        ],
        "score",
        work,
        got,
        order_legendre,
        target,
        reorder,
    )
    returned = swap(back)
    packed = call(
        functools.partial(pack_kernel, members, used, per_owner),
        jax.ShapeDtypeStruct(
            (ens_parts, groups, members * share, up(used * per_owner, 128)), BF16
        ),
        [],
        "pack",
        work,
        grads,
    )
    owned = swap(packed)
    grad_fields = call(
        functools.partial(backward_kernel, share),
        jax.ShapeDtypeStruct(grid_shape, BF16),
        [
            pltpu.VMEM((rows + 2 * halo, depth, wide), F32),
            pltpu.VMEM(taps_out.shape, F32),
            pltpu.VMEM((rows + 2 * halo, depth, nlon), F32),
            pltpu.VMEM((rows, depth, nlon), F32),
        ],
        "backward",
        work,
        flags,
        returned,
        near,
        far,
        kernel,
        mixer,
        table,
        slope,
    )
    score_grad = call(
        functools.partial(unpack_kernel, members),
        jax.ShapeDtypeStruct((members, chans, per_owner, 2, orders), F32),
        [],
        "unpack",
        work,
        owned,
    )
    return grad_fields.transpose(0, 2, 1, 3), score_grad.transpose(0, 1, 3, 4, 2)


def solution(mesh):
    placed = (P("ens", None, "lat", None), P(), P(), P("lat", None, None), P(), P())
    return jax.shard_map(
        local,
        mesh=mesh,
        in_specs=placed,
        out_specs=(P("ens", None, "lat", None), P("ens", None, None, None, "lat")),
        check_vma=False,
    )
```

time: 142 us -> 153 us (1.077)
  waiting for transfers between devices: 37.4 us -> 55.4 us
  Pallas kernels: 63.3 us -> 56.4 us
    ppermute x4, waiting for transfers between devices: 18.9 us -> 42.1 us  [partners(): return (lax.ppermute(inner, 'lat', near), lax.ppermute(outer, 'lat', far))]
    pallas_call x8 -> x6, Pallas kernels: 63.3 us -> 56.4 us  [call(): pl.pallas_call(body, out_shape=outs, in_specs=specs, scratch_shapes=scrat...]
    all_to_all x3, waiting for transfers between devices: 18.5 us -> 13.2 us  [swap(): lax.all_to_all(flat, ('ens', 'lat'), split_axis=0, concat_axis=0, tiled=T...]
    unnamed x22 -> x25, local copies, waits for them, and re-layouts: 7.13 us -> 5.68 us
  transfers between devices with their start and end apart: 8 -> 8, of which waited for: 4 -> 4; matrix products, arithmetic and copies ran while one was open for 4% -> 3% of each run, Pallas kernels for 34% -> 21%
where the time goes in v2:
time: 153 us; the launch traced here: 152 us
  Pallas kernels  56.4 us (37%)
  waiting for transfers between devices  55.4 us (36%)
  starting transfers between devices  28.3 us (18%)
  local copies, waits for them, and re-layouts  9.79 us (6%)
    pallas_call x6, Pallas kernels, call(): pl.pallas_call(body, out_shape=outs, in_specs=specs, scratch_shapes=scrat...  56.4 us
    ppermute x4, waiting for transfers between devices, partners(): return (lax.ppermute(inner, 'lat', near), lax.ppermute(outer, 'lat', far))  42.1 us
    all_to_all x3, waiting for transfers between devices, swap(): lax.all_to_all(flat, ('ens', 'lat'), split_axis=0, concat_axis=0, tiled=T...  13.2 us
    all_to_all x3, starting transfers between devices, swap(): lax.all_to_all(flat, ('ens', 'lat'), split_axis=0, concat_axis=0, tiled=T...  10.7 us
    ppermute x4, starting transfers between devices, partners(): return (lax.ppermute(inner, 'lat', near), lax.ppermute(outer, 'lat', far))  10.3 us
    all_to_all x1, starting transfers between devices, local(): lax.all_to_all(legendre, 'lat', split_axis=1, concat_axis=0, tiled=True)  7.31 us
    unnamed x25, local copies, waits for them, and re-layouts  5.68 us
  transfers between devices with their start and end apart: 8, of which 4 were waited for; matrix products, arithmetic and copies ran while one was open for 3% of the time, Pallas kernels for 21%

profile of v2, /device:TPU:0, one launch (start us, length us, event | category | flops | bytes accessed | tf_op | source)
XLA Modules:
  0.0 151.9 jit_solution(16799371851047166962)
XLA Ops:
  0.6 9.2 %prepare.1 = (f32[6,48,1440]{2,1,0:T(8,128)}, f32[49,48,128]{2,1,0:T(8,128)}, bf16[2,96,48]{2,1,0:T(8,128)(2,1)}) custom-call(bf16[2,6,24,1440]{3,2,1,0:T(8,128)(2,1)} %bitcast.32, f32[7,7,24]{2,1,0:T(8,128)} %bitcast.46, bf16[24,24]{1,0:T(8,128)(2,1)} %weight.1, bf16[2,2,96,24]{3,2,1,0:T(8,128)(2,1)} %constant.44.clone.pick), custom_call_target="tpu_custom_call" | custom-call | flops 40642560 | bytes 3317760 | tf_op jit(solution)/shard_map/prepare/pallas_call | solution.py:411
  9.9 1.3 copy.28
  11.2 1.5 %reshape.35 = bf16[8,2,9600]{2,1,0:T(2,128)(2,1)} reshape(bf16[160,6,160]{2,1,0:T(8,128)(2,1)S(1)} %bitcast.35) | data formatting | bytes 614400
  12.7 7.3 %all-to-all-start.1 = ((bf16[8,2,9600]{2,1,0:T(2,128)(2,1)}), bf16[8,2,9600]{2,1,0:T(2,128)(2,1)S(1)}, u32[]{:S(2)}, u32[]{:S(2)}) async-start(bf16[8,2,9600]{2,1,0:T(2,128)(2,1)} %reshape.35), calls=%async_computation.1 | async-start | bytes 614400 | tf_op jit(solution)/shard_map/all_to_all | solution.py:441
  20.2 2.1 %collective-permute-start = (bf16[2,3,24,1440]{3,2,1,0:T(8,128)(2,1)S(1)}, bf16[2,3,24,1440]{3,2,1,0:T(8,128)(2,1)S(1)}, u32[]{:S(2)}, u32[]{:S(2)}) collective-permute-start(bf16[2,3,24,1440]{3,2,1,0:T(8,128)(2,1)S(1)} %get-tuple-element.25), channel_id=1, source_target_pairs={{0,1},{1,0},{2,3},{3,2},{4,5},{5,4},{6,7},{7,6},{8,9},{9,8},{10,11... | collective-permute-start | bytes 1244168 | tf_op jit(solution)/shard_map/ppermute | solution.py:40
  22.2 3.3 %collective-permute-start.1 = (bf16[2,3,24,1440]{3,2,1,0:T(8,128)(2,1)S(1)}, bf16[2,3,24,1440]{3,2,1,0:T(8,128)(2,1)S(1)}, u32[]{:S(2)}, u32[]{:S(2)}) collective-permute-start(bf16[2,3,24,1440]{3,2,1,0:T(8,128)(2,1)S(1)} %get-tuple-element.24), channel_id=1, source_target_pairs={{0,7},{1,2},{2,1},{3,4},{4,3},{5,6},{6,5},{7,0},{8,15},{9,10},{10,... | collective-permute-start | bytes 1244168 | tf_op jit(solution)/shard_map/ppermute | solution.py:40
  26.1 18.5 %collective-permute-done.near = bf16[2,3,24,1440]{3,2,1,0:T(8,128)(2,1)S(1)} collective-permute-done((bf16[2,3,24,1440]{3,2,1,0:T(8,128)(2,1)S(1)}, bf16[2,3,24,1440]{3,2,1,0:T(8,128)(2,1)S(1)}, u32[]{:S(2)}, u32[]{:S(2)}) %collective-permute-start) | collective-permute-done | bytes 414752 | tf_op jit(solution)/shard_map/ppermute | solution.py:40
  45.6 11.1 %forward.1 = (bf16[4,8,24,128]{3,2,1,0:T(8,128)(2,1)}, f32[6,48,1440]{2,1,0:T(8,128)}, bf16[2,3,24,1440]{3,2,1,0:T(8,128)(2,1)}, bf16[2,3,24,1440]{3,2,1,0:T(8,128)(2,1)}) custom-call(s32[3]{0:T(128)} %pad_add_fusion.flags, bf16[2,3,24,1440]{3,2,1,0:T(8,128)(2,1)} %copy-done.6, bf16[2,3,24,1440]{3,2,1,0:T(8,128)(2,1)} %copy-done.7, ...), custom_call_target="tpu_custom_call" | custom-call | flops 40642560 | bytes 3317760 | tf_op jit(solution)/shard_map/forward/pallas_call | solution.py:411
  56.7 4.6 %all-to-all-start = ((bf16[32,24,128]{2,1,0:T(8,128)(2,1)}), bf16[32,24,128]{2,1,0:T(8,128)(2,1)S(1)}, u32[]{:S(2)}, u32[]{:S(2)}) async-start(bf16[32,24,128]{2,1,0:T(8,128)(2,1)} %bitcast.45), calls=%async_computation | async-start | bytes 393216 | tf_op jit(solution)/shard_map/all_to_all | solution.py:425
  61.2 1.0 constant_dynamic-slice_fusion
  64.5 0.9 copy.27
  65.4 4.1 %all-to-all-done = bf16[32,24,128]{2,1,0:T(8,128)(2,1)S(1)} async-done(((bf16[32,24,128]{2,1,0:T(8,128)(2,1)}), bf16[32,24,128]{2,1,0:T(8,128)(2,1)S(1)}, u32[]{:S(2)}, u32[]{:S(2)}) %all-to-all-start) | async-done | bytes 196640 | tf_op jit(solution)/shard_map/all_to_all | solution.py:425
  70.2 11.9 %score.1 = (bf16[4,8,24,256]{3,2,1,0:T(8,128)(2,1)}, f32[2,2560,128]{2,1,0:T(8,128)}) custom-call(bf16[4,8,24,128]{3,2,1,0:T(8,128)(2,1)} %bitcast.42, bf16[20,48,160]{2,1,0:T(8,128)(2,1)} %bitcast.39, bf16[20,16,160]{2,1,0:T(8,128)(2,1)} %pad.4.target, bf16[160,160]{1,0:T(8,128)(2,1)} %fusion.order), custom_call_target="tpu_custom_call" | custom-call | flops 40642560 | bytes 3317760 | tf_op jit(solution)/shard_map/score/pallas_call | solution.py:411
  82.1 3.3 %all-to-all-start.2 = ((bf16[32,24,256]{2,1,0:T(8,128)(2,1)}), bf16[32,24,256]{2,1,0:T(8,128)(2,1)S(1)}, u32[]{:S(2)}, u32[]{:S(2)}) async-start(bf16[32,24,256]{2,1,0:T(8,128)(2,1)} %bitcast.44), calls=%async_computation.2 | async-start | bytes 786432 | tf_op jit(solution)/shard_map/all_to_all | solution.py:425
  85.5 4.3 %pack.1 = bf16[4,8,40,256]{3,2,1,0:T(8,128)(2,1)} custom-call(f32[2,2560,128]{2,1,0:T(8,128)} %get-tuple-element.23.grads), custom_call_target="tpu_custom_call" | custom-call | flops 40642560 | bytes 3317760 | tf_op jit(solution)/shard_map/pack/pallas_call | solution.py:411
  89.7 9.2 %all-to-all-done.2 = bf16[32,24,256]{2,1,0:T(8,128)(2,1)S(1)} async-done(((bf16[32,24,256]{2,1,0:T(8,128)(2,1)}), bf16[32,24,256]{2,1,0:T(8,128)(2,1)S(1)}, u32[]{:S(2)}, u32[]{:S(2)}) %all-to-all-start.2) | async-done | bytes 393248 | tf_op jit(solution)/shard_map/all_to_all | solution.py:425
  98.9 2.8 %all-to-all-start.3 = ((bf16[32,40,256]{2,1,0:T(8,128)(2,1)}), bf16[32,40,256]{2,1,0:T(8,128)(2,1)S(1)}, u32[]{:S(2)}, u32[]{:S(2)}) async-start(bf16[32,40,256]{2,1,0:T(8,128)(2,1)} %bitcast.36), calls=%async_computation.3 | async-start | bytes 1310720 | tf_op jit(solution)/shard_map/all_to_all | solution.py:425
  101.7 1.5 %collective-permute-start.2 = (bf16[2,3,24,1440]{3,2,1,0:T(8,128)(2,1)S(1)}, bf16[2,3,24,1440]{3,2,1,0:T(8,128)(2,1)S(1)}, u32[]{:S(2)}, u32[]{:S(2)}) collective-permute-start(bf16[2,3,24,1440]{3,2,1,0:T(8,128)(2,1)S(1)} %copy-done.10), channel_id=1, source_target_pairs={{0,1},{1,0},{2,3},{3,2},{4,5},{5,4},{6,7},{7,6},{8,9},{9,8},{10,11... | collective-permute-start | bytes 1244168 | tf_op jit(solution)/shard_map/ppermute | solution.py:40
  103.2 3.4 %collective-permute-start.3 = (bf16[2,3,24,1440]{3,2,1,0:T(8,128)(2,1)S(1)}, bf16[2,3,24,1440]{3,2,1,0:T(8,128)(2,1)S(1)}, u32[]{:S(2)}, u32[]{:S(2)}) collective-permute-start(bf16[2,3,24,1440]{3,2,1,0:T(8,128)(2,1)S(1)} %copy-done.9), channel_id=1, source_target_pairs={{0,7},{1,2},{2,1},{3,4},{4,3},{5,6},{6,5},{7,0},{8,15},{9,10},{10,... | collective-permute-start | bytes 1244168 | tf_op jit(solution)/shard_map/ppermute | solution.py:40
  106.7 23.6 %collective-permute-done.2.near = bf16[2,3,24,1440]{3,2,1,0:T(8,128)(2,1)S(1)} collective-permute-done((bf16[2,3,24,1440]{3,2,1,0:T(8,128)(2,1)S(1)}, bf16[2,3,24,1440]{3,2,1,0:T(8,128)(2,1)S(1)}, u32[]{:S(2)}, u32[]{:S(2)}) %collective-permute-start.2) | collective-permute-done | bytes 414752 | tf_op jit(solution)/shard_map/ppermute | solution.py:40
  130.2 0.8 copy-done.4
  131.2 16.5 %backward.1 = bf16[2,6,24,1440]{3,2,1,0:T(8,128)(2,1)} custom-call(s32[3]{0:T(128)} %pad_add_fusion.flags, bf16[4,8,24,256]{3,2,1,0:T(8,128)(2,1)} %bitcast.40, bf16[2,3,24,1440]{3,2,1,0:T(8,128)(2,1)} %copy-done.4, bf16[2,3,24,1440]{3,2,1,0:T(8,128)(2,1)} %copy-done.5, f32[7,7,24]{2,1,0:T(8,128)} %bitcast.47, bf16[2,96,48]{2,1,0:T(8,128)(2,1)} %get-tuple-element.16.mixer, ...), custom_call_target="tpu_custom_call" | custom-call | flops 40642560 | bytes 3317760 | tf_op jit(solution)/shard_map/backward/pallas_call | solution.py:411
  147.7 0.9 copy-done.1
  148.5 3.4 %unpack.1 = f32[2,24,20,2,160]{4,3,2,1,0:T(2,128)} custom-call(bf16[4,8,40,256]{3,2,1,0:T(8,128)(2,1)} %bitcast.33), custom_call_target="tpu_custom_call" | custom-call | flops 40642560 | bytes 3317760 | tf_op jit(solution)/shard_map/unpack/pallas_call | solution.py:411
  (32 shorter events, 4.7 us)
Async XLA Ops:
  0.6 19.4 %copy-start = (bf16[2,24,6,1440]{3,1,2,0:T(8,128)(2,1)S(1)}, bf16[2,24,6,1440]{3,1,2,0:T(8,128)(2,1)}, u32[]{:S(2)}) copy-start(bf16[2,24,6,1440]{3,1,2,0:T(8,128)(2,1)} %param.8) | copy-start | bytes 2488324
  12.7 43.9 %all-to-all-start.1 = ((bf16[8,2,9600]{2,1,0:T(2,128)(2,1)}), bf16[8,2,9600]{2,1,0:T(2,128)(2,1)S(1)}, u32[]{:S(2)}, u32[]{:S(2)}) async-start(bf16[8,2,9600]{2,1,0:T(2,128)(2,1)} %reshape.35), calls=%async_computation.1 | async-start | bytes 614400 | tf_op jit(solution)/shard_map/all_to_all | solution.py:441
  20.2 24.5 %collective-permute-start = (bf16[2,3,24,1440]{3,2,1,0:T(8,128)(2,1)S(1)}, bf16[2,3,24,1440]{3,2,1,0:T(8,128)(2,1)S(1)}, u32[]{:S(2)}, u32[]{:S(2)}) collective-permute-start(bf16[2,3,24,1440]{3,2,1,0:T(8,128)(2,1)S(1)} %get-tuple-element.25), channel_id=1, source_target_pairs={{0,1},{1,0},{2,3},{3,2},{4,5},{5,4},{6,7},{7,6},{8,9},{9,8},{10,11... | collective-permute-start | bytes 1244168 | tf_op jit(solution)/shard_map/ppermute | solution.py:40
  22.2 22.4 %collective-permute-start.1 = (bf16[2,3,24,1440]{3,2,1,0:T(8,128)(2,1)S(1)}, bf16[2,3,24,1440]{3,2,1,0:T(8,128)(2,1)S(1)}, u32[]{:S(2)}, u32[]{:S(2)}) collective-permute-start(bf16[2,3,24,1440]{3,2,1,0:T(8,128)(2,1)S(1)} %get-tuple-element.24), channel_id=1, source_target_pairs={{0,7},{1,2},{2,1},{3,4},{4,3},{5,6},{6,5},{7,0},{8,15},{9,10},{10,... | collective-permute-start | bytes 1244168 | tf_op jit(solution)/shard_map/ppermute | solution.py:40
  44.6 0.8 copy-start.6
  44.7 0.9 copy-start.7
  45.6 17.4 %copy-start.8 = (s32[160]{0:T(256)S(1)}, s32[160]{0:T(256)}, u32[]{:S(2)}) copy-start(s32[160]{0:T(256)} %param.13) | copy-start | bytes 1924
  56.7 12.8 %all-to-all-start = ((bf16[32,24,128]{2,1,0:T(8,128)(2,1)}), bf16[32,24,128]{2,1,0:T(8,128)(2,1)S(1)}, u32[]{:S(2)}, u32[]{:S(2)}) async-start(bf16[32,24,128]{2,1,0:T(8,128)(2,1)} %bitcast.45), calls=%async_computation | async-start | bytes 393216 | tf_op jit(solution)/shard_map/all_to_all | solution.py:425
  69.5 0.7 copy-start.3
  82.1 16.8 %all-to-all-start.2 = ((bf16[32,24,256]{2,1,0:T(8,128)(2,1)}), bf16[32,24,256]{2,1,0:T(8,128)(2,1)S(1)}, u32[]{:S(2)}, u32[]{:S(2)}) async-start(bf16[32,24,256]{2,1,0:T(8,128)(2,1)} %bitcast.44), calls=%async_computation.2 | async-start | bytes 786432 | tf_op jit(solution)/shard_map/all_to_all | solution.py:425
  85.4 16.2 %copy-start.10 = (bf16[2,3,24,1440]{3,2,1,0:T(8,128)(2,1)S(1)}, bf16[2,3,24,1440]{3,2,1,0:T(8,128)(2,1)}, u32[]{:S(2)}) copy-start(bf16[2,3,24,1440]{3,2,1,0:T(8,128)(2,1)} %get-tuple-element.20) | copy-start | bytes 1244164
  85.4 17.8 %copy-start.9 = (bf16[2,3,24,1440]{3,2,1,0:T(8,128)(2,1)S(1)}, bf16[2,3,24,1440]{3,2,1,0:T(8,128)(2,1)}, u32[]{:S(2)}) copy-start(bf16[2,3,24,1440]{3,2,1,0:T(8,128)(2,1)} %get-tuple-element.21) | copy-start | bytes 1244164
  98.9 31.4 %copy-start.2 = (bf16[32,24,256]{2,1,0:T(8,128)(2,1)}, bf16[32,24,256]{2,1,0:T(8,128)(2,1)S(1)}, u32[]{:S(2)}) copy-start(bf16[32,24,256]{2,1,0:T(8,128)(2,1)S(1)} %all-to-all-done.2) | copy-start | bytes 1179652
  98.9 48.8 %all-to-all-start.3 = ((bf16[32,40,256]{2,1,0:T(8,128)(2,1)}), bf16[32,40,256]{2,1,0:T(8,128)(2,1)S(1)}, u32[]{:S(2)}, u32[]{:S(2)}) async-start(bf16[32,40,256]{2,1,0:T(8,128)(2,1)} %bitcast.36), calls=%async_computation.3 | async-start | bytes 1310720 | tf_op jit(solution)/shard_map/all_to_all | solution.py:425
  101.7 28.6 %collective-permute-start.2 = (bf16[2,3,24,1440]{3,2,1,0:T(8,128)(2,1)S(1)}, bf16[2,3,24,1440]{3,2,1,0:T(8,128)(2,1)S(1)}, u32[]{:S(2)}, u32[]{:S(2)}) collective-permute-start(bf16[2,3,24,1440]{3,2,1,0:T(8,128)(2,1)S(1)} %copy-done.10), channel_id=1, source_target_pairs={{0,1},{1,0},{2,3},{3,2},{4,5},{5,4},{6,7},{7,6},{8,9},{9,8},{10,11... | collective-permute-start | bytes 1244168 | tf_op jit(solution)/shard_map/ppermute | solution.py:40
  103.2 27.0 %collective-permute-start.3 = (bf16[2,3,24,1440]{3,2,1,0:T(8,128)(2,1)S(1)}, bf16[2,3,24,1440]{3,2,1,0:T(8,128)(2,1)S(1)}, u32[]{:S(2)}, u32[]{:S(2)}) collective-permute-start(bf16[2,3,24,1440]{3,2,1,0:T(8,128)(2,1)S(1)} %copy-done.9), channel_id=1, source_target_pairs={{0,7},{1,2},{2,1},{3,4},{4,3},{5,6},{6,5},{7,0},{8,15},{9,10},{10,... | collective-permute-start | bytes 1244168 | tf_op jit(solution)/shard_map/ppermute | solution.py:40
  130.2 0.8 copy-start.4
  130.2 0.9 copy-start.5
  147.7 0.9 copy-start.1

commit v3 on v2

--- a/solution.py
+++ b/solution.py
@@ -9,6 +9,7 @@
 from jax.experimental.pallas import tpu as pltpu
 from jax.sharding import PartitionSpec as P
 
+
 smooth_width = 0.5
 LEAD = 8
 F32 = jnp.float32
@@ -17,10 +18,6 @@
 
 def up(value, step):
     return -(-value // step) * step
-
-
-def full(shape):
-    return pl.BlockSpec(shape, lambda *_: (0,) * len(shape), memory_space=pltpu.VMEM)
 
 
 def wave_table(nlon, orders, span):
@@ -37,7 +34,9 @@
     count = lax.axis_size("lat")
     near = [(i, i ^ 1) for i in range(count)]
     far = [(i, (i + (1 if i % 2 else -1)) % count) for i in range(count)]
-    return lax.ppermute(inner, "lat", near), lax.ppermute(outer, "lat", far)
+    one = lax.ppermute(inner, "lat", near)
+    other = lax.ppermute(outer, "lat", far)
+    return one, other
 
 
 def place():
@@ -137,7 +136,7 @@
 
 
 def prepare_kernel(own, kernel, weight, pick, partial, taps, mixer, padded):
-    members, rows, chans, nlon = own.shape
+    members, rows, _, _ = own.shape
     size = kernel.shape[0]
     spread_taps(kernel, taps, False)
     for row in range(rows):
@@ -263,7 +262,7 @@
 
 
 def backward_kernel(share, flags, got, near, far, kernel, mixer, table, slope, out, padded, taps, flat, stage):
-    owners, groups, height, lanes = got.shape
+    owners, groups, height, _ = got.shape
     rows, depth, nlon = slope.shape
     members, _, chans, _ = out.shape
     size = kernel.shape[0]
@@ -406,7 +405,7 @@
     edge = jax.ShapeDtypeStruct((members, halo, chans, nlon), BF16)
     taps_out = jax.ShapeDtypeStruct((size * size, depth, 128), F32)
 
-    def call(body, outs, scratch, name, work, *args):
+    def call(body, outs, scratch, work, *args):
         specs = [scalars if a is flags else whole for a in args]
         return pl.pallas_call(
             body,
@@ -417,7 +416,6 @@
             cost_estimate=pl.CostEstimate(
                 flops=work, transcendentals=0, bytes_accessed=8 * rows * depth * nlon
             ),
-            name=name,
         )(*args)
 
     def swap(x):
@@ -430,7 +428,6 @@
         prepare_kernel,
         (lined, taps_out, jax.ShapeDtypeStruct((2, ens_parts * height, depth), BF16)),
         [pltpu.VMEM((rows, depth, wide), F32)],
-        "prepare",
         work,
         own,
         kernel,
@@ -454,7 +451,6 @@
         functools.partial(forward_kernel, share),
         (chunk(rows), lined, edge, edge),
         [pltpu.VMEM((2 * halo, depth, wide), F32), pltpu.VMEM((rows, depth, nlon), F32)],
-        "forward",
         work,
         flags,
         near,
@@ -465,6 +461,7 @@
         mixer,
     )
     got = swap(sent)
+    got, inner, outer = lax.optimization_barrier((got, inner, outer))
     near, far = partners(inner, outer)
     back, grads = call(
         functools.partial(score_kernel, members, used, rows, halo),
@@ -476,7 +473,6 @@
             pltpu.VMEM((nlat * share, ens * slots), F32),
             pltpu.VMEM(((nlat + 2 * halo) * share, ens * slots), F32),
         ],
-        "score",
         work,
         got,
         order_legendre,
@@ -490,7 +486,6 @@
             (ens_parts, groups, members * share, up(used * per_owner, 128)), BF16
         ),
         [],
-        "pack",
         work,
         grads,
     )
@@ -504,7 +499,6 @@
             pltpu.VMEM((rows + 2 * halo, depth, nlon), F32),
             pltpu.VMEM((rows, depth, nlon), F32),
         ],
-        "backward",
         work,
         flags,
         returned,
@@ -519,7 +513,6 @@
         functools.partial(unpack_kernel, members),
         jax.ShapeDtypeStruct((members, chans, per_owner, 2, orders), F32),
         [],
-        "unpack",
         work,
         owned,
     )
@@ -528,6 +521,7 @@
 
 def solution(mesh):
     placed = (P("ens", None, "lat", None), P(), P(), P("lat", None, None), P(), P())
+
     return jax.shard_map(
         local,
         mesh=mesh,

time: 153 us -> 153 us (level)
  no operation moved by 1% of the time
where the time goes in v3:
time: 153 us; the launch traced here: 152 us
  Pallas kernels  56.4 us (37%)
  waiting for transfers between devices  55.4 us (36%)
  starting transfers between devices  28.3 us (18%)
  local copies, waits for them, and re-layouts  9.79 us (6%)
    pallas_call x6, Pallas kernels, call(): pl.pallas_call(body, out_shape=outs, in_specs=specs, scratch_shapes=scrat...  56.4 us
    ppermute x2, waiting for transfers between devices, partners(): one = lax.ppermute(inner, 'lat', near)  42.1 us
    all_to_all x3, waiting for transfers between devices, swap(): lax.all_to_all(flat, ('ens', 'lat'), split_axis=0, concat_axis=0, tiled=T...  13.2 us
    all_to_all x3, starting transfers between devices, swap(): lax.all_to_all(flat, ('ens', 'lat'), split_axis=0, concat_axis=0, tiled=T...  10.7 us
    all_to_all x1, starting transfers between devices, local(): lax.all_to_all(legendre, 'lat', split_axis=1, concat_axis=0, tiled=True)  7.31 us
    ppermute x2, starting transfers between devices, partners(): other = lax.ppermute(outer, 'lat', far)  6.69 us
    unnamed x25, local copies, waits for them, and re-layouts  5.68 us
    ppermute x2, starting transfers between devices, partners(): one = lax.ppermute(inner, 'lat', near)  3.62 us
  transfers between devices with their start and end apart: 8, of which 4 were waited for; matrix products, arithmetic and copies ran while one was open for 3% of the time, Pallas kernels for 21%

profile of v3, /device:TPU:0, one launch (start us, length us, event | category | flops | bytes accessed | tf_op | source)
XLA Modules:
  0.0 151.9 jit_solution(16799371851047166962)
XLA Ops:
  0.6 9.2 %shard_map.95 = (f32[6,48,1440]{2,1,0:T(8,128)}, f32[49,48,128]{2,1,0:T(8,128)}, bf16[2,96,48]{2,1,0:T(8,128)(2,1)}) custom-call(bf16[2,6,24,1440]{3,2,1,0:T(8,128)(2,1)} %bitcast.32, f32[7,7,24]{2,1,0:T(8,128)} %bitcast.46, bf16[24,24]{1,0:T(8,128)(2,1)} %weight.1, bf16[2,2,96,24]{3,2,1,0:T(8,128)(2,1)} %constant.44.clone.pick), custom_call_target="tpu_custom_call" | custom-call | flops 40642560 | bytes 3317760 | tf_op jit(solution)/shard_map/pallas_call | solution.py:410
  9.9 1.3 copy.28
  11.2 1.5 %reshape.35 = bf16[8,2,9600]{2,1,0:T(2,128)(2,1)} reshape(bf16[160,6,160]{2,1,0:T(8,128)(2,1)S(1)} %bitcast.35) | data formatting | bytes 614400
  12.7 7.3 %all-to-all-start.1 = ((bf16[8,2,9600]{2,1,0:T(2,128)(2,1)}), bf16[8,2,9600]{2,1,0:T(2,128)(2,1)S(1)}, u32[]{:S(2)}, u32[]{:S(2)}) async-start(bf16[8,2,9600]{2,1,0:T(2,128)(2,1)} %reshape.35), calls=%async_computation.1 | async-start | bytes 614400 | tf_op jit(solution)/shard_map/all_to_all | solution.py:438
  20.2 2.1 %collective-permute-start = (bf16[2,3,24,1440]{3,2,1,0:T(8,128)(2,1)S(1)}, bf16[2,3,24,1440]{3,2,1,0:T(8,128)(2,1)S(1)}, u32[]{:S(2)}, u32[]{:S(2)}) collective-permute-start(bf16[2,3,24,1440]{3,2,1,0:T(8,128)(2,1)S(1)} %get-tuple-element.31), channel_id=1, source_target_pairs={{0,1},{1,0},{2,3},{3,2},{4,5},{5,4},{6,7},{7,6},{8,9},{9,8},{10,11... | collective-permute-start | bytes 1244168 | tf_op jit(solution)/shard_map/ppermute | solution.py:37
  22.2 3.3 %collective-permute-start.1 = (bf16[2,3,24,1440]{3,2,1,0:T(8,128)(2,1)S(1)}, bf16[2,3,24,1440]{3,2,1,0:T(8,128)(2,1)S(1)}, u32[]{:S(2)}, u32[]{:S(2)}) collective-permute-start(bf16[2,3,24,1440]{3,2,1,0:T(8,128)(2,1)S(1)} %get-tuple-element.30), channel_id=1, source_target_pairs={{0,7},{1,2},{2,1},{3,4},{4,3},{5,6},{6,5},{7,0},{8,15},{9,10},{10,... | collective-permute-start | bytes 1244168 | tf_op jit(solution)/shard_map/ppermute | solution.py:38
  26.1 18.5 %collective-permute-done.near = bf16[2,3,24,1440]{3,2,1,0:T(8,128)(2,1)S(1)} collective-permute-done((bf16[2,3,24,1440]{3,2,1,0:T(8,128)(2,1)S(1)}, bf16[2,3,24,1440]{3,2,1,0:T(8,128)(2,1)S(1)}, u32[]{:S(2)}, u32[]{:S(2)}) %collective-permute-start) | collective-permute-done | bytes 414752 | tf_op jit(solution)/shard_map/ppermute | solution.py:37
  45.6 11.1 %shard_map.96 = (bf16[4,8,24,128]{3,2,1,0:T(8,128)(2,1)}, f32[6,48,1440]{2,1,0:T(8,128)}, bf16[2,3,24,1440]{3,2,1,0:T(8,128)(2,1)}, bf16[2,3,24,1440]{3,2,1,0:T(8,128)(2,1)}) custom-call(s32[3]{0:T(128)} %pad_add_fusion.flags, bf16[2,3,24,1440]{3,2,1,0:T(8,128)(2,1)} %copy-done.6, bf16[2,3,24,1440]{3,2,1,0:T(8,128)(2,1)} %copy-done.7, ...), custom_call_target="tpu_custom_call" | custom-call | flops 40642560 | bytes 3317760 | tf_op jit(solution)/shard_map/pallas_call | solution.py:410
  56.7 4.6 %all-to-all-start = ((bf16[32,24,128]{2,1,0:T(8,128)(2,1)}), bf16[32,24,128]{2,1,0:T(8,128)(2,1)S(1)}, u32[]{:S(2)}, u32[]{:S(2)}) async-start(bf16[32,24,128]{2,1,0:T(8,128)(2,1)} %bitcast.45), calls=%async_computation | async-start | bytes 393216 | tf_op jit(solution)/shard_map/all_to_all | solution.py:423
  61.2 1.0 constant_dynamic-slice_fusion
  64.5 0.9 copy.27
  65.4 4.1 %all-to-all-done = bf16[32,24,128]{2,1,0:T(8,128)(2,1)S(1)} async-done(((bf16[32,24,128]{2,1,0:T(8,128)(2,1)}), bf16[32,24,128]{2,1,0:T(8,128)(2,1)S(1)}, u32[]{:S(2)}, u32[]{:S(2)}) %all-to-all-start) | async-done | bytes 196640 | tf_op jit(solution)/shard_map/all_to_all | solution.py:423
  70.2 11.9 %shard_map.97 = (bf16[4,8,24,256]{3,2,1,0:T(8,128)(2,1)}, f32[2,2560,128]{2,1,0:T(8,128)}) custom-call(bf16[4,8,24,128]{3,2,1,0:T(8,128)(2,1)} %bitcast.42, bf16[20,48,160]{2,1,0:T(8,128)(2,1)} %bitcast.39, bf16[20,16,160]{2,1,0:T(8,128)(2,1)} %pad.4.target, bf16[160,160]{1,0:T(8,128)(2,1)} %fusion.order), custom_call_target="tpu_custom_call" | custom-call | flops 40642560 | bytes 3317760 | tf_op jit(solution)/shard_map/pallas_call | solution.py:410
  82.1 3.3 %all-to-all-start.2 = ((bf16[32,24,256]{2,1,0:T(8,128)(2,1)}), bf16[32,24,256]{2,1,0:T(8,128)(2,1)S(1)}, u32[]{:S(2)}, u32[]{:S(2)}) async-start(bf16[32,24,256]{2,1,0:T(8,128)(2,1)} %bitcast.44), calls=%async_computation.2 | async-start | bytes 786432 | tf_op jit(solution)/shard_map/all_to_all | solution.py:423
  85.5 4.3 %shard_map.99 = bf16[4,8,40,256]{3,2,1,0:T(8,128)(2,1)} custom-call(f32[2,2560,128]{2,1,0:T(8,128)} %get-tuple-element.29.grads), custom_call_target="tpu_custom_call" | custom-call | flops 40642560 | bytes 3317760 | tf_op jit(solution)/shard_map/pallas_call | solution.py:410
  89.7 9.2 %all-to-all-done.2 = bf16[32,24,256]{2,1,0:T(8,128)(2,1)S(1)} async-done(((bf16[32,24,256]{2,1,0:T(8,128)(2,1)}), bf16[32,24,256]{2,1,0:T(8,128)(2,1)S(1)}, u32[]{:S(2)}, u32[]{:S(2)}) %all-to-all-start.2) | async-done | bytes 393248 | tf_op jit(solution)/shard_map/all_to_all | solution.py:423
  98.9 2.8 %all-to-all-start.3 = ((bf16[32,40,256]{2,1,0:T(8,128)(2,1)}), bf16[32,40,256]{2,1,0:T(8,128)(2,1)S(1)}, u32[]{:S(2)}, u32[]{:S(2)}) async-start(bf16[32,40,256]{2,1,0:T(8,128)(2,1)} %bitcast.36), calls=%async_computation.3 | async-start | bytes 1310720 | tf_op jit(solution)/shard_map/all_to_all | solution.py:423
  101.7 1.5 %collective-permute-start.2 = (bf16[2,3,24,1440]{3,2,1,0:T(8,128)(2,1)S(1)}, bf16[2,3,24,1440]{3,2,1,0:T(8,128)(2,1)S(1)}, u32[]{:S(2)}, u32[]{:S(2)}) collective-permute-start(bf16[2,3,24,1440]{3,2,1,0:T(8,128)(2,1)S(1)} %copy-done.10), channel_id=1, source_target_pairs={{0,1},{1,0},{2,3},{3,2},{4,5},{5,4},{6,7},{7,6},{8,9},{9,8},{10,11... | collective-permute-start | bytes 1244168 | tf_op jit(solution)/shard_map/ppermute | solution.py:37
  103.2 3.4 %collective-permute-start.3 = (bf16[2,3,24,1440]{3,2,1,0:T(8,128)(2,1)S(1)}, bf16[2,3,24,1440]{3,2,1,0:T(8,128)(2,1)S(1)}, u32[]{:S(2)}, u32[]{:S(2)}) collective-permute-start(bf16[2,3,24,1440]{3,2,1,0:T(8,128)(2,1)S(1)} %copy-done.9), channel_id=1, source_target_pairs={{0,7},{1,2},{2,1},{3,4},{4,3},{5,6},{6,5},{7,0},{8,15},{9,10},{10,... | collective-permute-start | bytes 1244168 | tf_op jit(solution)/shard_map/ppermute | solution.py:38
  106.7 23.6 %collective-permute-done.2.near = bf16[2,3,24,1440]{3,2,1,0:T(8,128)(2,1)S(1)} collective-permute-done((bf16[2,3,24,1440]{3,2,1,0:T(8,128)(2,1)S(1)}, bf16[2,3,24,1440]{3,2,1,0:T(8,128)(2,1)S(1)}, u32[]{:S(2)}, u32[]{:S(2)}) %collective-permute-start.2) | collective-permute-done | bytes 414752 | tf_op jit(solution)/shard_map/ppermute | solution.py:37
  130.2 0.8 copy-done.4
  131.2 16.5 %shard_map.98 = bf16[2,6,24,1440]{3,2,1,0:T(8,128)(2,1)} custom-call(s32[3]{0:T(128)} %pad_add_fusion.flags, bf16[4,8,24,256]{3,2,1,0:T(8,128)(2,1)} %bitcast.40, bf16[2,3,24,1440]{3,2,1,0:T(8,128)(2,1)} %copy-done.4, bf16[2,3,24,1440]{3,2,1,0:T(8,128)(2,1)} %copy-done.5, f32[7,7,24]{2,1,0:T(8,128)} %bitcast.47, bf16[2,96,48]{2,1,0:T(8,128)(2,1)} %get-tuple-element.19.mixer, ...), custom_call_target="tpu_custom_call" | custom-call | flops 40642560 | bytes 3317760 | tf_op jit(solution)/shard_map/pallas_call | solution.py:410
  147.7 0.9 copy-done.1
  148.5 3.4 %shard_map.100 = f32[2,24,20,2,160]{4,3,2,1,0:T(2,128)} custom-call(bf16[4,8,40,256]{3,2,1,0:T(8,128)(2,1)} %bitcast.33), custom_call_target="tpu_custom_call" | custom-call | flops 40642560 | bytes 3317760 | tf_op jit(solution)/shard_map/pallas_call | solution.py:410
  (32 shorter events, 4.7 us)
Async XLA Ops:
  0.6 19.4 %copy-start = (bf16[2,24,6,1440]{3,1,2,0:T(8,128)(2,1)S(1)}, bf16[2,24,6,1440]{3,1,2,0:T(8,128)(2,1)}, u32[]{:S(2)}) copy-start(bf16[2,24,6,1440]{3,1,2,0:T(8,128)(2,1)} %param.8) | copy-start | bytes 2488324
  12.7 43.9 %all-to-all-start.1 = ((bf16[8,2,9600]{2,1,0:T(2,128)(2,1)}), bf16[8,2,9600]{2,1,0:T(2,128)(2,1)S(1)}, u32[]{:S(2)}, u32[]{:S(2)}) async-start(bf16[8,2,9600]{2,1,0:T(2,128)(2,1)} %reshape.35), calls=%async_computation.1 | async-start | bytes 614400 | tf_op jit(solution)/shard_map/all_to_all | solution.py:438
  20.2 24.5 %collective-permute-start = (bf16[2,3,24,1440]{3,2,1,0:T(8,128)(2,1)S(1)}, bf16[2,3,24,1440]{3,2,1,0:T(8,128)(2,1)S(1)}, u32[]{:S(2)}, u32[]{:S(2)}) collective-permute-start(bf16[2,3,24,1440]{3,2,1,0:T(8,128)(2,1)S(1)} %get-tuple-element.31), channel_id=1, source_target_pairs={{0,1},{1,0},{2,3},{3,2},{4,5},{5,4},{6,7},{7,6},{8,9},{9,8},{10,11... | collective-permute-start | bytes 1244168 | tf_op jit(solution)/shard_map/ppermute | solution.py:37
  22.2 22.4 %collective-permute-start.1 = (bf16[2,3,24,1440]{3,2,1,0:T(8,128)(2,1)S(1)}, bf16[2,3,24,1440]{3,2,1,0:T(8,128)(2,1)S(1)}, u32[]{:S(2)}, u32[]{:S(2)}) collective-permute-start(bf16[2,3,24,1440]{3,2,1,0:T(8,128)(2,1)S(1)} %get-tuple-element.30), channel_id=1, source_target_pairs={{0,7},{1,2},{2,1},{3,4},{4,3},{5,6},{6,5},{7,0},{8,15},{9,10},{10,... | collective-permute-start | bytes 1244168 | tf_op jit(solution)/shard_map/ppermute | solution.py:38
  44.6 0.8 copy-start.6
  44.7 0.9 copy-start.7
  45.6 17.4 %copy-start.8 = (s32[160]{0:T(256)S(1)}, s32[160]{0:T(256)}, u32[]{:S(2)}) copy-start(s32[160]{0:T(256)} %param.13) | copy-start | bytes 1924
  56.7 12.8 %all-to-all-start = ((bf16[32,24,128]{2,1,0:T(8,128)(2,1)}), bf16[32,24,128]{2,1,0:T(8,128)(2,1)S(1)}, u32[]{:S(2)}, u32[]{:S(2)}) async-start(bf16[32,24,128]{2,1,0:T(8,128)(2,1)} %bitcast.45), calls=%async_computation | async-start | bytes 393216 | tf_op jit(solution)/shard_map/all_to_all | solution.py:423
  69.5 0.7 copy-start.3
  82.1 16.8 %all-to-all-start.2 = ((bf16[32,24,256]{2,1,0:T(8,128)(2,1)}), bf16[32,24,256]{2,1,0:T(8,128)(2,1)S(1)}, u32[]{:S(2)}, u32[]{:S(2)}) async-start(bf16[32,24,256]{2,1,0:T(8,128)(2,1)} %bitcast.44), calls=%async_computation.2 | async-start | bytes 786432 | tf_op jit(solution)/shard_map/all_to_all | solution.py:423
  85.4 16.2 %copy-start.10 = (bf16[2,3,24,1440]{3,2,1,0:T(8,128)(2,1)S(1)}, bf16[2,3,24,1440]{3,2,1,0:T(8,128)(2,1)}, u32[]{:S(2)}) copy-start(bf16[2,3,24,1440]{3,2,1,0:T(8,128)(2,1)} %get-tuple-element.26) | copy-start | bytes 1244164
  85.4 17.8 %copy-start.9 = (bf16[2,3,24,1440]{3,2,1,0:T(8,128)(2,1)S(1)}, bf16[2,3,24,1440]{3,2,1,0:T(8,128)(2,1)}, u32[]{:S(2)}) copy-start(bf16[2,3,24,1440]{3,2,1,0:T(8,128)(2,1)} %get-tuple-element.27) | copy-start | bytes 1244164
  98.9 31.4 %copy-start.2 = (bf16[32,24,256]{2,1,0:T(8,128)(2,1)}, bf16[32,24,256]{2,1,0:T(8,128)(2,1)S(1)}, u32[]{:S(2)}) copy-start(bf16[32,24,256]{2,1,0:T(8,128)(2,1)S(1)} %all-to-all-done.2) | copy-start | bytes 1179652
  98.9 48.8 %all-to-all-start.3 = ((bf16[32,40,256]{2,1,0:T(8,128)(2,1)}), bf16[32,40,256]{2,1,0:T(8,128)(2,1)S(1)}, u32[]{:S(2)}, u32[]{:S(2)}) async-start(bf16[32,40,256]{2,1,0:T(8,128)(2,1)} %bitcast.36), calls=%async_computation.3 | async-start | bytes 1310720 | tf_op jit(solution)/shard_map/all_to_all | solution.py:423
  101.7 28.6 %collective-permute-start.2 = (bf16[2,3,24,1440]{3,2,1,0:T(8,128)(2,1)S(1)}, bf16[2,3,24,1440]{3,2,1,0:T(8,128)(2,1)S(1)}, u32[]{:S(2)}, u32[]{:S(2)}) collective-permute-start(bf16[2,3,24,1440]{3,2,1,0:T(8,128)(2,1)S(1)} %copy-done.10), channel_id=1, source_target_pairs={{0,1},{1,0},{2,3},{3,2},{4,5},{5,4},{6,7},{7,6},{8,9},{9,8},{10,11... | collective-permute-start | bytes 1244168 | tf_op jit(solution)/shard_map/ppermute | solution.py:37
  103.2 27.0 %collective-permute-start.3 = (bf16[2,3,24,1440]{3,2,1,0:T(8,128)(2,1)S(1)}, bf16[2,3,24,1440]{3,2,1,0:T(8,128)(2,1)S(1)}, u32[]{:S(2)}, u32[]{:S(2)}) collective-permute-start(bf16[2,3,24,1440]{3,2,1,0:T(8,128)(2,1)S(1)} %copy-done.9), channel_id=1, source_target_pairs={{0,7},{1,2},{2,1},{3,4},{4,3},{5,6},{6,5},{7,0},{8,15},{9,10},{10,... | collective-permute-start | bytes 1244168 | tf_op jit(solution)/shard_map/ppermute | solution.py:38
  130.2 0.8 copy-start.4
  130.2 0.9 copy-start.5
  147.7 0.9 copy-start.1

commit v4 on v3

--- a/solution.py
+++ b/solution.py
@@ -11,7 +11,7 @@
 
 
 smooth_width = 0.5
-LEAD = 8
+TILE = 16
 F32 = jnp.float32
 BF16 = jnp.bfloat16
 
@@ -41,14 +41,19 @@
 
 def place():
     at, count = lax.axis_index("lat"), lax.axis_size("lat")
-    return jnp.stack([at % 2, at > 0, at < count - 1]).astype(jnp.int32)
-
-
-def fill_row(padded, row, value):
-    nlon, wide = value.shape[-1], padded.shape[-1]
-    padded[row] = jnp.concatenate(
-        [value[:, nlon - LEAD :], value, value[:, : wide - nlon - LEAD]], axis=-1
-    )
+    return jnp.stack([at % 2, (at > 0) & (at < count - 1)]).astype(jnp.int32)
+
+
+def fill_row(padded, row, value, half):
+    depth, nlon = value.shape
+    wide = padded.shape[-1]
+    base = nlon // 128 * 128
+    tail = [value[:, base:], value[:, :half]]
+    if wide > nlon + 2 * half:
+        tail.append(jnp.zeros((depth, wide - nlon - 2 * half), value.dtype))
+    tail.append(value[:, nlon - half :])
+    padded[row, :, :base] = value[:, :base].astype(padded.dtype)
+    padded[row, :, base:] = jnp.concatenate(tail, axis=-1).astype(padded.dtype)
 
 
 def tap_sum(padded, taps, c0, lines, size):
@@ -57,9 +62,10 @@
     for q in range(size):
         part = None
         for row, p in lines:
-            weight = jnp.tile(taps[p * size + q, pl.ds(c0, 8), :], (1, wide // 128))
-            term = weight * padded[row, pl.ds(c0, 8), :]
+            weight = jnp.tile(taps[p * size + q, pl.ds(c0, TILE), :], (1, wide // 128))
+            term = weight * padded[row, pl.ds(c0, TILE), :]
             part = term if part is None else part + term
+        part = part.astype(F32)
         shift = (size // 2 - q) % wide
         if shift:
             part = pltpu.roll(part, shift, 1)
@@ -72,54 +78,11 @@
     for p in range(size):
         plane = kernel[p].T
         for q in range(size):
-            value = plane[:, q : q + 1]
-            if p == q == size // 2:
-                value = value + 1.0
             at = p * size + q
             at = size * size - 1 - at if flip else at
-            value = jnp.broadcast_to(value, (chans, 128))
-            taps[at] = jnp.concatenate([value] * (taps.shape[1] // chans), axis=0)
-
-
-def own_part(taps, partial, padded, size):
-    rows, depth, nlon = partial.shape
-    half = size // 2
-
-    @pl.loop(0, depth // 8)
-    def _(ct):
-        c0 = pl.multiple_of(ct * 8, 8)
-        for i in range(rows):
-            lines = [(i + p - half, p) for p in range(size) if 0 <= i + p - half < rows]
-            total = tap_sum(padded, taps, c0, lines, size)
-            partial[i, pl.ds(c0, 8), :] = total[:, LEAD : LEAD + nlon]
-
-
-def halo_part(flags, near, far, taps, partial, padded, size, emit):
-    rows, depth, nlon = partial.shape
-    half = size // 2
-    odd, below, above = flags[0] == 1, flags[1] == 1, flags[2] == 1
-    for row in range(half):
-        one, other = joined(near, row), joined(far, row)
-        zero = jnp.zeros_like(one)
-        fill_row(padded, row, jnp.where(below, jnp.where(odd, one, other), zero))
-        fill_row(padded, half + row, jnp.where(above, jnp.where(odd, other, one), zero))
-
-    @pl.loop(0, depth // 8)
-    def _(ct):
-        c0 = pl.multiple_of(ct * 8, 8)
-        for i in range(rows):
-            lines = []
-            for p in range(size):
-                at = i + p - half
-                if at < 0:
-                    lines.append((at + half, p))
-                elif at >= rows:
-                    lines.append((at - rows + half, p))
-            value = partial[i, pl.ds(c0, 8), :]
-            if lines:
-                total = tap_sum(padded, taps, c0, lines, size)
-                value = value + total[:, LEAD : LEAD + nlon]
-            emit(i, c0, value)
+            value = jnp.broadcast_to(plane[:, q : q + 1], (chans, 128))
+            value = jnp.concatenate([value] * (taps.shape[1] // chans), axis=0)
+            taps[at] = value.astype(taps.dtype)
 
 
 def joined(block, row):
@@ -136,12 +99,23 @@
 
 
 def prepare_kernel(own, kernel, weight, pick, partial, taps, mixer, padded):
-    members, rows, _, _ = own.shape
+    members, rows, chans, nlon = own.shape
+    depth = members * chans
     size = kernel.shape[0]
+    half = size // 2
     spread_taps(kernel, taps, False)
     for row in range(rows):
-        fill_row(padded, row, joined(own, row))
-    own_part(taps, partial, padded, size)
+        fill_row(padded, row, joined(own, row), half)
+
+    @pl.loop(0, depth // TILE)
+    def _(ct):
+        c0 = pl.multiple_of(ct * TILE, TILE)
+        for i in range(rows):
+            lines = [(i + p - half, p) for p in range(size) if 0 <= i + p - half < rows]
+            total = tap_sum(padded, taps, c0, lines, size)
+            total = total + padded[i, pl.ds(c0, TILE), :].astype(F32)
+            partial[i, pl.ds(c0, TILE), :] = total[:, :nlon]
+
     for r in range(2):
         lines = []
         for b in range(members):
@@ -149,42 +123,67 @@
         mixer[r] = jnp.concatenate(lines, axis=1).astype(BF16)
 
 
-def forward_kernel(share, flags, near, far, partial, taps, table, mixer, out, slope, inner, outer, padded, act):
+def finish_rows(lower, present, edge, partial, taps, table, mixer, slope, padded, act):
     rows, depth, nlon = partial.shape
-    owners, groups, height, lanes = out.shape
-    members, width, chans, _ = inner.shape
     size = math.isqrt(taps.shape[0])
+    half = size // 2
     span = table.shape[1] // 2
-
-    def emit(i, c0, value):
-        value, grad = gelu_pair(value)
-        act[i, pl.ds(c0, 8), :] = value
-        slope[i, pl.ds(c0, 8), :] = grad
-
-    halo_part(flags, near, far, taps, partial, padded, size, emit)
-    odd = flags[0] == 1
-    for row in range(width):
-        first, last = slope[row], slope[rows - width + row]
-        ours, theirs = jnp.where(odd, first, last), jnp.where(odd, last, first)
-        for b in range(members):
-            inner[b, row] = ours[b * chans : (b + 1) * chans].astype(BF16)
-            outer[b, row] = theirs[b * chans : (b + 1) * chans].astype(BF16)
-    flat = act[...].reshape(rows * depth, nlon).astype(BF16)
+    for row in range(half):
+        at = jnp.where(lower, row, half - 1 - row)
+        value = joined(edge, at)
+        if present is not None:
+            value = jnp.where(present, value, jnp.zeros_like(value))
+        fill_row(padded, row, value, half)
+
+    @pl.loop(0, depth // TILE)
+    def _(ct):
+        c0 = pl.multiple_of(ct * TILE, TILE)
+        for j in range(half):
+            lines = [
+                (row, jnp.where(lower, row - j, size - 1 - (row - j))) for row in range(j, half)
+            ]
+            at = jnp.where(lower, j, half - 1 - j)
+            value = partial[jnp.where(lower, j, rows - 1 - j), pl.ds(c0, TILE), :]
+            value = value + tap_sum(padded, taps, c0, lines, size)[:, :nlon]
+            value, grad = gelu_pair(value)
+            act[at, pl.ds(c0, TILE), :] = value.astype(BF16)
+            slope[at, pl.ds(c0, TILE), :] = grad.astype(BF16)
+
+    flat = act[...].reshape(half * depth, nlon)
     spectral = jnp.dot(flat, table[...], preferred_element_type=F32).astype(BF16)
     mixed = []
-    for i in range(rows):
-        line = spectral[i * depth : (i + 1) * depth]
+    for j in range(half):
+        line = spectral[j * depth : (j + 1) * depth]
         mixed.append(
             jnp.dot(mixer[0], line[:, :span], preferred_element_type=F32)
             + jnp.dot(mixer[1], line[:, span:], preferred_element_type=F32)
         )
+    return mixed
+
+
+def near_kernel(flags, edge, partial, taps, table, mixer, mixed, slope, padded, act):
+    lines = finish_rows(flags[0] == 1, None, edge, partial, taps, table, mixer, slope, padded, act)
+    for j, line in enumerate(lines):
+        mixed[j] = line
+
+
+def far_kernel(share, flags, edge, partial, taps, table, mixer, nearer, out, slope, padded, act):
+    owners, groups, height, lanes = out.shape
+    lines = finish_rows(
+        flags[0] != 1, flags[1] == 1, edge, partial, taps, table, mixer, slope, padded, act
+    )
+    lines = [nearer[j] for j in range(nearer.shape[0])] + lines
     for t in range(groups):
-        pieces = [x[:, t * share : (t + 1) * share] for x in mixed]
-        if lanes > rows * share:
-            pieces.append(jnp.zeros((owners * height, lanes - rows * share), F32))
+        pieces = [x[:, t * share : (t + 1) * share] for x in lines]
+        if lanes > len(lines) * share:
+            pieces.append(jnp.zeros((owners * height, lanes - len(lines) * share), F32))
         block = jnp.concatenate(pieces, axis=1)
         for e in range(owners):
             out[e, t] = block[e * height : (e + 1) * height].astype(BF16)
+
+
+def flip_kernel(kernel, taps):
+    spread_taps(kernel, taps, True)
 
 
 def soft_sign(gaps):
@@ -205,14 +204,15 @@
                 if slots > used:
                     pieces.append(jnp.zeros((slots - used, lanes), F32))
         block = jnp.concatenate(pieces, axis=0).T
-        at = t * rows * orders
-        spread[at : at + rows * orders, :] = block[: rows * orders]
+        at, part = t * rows * orders, halo * orders
+        first, second = (at, at + part) if t % 2 else (at + part, at)
+        spread[first : first + part, :] = block[:part]
+        spread[second : second + part, :] = block[part : 2 * part]
     edge = halo * orders
     gather[:edge, :] = jnp.zeros((edge, ens * slots), F32)
     gather[edge + nlat * orders :, :] = jnp.zeros((edge, ens * slots), F32)
 
-    @pl.loop(0, orders)
-    def _(m):
+    def one(m):
         block = spread[pl.ds(m, nlat, stride=orders), :].astype(BF16)
         leg = legendre[m]
         coeff = lax.dot_general(
@@ -243,6 +243,13 @@
             last = min(degrees, (j + 1) * 128)
             grads[j, pl.ds(at, ens * slots), : last - j * 128] = ordered[:, j * 128 : last]
 
+    step = 4 if orders % 4 == 0 else 1
+
+    @pl.loop(0, orders // step)
+    def _(trip):
+        for j in range(step):
+            one(trip * step + j)
+
     wide = back.shape[3]
     tall = (rows + 2 * halo) * orders
     for t in range(groups):
@@ -261,15 +268,13 @@
             back[e, t] = jnp.concatenate(pieces, axis=0).astype(BF16)
 
 
-def backward_kernel(share, flags, got, near, far, kernel, mixer, table, slope, out, padded, taps, flat, stage):
+def backward_kernel(share, flags, got, near, far, inner, outer, taps, mixer, table, out, padded, flat, stage):
     owners, groups, height, _ = got.shape
-    rows, depth, nlon = slope.shape
-    members, _, chans, _ = out.shape
-    size = kernel.shape[0]
-    half = size // 2
+    half, depth, nlon = inner.shape
+    members, rows, chans, _ = out.shape
+    size = math.isqrt(taps.shape[0])
     span = table.shape[1] // 2
     total = rows + 2 * half
-    spread_taps(kernel, taps, True)
     blocks = [
         jnp.concatenate([got[e, t].astype(F32) for e in range(owners)], axis=0) for t in range(groups)
     ]
@@ -296,22 +301,22 @@
         preferred_element_type=F32,
     ).reshape(flat.shape)
     odd = flags[0] == 1
-    for row in range(half):
-        one, other = joined(near, row), joined(far, row)
-        fill_row(padded, row, flat[row] * jnp.where(odd, one, other))
-        at = half + rows + row
-        fill_row(padded, at, flat[at] * jnp.where(odd, other, one))
-    for row in range(rows):
-        fill_row(padded, half + row, flat[half + row] * slope[row])
-
-    @pl.loop(0, depth // 8)
+    pairs = ((near, far), (inner, outer), (outer, inner), (far, near))
+    for part, (one, other) in enumerate(pairs):
+        for row in range(half):
+            at = part * half + row
+            slope = jnp.where(odd, one[row].astype(F32), other[row].astype(F32))
+            fill_row(padded, at, flat[at] * slope, half)
+
+    @pl.loop(0, depth // TILE)
     def _(ct):
-        c0 = pl.multiple_of(ct * 8, 8)
+        c0 = pl.multiple_of(ct * TILE, TILE)
 
         @pl.loop(0, rows)
         def _(i):
             value = tap_sum(padded, taps, c0, [(i + p, p) for p in range(size)], size)
-            stage[i, pl.ds(c0, 8), :] = value[:, LEAD : LEAD + nlon]
+            value = value + padded[i + half, pl.ds(c0, TILE), :].astype(F32)
+            stage[i, pl.ds(c0, TILE), :] = value[:, :nlon]
 
     for b in range(members):
         for i in range(rows):
@@ -373,10 +378,10 @@
     used = 2 * chan_share
     slots = up(used, 8)
     height = up(members * used, 8)
-    wide = up(nlon + 2 * LEAD, 128)
     span = up(orders, 128)
     size = depth_kernel.shape[1]
     halo = size // 2
+    wide = up(nlon + 2 * halo, 128)
     depth = members * chans
 
     table = jnp.asarray(wave_table(nlon, orders, span))
@@ -402,8 +407,8 @@
     whole = pl.BlockSpec(memory_space=pltpu.VMEM)
     grid_shape = (members, rows, chans, nlon)
     lined = jax.ShapeDtypeStruct((rows, depth, nlon), F32)
-    edge = jax.ShapeDtypeStruct((members, halo, chans, nlon), BF16)
-    taps_out = jax.ShapeDtypeStruct((size * size, depth, 128), F32)
+    edge = jax.ShapeDtypeStruct((halo, depth, nlon), BF16)
+    taps_out = jax.ShapeDtypeStruct((size * size, depth, 128), BF16)
 
     def call(body, outs, scratch, work, *args):
         specs = [scalars if a is flags else whole for a in args]
@@ -427,7 +432,7 @@
     partial, taps, mixer = call(
         prepare_kernel,
         (lined, taps_out, jax.ShapeDtypeStruct((2, ens_parts * height, depth), BF16)),
-        [pltpu.VMEM((rows, depth, wide), F32)],
+        [pltpu.VMEM((rows, depth, wide), BF16)],
         work,
         own,
         kernel,
@@ -447,18 +452,31 @@
     def chunk(lines):
         return jax.ShapeDtypeStruct((ens_parts, groups, height, up(lines * share, 128)), BF16)
 
-    sent, slope, inner, outer = call(
-        functools.partial(forward_kernel, share),
-        (chunk(rows), lined, edge, edge),
-        [pltpu.VMEM((2 * halo, depth, wide), F32), pltpu.VMEM((rows, depth, nlon), F32)],
-        work,
+    half_scratch = [pltpu.VMEM((halo, depth, wide), BF16), pltpu.VMEM((halo, depth, nlon), BF16)]
+    mixed, inner = call(
+        near_kernel,
+        (jax.ShapeDtypeStruct((halo, ens_parts * height, span), F32), edge),
+        half_scratch,
+        work // 2,
         flags,
         near,
+        partial,
+        taps,
+        table,
+        mixer,
+    )
+    sent, outer = call(
+        functools.partial(far_kernel, share),
+        (chunk(rows), edge),
+        half_scratch,
+        work // 2,
+        flags,
         far,
         partial,
         taps,
         table,
         mixer,
+        mixed,
     )
     got = swap(sent)
     got, inner, outer = lax.optimization_barrier((got, inner, outer))
@@ -490,12 +508,12 @@
         grads,
     )
     owned = swap(packed)
+    flipped = call(flip_kernel, taps_out, [], work // 8, kernel)
     grad_fields = call(
         functools.partial(backward_kernel, share),
         jax.ShapeDtypeStruct(grid_shape, BF16),
         [
-            pltpu.VMEM((rows + 2 * halo, depth, wide), F32),
-            pltpu.VMEM(taps_out.shape, F32),
+            pltpu.VMEM((rows + 2 * halo, depth, wide), BF16),
             pltpu.VMEM((rows + 2 * halo, depth, nlon), F32),
             pltpu.VMEM((rows, depth, nlon), F32),
         ],
@@ -504,10 +522,11 @@
         returned,
         near,
         far,
-        kernel,
+        inner,
+        outer,
+        flipped,
         mixer,
         table,
-        slope,
     )
     score_grad = call(
         functools.partial(unpack_kernel, members),

time: 153 us -> 141 us (0.922)
  Pallas kernels: 56.4 us -> 46.4 us
  waiting for transfers between devices: 55.4 us -> 53.6 us
    pallas_call x6 -> x8, Pallas kernels: 56.4 us -> 46.4 us  [call(): pl.pallas_call(body, out_shape=outs, in_specs=specs, scratch_shapes=scrat...]
    ppermute x2, waiting for transfers between devices: 42.1 us -> 40.2 us  [partners(): one = lax.ppermute(inner, 'lat', near)]
  transfers between devices with their start and end apart: 8 -> 8, of which waited for: 4 -> 4; matrix products, arithmetic and copies ran while one was open for 3% -> 3% of each run, Pallas kernels for 21% -> 19%
where the time goes in v4:
time: 141 us
  waiting for transfers between devices  53.6 us (38%)
  Pallas kernels  46.4 us (33%)
  starting transfers between devices  28.3 us (20%)
  local copies, waits for them, and re-layouts  10.4 us (7%)
    pallas_call x8, Pallas kernels, call(): pl.pallas_call(body, out_shape=outs, in_specs=specs, scratch_shapes=scrat...  46.4 us
    ppermute x2, waiting for transfers between devices, partners(): one = lax.ppermute(inner, 'lat', near)  40.2 us
    all_to_all x3, waiting for transfers between devices, swap(): lax.all_to_all(flat, ('ens', 'lat'), split_axis=0, concat_axis=0, tiled=T...  13.4 us
    all_to_all x3, starting transfers between devices, swap(): lax.all_to_all(flat, ('ens', 'lat'), split_axis=0, concat_axis=0, tiled=T...  10.7 us
    all_to_all x1, starting transfers between devices, local(): lax.all_to_all(legendre, 'lat', split_axis=1, concat_axis=0, tiled=True)  7.31 us
    ppermute x2, starting transfers between devices, partners(): other = lax.ppermute(outer, 'lat', far)  6.69 us
    unnamed x25, local copies, waits for them, and re-layouts  6.29 us
    ppermute x2, starting transfers between devices, partners(): one = lax.ppermute(inner, 'lat', near)  3.62 us
  transfers between devices with their start and end apart: 8, of which 4 were waited for; matrix products, arithmetic and copies ran while one was open for 3% of the time, Pallas kernels for 19%

profile of v4, /device:TPU:0, one launch (start us, length us, event | category | flops | bytes accessed | tf_op | source)
XLA Modules:
  0.0 140.7 jit_solution(2090622651593429349)
XLA Ops:
  0.6 6.6 %shard_map.95 = (f32[6,48,1440]{2,1,0:T(8,128)}, bf16[49,48,128]{2,1,0:T(8,128)(2,1)}, bf16[2,96,48]{2,1,0:T(8,128)(2,1)}) custom-call(bf16[2,6,24,1440]{3,2,1,0:T(8,128)(2,1)} %bitcast.31, f32[7,7,24]{2,1,0:T(8,128)} %bitcast.45, bf16[24,24]{1,0:T(8,128)(2,1)} %weight.1, bf16[2,2,96,24]{3,2,1,0:T(8,128)(2,1)} %constant.44.clone.pick), custom_call_target="tpu_custom_call" | custom-call | flops 40642560 | bytes 3317760 | tf_op jit(solution)/shard_map/pallas_call | solution.py:415
  7.2 1.3 copy.28
  8.5 1.5 %reshape.34 = bf16[8,2,9600]{2,1,0:T(2,128)(2,1)} reshape(bf16[160,6,160]{2,1,0:T(8,128)(2,1)S(1)} %bitcast.34) | data formatting | bytes 614400
  10.0 7.3 %all-to-all-start.1 = ((bf16[8,2,9600]{2,1,0:T(2,128)(2,1)}), bf16[8,2,9600]{2,1,0:T(2,128)(2,1)S(1)}, u32[]{:S(2)}, u32[]{:S(2)}) async-start(bf16[8,2,9600]{2,1,0:T(2,128)(2,1)} %reshape.34), calls=%async_computation.1 | async-start | bytes 614400 | tf_op jit(solution)/shard_map/all_to_all | solution.py:443
  17.4 2.1 %collective-permute-start.1 = (bf16[2,3,24,1440]{3,2,1,0:T(8,128)(2,1)S(1)}, bf16[2,3,24,1440]{3,2,1,0:T(8,128)(2,1)S(1)}, u32[]{:S(2)}, u32[]{:S(2)}) collective-permute-start(bf16[2,3,24,1440]{3,2,1,0:T(8,128)(2,1)S(1)} %get-tuple-element.30), channel_id=1, source_target_pairs={{0,1},{1,0},{2,3},{3,2},{4,5},{5,4},{6,7},{7,6},{8,9},{9,8},{10,11... | collective-permute-start | bytes 1244168 | tf_op jit(solution)/shard_map/ppermute | solution.py:37
  19.5 3.3 %collective-permute-start = (bf16[2,3,24,1440]{3,2,1,0:T(8,128)(2,1)S(1)}, bf16[2,3,24,1440]{3,2,1,0:T(8,128)(2,1)S(1)}, u32[]{:S(2)}, u32[]{:S(2)}) collective-permute-start(bf16[2,3,24,1440]{3,2,1,0:T(8,128)(2,1)S(1)} %get-tuple-element.31), channel_id=1, source_target_pairs={{0,7},{1,2},{2,1},{3,4},{4,3},{5,6},{6,5},{7,0},{8,15},{9,10},{10,... | collective-permute-start | bytes 1244168 | tf_op jit(solution)/shard_map/ppermute | solution.py:38
  23.4 18.5 %collective-permute-done.1.edge = bf16[2,3,24,1440]{3,2,1,0:T(8,128)(2,1)S(1)} collective-permute-done((bf16[2,3,24,1440]{3,2,1,0:T(8,128)(2,1)S(1)}, bf16[2,3,24,1440]{3,2,1,0:T(8,128)(2,1)S(1)}, u32[]{:S(2)}, u32[]{:S(2)}) %collective-permute-start.1) | collective-permute-done | bytes 414752 | tf_op jit(solution)/shard_map/ppermute | solution.py:37
  42.7 5.4 %shard_map.96 = (f32[3,96,256]{2,1,0:T(8,128)}, bf16[3,48,1440]{2,1,0:T(8,128)(2,1)}) custom-call(s32[2]{0:T(128)} %pad_add_fusion.flags, bf16[2,3,24,1440]{3,2,1,0:T(8,128)(2,1)} %copy-done.9, f32[6,48,1440]{2,1,0:T(8,128)} %get-tuple-element.17.partial, bf16[49,48,128]{2,1,0:T(8,128)(2,1)} %get-tuple-element.18.taps, ...), custom_call_target="tpu_custom_call" | custom-call | flops 20321280 | bytes 3317760 | tf_op jit(solution)/shard_map/pallas_call | solution.py:415
  48.9 5.6 %shard_map.97 = (bf16[4,8,24,128]{3,2,1,0:T(8,128)(2,1)}, bf16[3,48,1440]{2,1,0:T(8,128)(2,1)}) custom-call(s32[2]{0:T(128)} %pad_add_fusion.flags, bf16[2,3,24,1440]{3,2,1,0:T(8,128)(2,1)} %copy-done.8, f32[6,48,1440]{2,1,0:T(8,128)} %get-tuple-element.17.partial, bf16[49,48,128]{2,1,0:T(8,128)(2,1)} %get-tuple-element.18.taps, ...), custom_call_target="tpu_custom_call" | custom-call | flops 20321280 | bytes 3317760 | tf_op jit(solution)/shard_map/pallas_call | solution.py:415
  54.5 4.6 %all-to-all-start = ((bf16[32,24,128]{2,1,0:T(8,128)(2,1)}), bf16[32,24,128]{2,1,0:T(8,128)(2,1)S(1)}, u32[]{:S(2)}, u32[]{:S(2)}) async-start(bf16[32,24,128]{2,1,0:T(8,128)(2,1)} %bitcast.44), calls=%async_computation | async-start | bytes 393216 | tf_op jit(solution)/shard_map/all_to_all | solution.py:428
  59.0 1.0 constant_dynamic-slice_fusion
  62.3 0.9 copy.27
  63.2 4.1 %all-to-all-done = bf16[32,24,128]{2,1,0:T(8,128)(2,1)S(1)} async-done(((bf16[32,24,128]{2,1,0:T(8,128)(2,1)}), bf16[32,24,128]{2,1,0:T(8,128)(2,1)S(1)}, u32[]{:S(2)}, u32[]{:S(2)}) %all-to-all-start) | async-done | bytes 196640 | tf_op jit(solution)/shard_map/all_to_all | solution.py:428
  67.9 9.5 %shard_map.98 = (bf16[4,8,24,256]{3,2,1,0:T(8,128)(2,1)}, f32[2,2560,128]{2,1,0:T(8,128)}) custom-call(bf16[4,8,24,128]{3,2,1,0:T(8,128)(2,1)} %bitcast.41, bf16[20,48,160]{2,1,0:T(8,128)(2,1)} %bitcast.38, bf16[20,16,160]{2,1,0:T(8,128)(2,1)} %pad.4.target, bf16[160,160]{1,0:T(8,128)(2,1)} %fusion.order), custom_call_target="tpu_custom_call" | custom-call | flops 40642560 | bytes 3317760 | tf_op jit(solution)/shard_map/pallas_call | solution.py:415
  77.5 3.3 %all-to-all-start.2 = ((bf16[32,24,256]{2,1,0:T(8,128)(2,1)}), bf16[32,24,256]{2,1,0:T(8,128)(2,1)S(1)}, u32[]{:S(2)}, u32[]{:S(2)}) async-start(bf16[32,24,256]{2,1,0:T(8,128)(2,1)} %bitcast.43), calls=%async_computation.2 | async-start | bytes 786432 | tf_op jit(solution)/shard_map/all_to_all | solution.py:428
  80.8 4.2 %shard_map.101 = bf16[4,8,40,256]{3,2,1,0:T(8,128)(2,1)} custom-call(f32[2,2560,128]{2,1,0:T(8,128)} %get-tuple-element.29.grads), custom_call_target="tpu_custom_call" | custom-call | flops 40642560 | bytes 3317760 | tf_op jit(solution)/shard_map/pallas_call | solution.py:415
  85.0 9.2 %all-to-all-done.2 = bf16[32,24,256]{2,1,0:T(8,128)(2,1)S(1)} async-done(((bf16[32,24,256]{2,1,0:T(8,128)(2,1)}), bf16[32,24,256]{2,1,0:T(8,128)(2,1)S(1)}, u32[]{:S(2)}, u32[]{:S(2)}) %all-to-all-start.2) | async-done | bytes 393248 | tf_op jit(solution)/shard_map/all_to_all | solution.py:428
  94.2 2.8 %all-to-all-start.3 = ((bf16[32,40,256]{2,1,0:T(8,128)(2,1)}), bf16[32,40,256]{2,1,0:T(8,128)(2,1)S(1)}, u32[]{:S(2)}, u32[]{:S(2)}) async-start(bf16[32,40,256]{2,1,0:T(8,128)(2,1)} %bitcast.35), calls=%async_computation.3 | async-start | bytes 1310720 | tf_op jit(solution)/shard_map/all_to_all | solution.py:428
  97.0 1.5 %collective-permute-start.2 = (bf16[3,48,1440]{2,1,0:T(8,128)(2,1)S(1)}, bf16[3,48,1440]{2,1,0:T(8,128)(2,1)S(1)}, u32[]{:S(2)}, u32[]{:S(2)}) collective-permute-start(bf16[3,48,1440]{2,1,0:T(8,128)(2,1)S(1)} %copy-done.4), channel_id=1, source_target_pairs={{0,1},{1,0},{2,3},{3,2},{4,5},{5,4},{6,7},{7,6},{8,9},{9,8},{10,11... | collective-permute-start | bytes 1244168 | tf_op jit(solution)/shard_map/ppermute | solution.py:37
  98.6 3.4 %collective-permute-start.3 = (bf16[3,48,1440]{2,1,0:T(8,128)(2,1)S(1)}, bf16[3,48,1440]{2,1,0:T(8,128)(2,1)S(1)}, u32[]{:S(2)}, u32[]{:S(2)}) collective-permute-start(bf16[3,48,1440]{2,1,0:T(8,128)(2,1)S(1)} %copy-done.5), channel_id=1, source_target_pairs={{0,7},{1,2},{2,1},{3,4},{4,3},{5,6},{6,5},{7,0},{8,15},{9,10},{10,... | collective-permute-start | bytes 1244168 | tf_op jit(solution)/shard_map/ppermute | solution.py:38
  102.0 1.9 %shard_map.99.taps = bf16[49,48,128]{2,1,0:T(8,128)(2,1)} custom-call(f32[7,7,24]{2,1,0:T(8,128)} %bitcast.46), custom_call_target="tpu_custom_call" | custom-call | flops 5080320 | bytes 3317760 | tf_op jit(solution)/shard_map/pallas_call | solution.py:415
  103.9 21.7 %collective-permute-done.2.near = bf16[3,48,1440]{2,1,0:T(8,128)(2,1)S(1)} collective-permute-done((bf16[3,48,1440]{2,1,0:T(8,128)(2,1)S(1)}, bf16[3,48,1440]{2,1,0:T(8,128)(2,1)S(1)}, u32[]{:S(2)}, u32[]{:S(2)}) %collective-permute-start.2) | collective-permute-done | bytes 414752 | tf_op jit(solution)/shard_map/ppermute | solution.py:37
  126.5 9.9 %shard_map.100 = bf16[2,6,24,1440]{3,2,1,0:T(8,128)(2,1)} custom-call(s32[2]{0:T(128)} %pad_add_fusion.flags, bf16[4,8,24,256]{3,2,1,0:T(8,128)(2,1)} %bitcast.39, bf16[3,48,1440]{2,1,0:T(8,128)(2,1)} %copy-done.6, bf16[3,48,1440]{2,1,0:T(8,128)(2,1)} %copy-done.7, bf16[3,48,1440]{2,1,0:T(8,128)(2,1)} %get-tuple-element.27.inner, ...), custom_call_target="tpu_custom_call" | custom-call | flops 40642560 | bytes 3317760 | tf_op jit(solution)/shard_map/pallas_call | solution.py:415
  137.3 3.4 %shard_map.102 = f32[2,24,20,2,160]{4,3,2,1,0:T(2,128)} custom-call(bf16[4,8,40,256]{3,2,1,0:T(8,128)(2,1)} %bitcast.32), custom_call_target="tpu_custom_call" | custom-call | flops 40642560 | bytes 3317760 | tf_op jit(solution)/shard_map/pallas_call | solution.py:415
  (34 shorter events, 7.0 us)
Async XLA Ops:
  0.6 16.7 %copy-start = (bf16[2,24,6,1440]{3,1,2,0:T(8,128)(2,1)S(1)}, bf16[2,24,6,1440]{3,1,2,0:T(8,128)(2,1)}, u32[]{:S(2)}) copy-start(bf16[2,24,6,1440]{3,1,2,0:T(8,128)(2,1)} %param.8) | copy-start | bytes 2488324
  10.0 44.4 %all-to-all-start.1 = ((bf16[8,2,9600]{2,1,0:T(2,128)(2,1)}), bf16[8,2,9600]{2,1,0:T(2,128)(2,1)S(1)}, u32[]{:S(2)}, u32[]{:S(2)}) async-start(bf16[8,2,9600]{2,1,0:T(2,128)(2,1)} %reshape.34), calls=%async_computation.1 | async-start | bytes 614400 | tf_op jit(solution)/shard_map/all_to_all | solution.py:443
  17.4 24.5 %collective-permute-start.1 = (bf16[2,3,24,1440]{3,2,1,0:T(8,128)(2,1)S(1)}, bf16[2,3,24,1440]{3,2,1,0:T(8,128)(2,1)S(1)}, u32[]{:S(2)}, u32[]{:S(2)}) collective-permute-start(bf16[2,3,24,1440]{3,2,1,0:T(8,128)(2,1)S(1)} %get-tuple-element.30), channel_id=1, source_target_pairs={{0,1},{1,0},{2,3},{3,2},{4,5},{5,4},{6,7},{7,6},{8,9},{9,8},{10,11... | collective-permute-start | bytes 1244168 | tf_op jit(solution)/shard_map/ppermute | solution.py:37
  19.5 28.6 %collective-permute-start = (bf16[2,3,24,1440]{3,2,1,0:T(8,128)(2,1)S(1)}, bf16[2,3,24,1440]{3,2,1,0:T(8,128)(2,1)S(1)}, u32[]{:S(2)}, u32[]{:S(2)}) collective-permute-start(bf16[2,3,24,1440]{3,2,1,0:T(8,128)(2,1)S(1)} %get-tuple-element.31), channel_id=1, source_target_pairs={{0,7},{1,2},{2,1},{3,4},{4,3},{5,6},{6,5},{7,0},{8,15},{9,10},{10,... | collective-permute-start | bytes 1244168 | tf_op jit(solution)/shard_map/ppermute | solution.py:38
  41.9 0.8 copy-start.9
  48.1 0.8 copy-start.8
  48.9 11.9 %copy-start.10 = (s32[160]{0:T(256)S(1)}, s32[160]{0:T(256)}, u32[]{:S(2)}) copy-start(s32[160]{0:T(256)} %param.13) | copy-start | bytes 1924
  54.5 12.8 %all-to-all-start = ((bf16[32,24,128]{2,1,0:T(8,128)(2,1)}), bf16[32,24,128]{2,1,0:T(8,128)(2,1)S(1)}, u32[]{:S(2)}, u32[]{:S(2)}) async-start(bf16[32,24,128]{2,1,0:T(8,128)(2,1)} %bitcast.44), calls=%async_computation | async-start | bytes 393216 | tf_op jit(solution)/shard_map/all_to_all | solution.py:428
  67.3 0.7 copy-start.3
  77.4 19.6 %copy-start.4 = (bf16[3,48,1440]{2,1,0:T(8,128)(2,1)S(1)}, bf16[3,48,1440]{2,1,0:T(8,128)(2,1)}, u32[]{:S(2)}) copy-start(bf16[3,48,1440]{2,1,0:T(8,128)(2,1)} %get-tuple-element.27.inner) | copy-start | bytes 1244164
  77.4 21.1 %copy-start.5 = (bf16[3,48,1440]{2,1,0:T(8,128)(2,1)S(1)}, bf16[3,48,1440]{2,1,0:T(8,128)(2,1)}, u32[]{:S(2)}) copy-start(bf16[3,48,1440]{2,1,0:T(8,128)(2,1)} %get-tuple-element.28.outer) | copy-start | bytes 1244164
  77.5 16.8 %all-to-all-start.2 = ((bf16[32,24,256]{2,1,0:T(8,128)(2,1)}), bf16[32,24,256]{2,1,0:T(8,128)(2,1)S(1)}, u32[]{:S(2)}, u32[]{:S(2)}) async-start(bf16[32,24,256]{2,1,0:T(8,128)(2,1)} %bitcast.43), calls=%async_computation.2 | async-start | bytes 786432 | tf_op jit(solution)/shard_map/all_to_all | solution.py:428
  94.2 31.4 %copy-start.2 = (bf16[32,24,256]{2,1,0:T(8,128)(2,1)}, bf16[32,24,256]{2,1,0:T(8,128)(2,1)S(1)}, u32[]{:S(2)}) copy-start(bf16[32,24,256]{2,1,0:T(8,128)(2,1)S(1)} %all-to-all-done.2) | copy-start | bytes 1179652
  94.2 42.2 %all-to-all-start.3 = ((bf16[32,40,256]{2,1,0:T(8,128)(2,1)}), bf16[32,40,256]{2,1,0:T(8,128)(2,1)S(1)}, u32[]{:S(2)}, u32[]{:S(2)}) async-start(bf16[32,40,256]{2,1,0:T(8,128)(2,1)} %bitcast.35), calls=%async_computation.3 | async-start | bytes 1310720 | tf_op jit(solution)/shard_map/all_to_all | solution.py:428
  97.0 28.6 %collective-permute-start.2 = (bf16[3,48,1440]{2,1,0:T(8,128)(2,1)S(1)}, bf16[3,48,1440]{2,1,0:T(8,128)(2,1)S(1)}, u32[]{:S(2)}, u32[]{:S(2)}) collective-permute-start(bf16[3,48,1440]{2,1,0:T(8,128)(2,1)S(1)} %copy-done.4), channel_id=1, source_target_pairs={{0,1},{1,0},{2,3},{3,2},{4,5},{5,4},{6,7},{7,6},{8,9},{9,8},{10,11... | collective-permute-start | bytes 1244168 | tf_op jit(solution)/shard_map/ppermute | solution.py:37
  98.6 27.0 %collective-permute-start.3 = (bf16[3,48,1440]{2,1,0:T(8,128)(2,1)S(1)}, bf16[3,48,1440]{2,1,0:T(8,128)(2,1)S(1)}, u32[]{:S(2)}, u32[]{:S(2)}) collective-permute-start(bf16[3,48,1440]{2,1,0:T(8,128)(2,1)S(1)} %copy-done.5), channel_id=1, source_target_pairs={{0,7},{1,2},{2,1},{3,4},{4,3},{5,6},{6,5},{7,0},{8,15},{9,10},{10,... | collective-permute-start | bytes 1244168 | tf_op jit(solution)/shard_map/ppermute | solution.py:38
  125.6 0.8 copy-start.6
  125.6 0.9 copy-start.7
  136.4 0.8 copy-start.1

commit v5 on v4

--- a/solution.py
+++ b/solution.py
@@ -346,25 +346,22 @@
 
 
 def unpack_kernel(members, got, out):
-    owners, groups, depth, lanes = got.shape
-    _, chans, per_owner, _, orders = out.shape
-    share, chan_share = depth // members, chans // owners
+    _, groups, depth, lanes = got.shape
+    _, chan_share, per_owner, _, orders = out.shape
+    share = depth // members
     row = lax.broadcasted_iota(jnp.int32, (groups * depth, orders), 0)
     column = lax.broadcasted_iota(jnp.int32, (groups * depth, orders), 1)
+    block = got[0].reshape(groups * depth, lanes)
     for b in range(members):
         wanted = (column // share) * depth + b * share + column % share
         picker = jnp.where(row == wanted, 1.0, 0.0).astype(BF16)
-        for e in range(owners):
-            block = lax.dot_general(
-                got[e].reshape(groups * depth, lanes),
-                picker,
-                (((0,), (0,)), ((), ())),
-                preferred_element_type=F32,
-            )
-            for c in range(chan_share):
-                for r in range(2):
-                    at = (r * chan_share + c) * per_owner
-                    out[b, e * chan_share + c, :, r, :] = block[at : at + per_owner]
+        lines = lax.dot_general(
+            block, picker, (((0,), (0,)), ((), ())), preferred_element_type=F32
+        )
+        for c in range(chan_share):
+            for r in range(2):
+                at = (r * chan_share + c) * per_owner
+                out[b, c, :, r, :] = lines[at : at + per_owner]
 
 
 def local(fields, depth_kernel, mix_weight, legendre, truth, degree_order):
@@ -479,8 +476,8 @@
         mixed,
     )
     got = swap(sent)
-    got, inner, outer = lax.optimization_barrier((got, inner, outer))
-    near, far = partners(inner, outer)
+    got, held = lax.optimization_barrier((got, outer))
+    near, far = partners(inner, held)
     back, grads = call(
         functools.partial(score_kernel, members, used, rows, halo),
         (
@@ -528,13 +525,18 @@
         mixer,
         table,
     )
-    score_grad = call(
+    score_grad = pl.pallas_call(
         functools.partial(unpack_kernel, members),
-        jax.ShapeDtypeStruct((members, chans, per_owner, 2, orders), F32),
-        [],
-        work,
-        owned,
-    )
+        out_shape=jax.ShapeDtypeStruct((members, chans, per_owner, 2, orders), F32),
+        grid=(ens_parts,),
+        in_specs=[pl.BlockSpec((1,) + owned.shape[1:], lambda e: (e, 0, 0, 0))],
+        out_specs=pl.BlockSpec(
+            (members, chan_share, per_owner, 2, orders), lambda e: (0, e, 0, 0, 0)
+        ),
+        compiler_params=vmem,
+        cost_estimate=pl.CostEstimate(flops=work, transcendentals=0, bytes_accessed=1),
+        name="unpack",
+    )(owned)
     return grad_fields.transpose(0, 2, 1, 3), score_grad.transpose(0, 1, 3, 4, 2)
 
 

time: 141 us -> 142 us (level)
    pallas_call x0 -> x1, Pallas kernels: none -> 4.22 us  [local(): pl.pallas_call(functools.partial(unpack_kernel, members), out_shape=jax.S...]
    pallas_call x8 -> x7, Pallas kernels: 46.4 us -> 43 us  [call(): pl.pallas_call(body, out_shape=outs, in_specs=specs, scratch_shapes=scrat...]
where the time goes in v5:
time: 142 us; the launch traced here: 141 us
  waiting for transfers between devices  53.6 us (38%)
  Pallas kernels  47.2 us (33%)
  starting transfers between devices  28.3 us (20%)
  local copies, waits for them, and re-layouts  10.4 us (7%)
    pallas_call x7, Pallas kernels, call(): pl.pallas_call(body, out_shape=outs, in_specs=specs, scratch_shapes=scrat...  43 us
    ppermute x2, waiting for transfers between devices, partners(): one = lax.ppermute(inner, 'lat', near)  40.2 us
    all_to_all x3, waiting for transfers between devices, swap(): lax.all_to_all(flat, ('ens', 'lat'), split_axis=0, concat_axis=0, tiled=T...  13.4 us
    all_to_all x3, starting transfers between devices, swap(): lax.all_to_all(flat, ('ens', 'lat'), split_axis=0, concat_axis=0, tiled=T...  10.7 us
    all_to_all x1, starting transfers between devices, local(): lax.all_to_all(legendre, 'lat', split_axis=1, concat_axis=0, tiled=True)  7.31 us
    ppermute x2, starting transfers between devices, partners(): other = lax.ppermute(outer, 'lat', far)  6.69 us
    unnamed x25, local copies, waits for them, and re-layouts  6.29 us
    pallas_call x1, Pallas kernels, local(): pl.pallas_call(functools.partial(unpack_kernel, members), out_shape=jax.S...  4.22 us
  transfers between devices with their start and end apart: 8, of which 4 were waited for; matrix products, arithmetic and copies ran while one was open for 3% of the time, Pallas kernels for 19%

profile of v5, /device:TPU:0, one launch (start us, length us, event | category | flops | bytes accessed | tf_op | source)
XLA Modules:
  0.0 141.5 jit_solution(10624907100791053810)
XLA Ops:
  0.6 6.6 %shard_map.95 = (f32[6,48,1440]{2,1,0:T(8,128)}, bf16[49,48,128]{2,1,0:T(8,128)(2,1)}, bf16[2,96,48]{2,1,0:T(8,128)(2,1)}) custom-call(bf16[2,6,24,1440]{3,2,1,0:T(8,128)(2,1)} %bitcast.31, f32[7,7,24]{2,1,0:T(8,128)} %bitcast.45, bf16[24,24]{1,0:T(8,128)(2,1)} %weight.1, bf16[2,2,96,24]{3,2,1,0:T(8,128)(2,1)} %constant.44.clone.pick), custom_call_target="tpu_custom_call" | custom-call | flops 40642560 | bytes 3317760 | tf_op jit(solution)/shard_map/pallas_call | solution.py:412
  7.2 1.3 copy.28
  8.5 1.5 %reshape.34 = bf16[8,2,9600]{2,1,0:T(2,128)(2,1)} reshape(bf16[160,6,160]{2,1,0:T(8,128)(2,1)S(1)} %bitcast.34) | data formatting | bytes 614400
  10.0 7.3 %all-to-all-start.1 = ((bf16[8,2,9600]{2,1,0:T(2,128)(2,1)}), bf16[8,2,9600]{2,1,0:T(2,128)(2,1)S(1)}, u32[]{:S(2)}, u32[]{:S(2)}) async-start(bf16[8,2,9600]{2,1,0:T(2,128)(2,1)} %reshape.34), calls=%async_computation.1 | async-start | bytes 614400 | tf_op jit(solution)/shard_map/all_to_all | solution.py:440
  17.4 2.1 %collective-permute-start.1 = (bf16[2,3,24,1440]{3,2,1,0:T(8,128)(2,1)S(1)}, bf16[2,3,24,1440]{3,2,1,0:T(8,128)(2,1)S(1)}, u32[]{:S(2)}, u32[]{:S(2)}) collective-permute-start(bf16[2,3,24,1440]{3,2,1,0:T(8,128)(2,1)S(1)} %get-tuple-element.28), channel_id=1, source_target_pairs={{0,1},{1,0},{2,3},{3,2},{4,5},{5,4},{6,7},{7,6},{8,9},{9,8},{10,11... | collective-permute-start | bytes 1244168 | tf_op jit(solution)/shard_map/ppermute | solution.py:37
  19.5 3.3 %collective-permute-start = (bf16[2,3,24,1440]{3,2,1,0:T(8,128)(2,1)S(1)}, bf16[2,3,24,1440]{3,2,1,0:T(8,128)(2,1)S(1)}, u32[]{:S(2)}, u32[]{:S(2)}) collective-permute-start(bf16[2,3,24,1440]{3,2,1,0:T(8,128)(2,1)S(1)} %get-tuple-element.29), channel_id=1, source_target_pairs={{0,7},{1,2},{2,1},{3,4},{4,3},{5,6},{6,5},{7,0},{8,15},{9,10},{10,... | collective-permute-start | bytes 1244168 | tf_op jit(solution)/shard_map/ppermute | solution.py:38
  23.4 18.5 %collective-permute-done.1.edge = bf16[2,3,24,1440]{3,2,1,0:T(8,128)(2,1)S(1)} collective-permute-done((bf16[2,3,24,1440]{3,2,1,0:T(8,128)(2,1)S(1)}, bf16[2,3,24,1440]{3,2,1,0:T(8,128)(2,1)S(1)}, u32[]{:S(2)}, u32[]{:S(2)}) %collective-permute-start.1) | collective-permute-done | bytes 414752 | tf_op jit(solution)/shard_map/ppermute | solution.py:37
  42.7 5.4 %shard_map.96 = (f32[3,96,256]{2,1,0:T(8,128)}, bf16[3,48,1440]{2,1,0:T(8,128)(2,1)}) custom-call(s32[2]{0:T(128)} %pad_add_fusion.flags, bf16[2,3,24,1440]{3,2,1,0:T(8,128)(2,1)} %copy-done.9, f32[6,48,1440]{2,1,0:T(8,128)} %get-tuple-element.16.partial, bf16[49,48,128]{2,1,0:T(8,128)(2,1)} %get-tuple-element.17.taps, ...), custom_call_target="tpu_custom_call" | custom-call | flops 20321280 | bytes 3317760 | tf_op jit(solution)/shard_map/pallas_call | solution.py:412
  48.9 5.6 %shard_map.97 = (bf16[4,8,24,128]{3,2,1,0:T(8,128)(2,1)}, bf16[3,48,1440]{2,1,0:T(8,128)(2,1)}) custom-call(s32[2]{0:T(128)} %pad_add_fusion.flags, bf16[2,3,24,1440]{3,2,1,0:T(8,128)(2,1)} %copy-done.8, f32[6,48,1440]{2,1,0:T(8,128)} %get-tuple-element.16.partial, bf16[49,48,128]{2,1,0:T(8,128)(2,1)} %get-tuple-element.17.taps, ...), custom_call_target="tpu_custom_call" | custom-call | flops 20321280 | bytes 3317760 | tf_op jit(solution)/shard_map/pallas_call | solution.py:412
  54.5 4.6 %all-to-all-start = ((bf16[32,24,128]{2,1,0:T(8,128)(2,1)}), bf16[32,24,128]{2,1,0:T(8,128)(2,1)S(1)}, u32[]{:S(2)}, u32[]{:S(2)}) async-start(bf16[32,24,128]{2,1,0:T(8,128)(2,1)} %bitcast.44), calls=%async_computation | async-start | bytes 393216 | tf_op jit(solution)/shard_map/all_to_all | solution.py:425
  59.0 1.0 constant_dynamic-slice_fusion
  62.3 0.9 copy.27
  63.2 4.1 %all-to-all-done = bf16[32,24,128]{2,1,0:T(8,128)(2,1)S(1)} async-done(((bf16[32,24,128]{2,1,0:T(8,128)(2,1)}), bf16[32,24,128]{2,1,0:T(8,128)(2,1)S(1)}, u32[]{:S(2)}, u32[]{:S(2)}) %all-to-all-start) | async-done | bytes 196640 | tf_op jit(solution)/shard_map/all_to_all | solution.py:425
  67.9 9.5 %shard_map.98 = (bf16[4,8,24,256]{3,2,1,0:T(8,128)(2,1)}, f32[2,2560,128]{2,1,0:T(8,128)}) custom-call(bf16[4,8,24,128]{3,2,1,0:T(8,128)(2,1)} %bitcast.41, bf16[20,48,160]{2,1,0:T(8,128)(2,1)} %bitcast.38, bf16[20,16,160]{2,1,0:T(8,128)(2,1)} %pad.4.target, bf16[160,160]{1,0:T(8,128)(2,1)} %fusion.order), custom_call_target="tpu_custom_call" | custom-call | flops 40642560 | bytes 3317760 | tf_op jit(solution)/shard_map/pallas_call | solution.py:412
  77.5 3.3 %all-to-all-start.2 = ((bf16[32,24,256]{2,1,0:T(8,128)(2,1)}), bf16[32,24,256]{2,1,0:T(8,128)(2,1)S(1)}, u32[]{:S(2)}, u32[]{:S(2)}) async-start(bf16[32,24,256]{2,1,0:T(8,128)(2,1)} %bitcast.43), calls=%async_computation.2 | async-start | bytes 786432 | tf_op jit(solution)/shard_map/all_to_all | solution.py:425
  80.8 4.2 %shard_map.101 = bf16[4,8,40,256]{3,2,1,0:T(8,128)(2,1)} custom-call(f32[2,2560,128]{2,1,0:T(8,128)} %get-tuple-element.27.grads), custom_call_target="tpu_custom_call" | custom-call | flops 40642560 | bytes 3317760 | tf_op jit(solution)/shard_map/pallas_call | solution.py:412
  85.0 9.2 %all-to-all-done.2 = bf16[32,24,256]{2,1,0:T(8,128)(2,1)S(1)} async-done(((bf16[32,24,256]{2,1,0:T(8,128)(2,1)}), bf16[32,24,256]{2,1,0:T(8,128)(2,1)S(1)}, u32[]{:S(2)}, u32[]{:S(2)}) %all-to-all-start.2) | async-done | bytes 393248 | tf_op jit(solution)/shard_map/all_to_all | solution.py:425
  94.2 2.8 %all-to-all-start.3 = ((bf16[32,40,256]{2,1,0:T(8,128)(2,1)}), bf16[32,40,256]{2,1,0:T(8,128)(2,1)S(1)}, u32[]{:S(2)}, u32[]{:S(2)}) async-start(bf16[32,40,256]{2,1,0:T(8,128)(2,1)} %bitcast.35), calls=%async_computation.3 | async-start | bytes 1310720 | tf_op jit(solution)/shard_map/all_to_all | solution.py:425
  97.0 1.5 %collective-permute-start.2 = (bf16[3,48,1440]{2,1,0:T(8,128)(2,1)S(1)}, bf16[3,48,1440]{2,1,0:T(8,128)(2,1)S(1)}, u32[]{:S(2)}, u32[]{:S(2)}) collective-permute-start(bf16[3,48,1440]{2,1,0:T(8,128)(2,1)S(1)} %copy-done.4), channel_id=1, source_target_pairs={{0,1},{1,0},{2,3},{3,2},{4,5},{5,4},{6,7},{7,6},{8,9},{9,8},{10,11... | collective-permute-start | bytes 1244168 | tf_op jit(solution)/shard_map/ppermute | solution.py:37
  98.6 3.4 %collective-permute-start.3 = (bf16[3,48,1440]{2,1,0:T(8,128)(2,1)S(1)}, bf16[3,48,1440]{2,1,0:T(8,128)(2,1)S(1)}, u32[]{:S(2)}, u32[]{:S(2)}) collective-permute-start(bf16[3,48,1440]{2,1,0:T(8,128)(2,1)S(1)} %copy-done.5), channel_id=1, source_target_pairs={{0,7},{1,2},{2,1},{3,4},{4,3},{5,6},{6,5},{7,0},{8,15},{9,10},{10,... | collective-permute-start | bytes 1244168 | tf_op jit(solution)/shard_map/ppermute | solution.py:38
  102.0 1.9 %shard_map.99.taps = bf16[49,48,128]{2,1,0:T(8,128)(2,1)} custom-call(f32[7,7,24]{2,1,0:T(8,128)} %bitcast.46), custom_call_target="tpu_custom_call" | custom-call | flops 5080320 | bytes 3317760 | tf_op jit(solution)/shard_map/pallas_call | solution.py:412
  103.9 21.7 %collective-permute-done.2.near = bf16[3,48,1440]{2,1,0:T(8,128)(2,1)S(1)} collective-permute-done((bf16[3,48,1440]{2,1,0:T(8,128)(2,1)S(1)}, bf16[3,48,1440]{2,1,0:T(8,128)(2,1)S(1)}, u32[]{:S(2)}, u32[]{:S(2)}) %collective-permute-start.2) | collective-permute-done | bytes 414752 | tf_op jit(solution)/shard_map/ppermute | solution.py:37
  126.5 9.9 %shard_map.100 = bf16[2,6,24,1440]{3,2,1,0:T(8,128)(2,1)} custom-call(s32[2]{0:T(128)} %pad_add_fusion.flags, bf16[4,8,24,256]{3,2,1,0:T(8,128)(2,1)} %bitcast.39, bf16[3,48,1440]{2,1,0:T(8,128)(2,1)} %copy-done.6, bf16[3,48,1440]{2,1,0:T(8,128)(2,1)} %copy-done.7, bf16[3,48,1440]{2,1,0:T(8,128)(2,1)} %get-tuple-element.25.inner, ...), custom_call_target="tpu_custom_call" | custom-call | flops 40642560 | bytes 3317760 | tf_op jit(solution)/shard_map/pallas_call | solution.py:412
  137.3 4.2 %unpack.1 = f32[2,24,20,2,160]{4,3,2,1,0:T(2,128)} custom-call(bf16[4,8,40,256]{3,2,1,0:T(8,128)(2,1)} %bitcast.32), custom_call_target="tpu_custom_call" | custom-call | flops 40642560 | bytes 1 | tf_op jit(solution)/shard_map/unpack/pallas_call | solution.py:528
  (34 shorter events, 7.0 us)
Async XLA Ops:
  0.6 16.7 %copy-start = (bf16[2,24,6,1440]{3,1,2,0:T(8,128)(2,1)S(1)}, bf16[2,24,6,1440]{3,1,2,0:T(8,128)(2,1)}, u32[]{:S(2)}) copy-start(bf16[2,24,6,1440]{3,1,2,0:T(8,128)(2,1)} %param.8) | copy-start | bytes 2488324
  10.0 44.4 %all-to-all-start.1 = ((bf16[8,2,9600]{2,1,0:T(2,128)(2,1)}), bf16[8,2,9600]{2,1,0:T(2,128)(2,1)S(1)}, u32[]{:S(2)}, u32[]{:S(2)}) async-start(bf16[8,2,9600]{2,1,0:T(2,128)(2,1)} %reshape.34), calls=%async_computation.1 | async-start | bytes 614400 | tf_op jit(solution)/shard_map/all_to_all | solution.py:440
  17.4 24.5 %collective-permute-start.1 = (bf16[2,3,24,1440]{3,2,1,0:T(8,128)(2,1)S(1)}, bf16[2,3,24,1440]{3,2,1,0:T(8,128)(2,1)S(1)}, u32[]{:S(2)}, u32[]{:S(2)}) collective-permute-start(bf16[2,3,24,1440]{3,2,1,0:T(8,128)(2,1)S(1)} %get-tuple-element.28), channel_id=1, source_target_pairs={{0,1},{1,0},{2,3},{3,2},{4,5},{5,4},{6,7},{7,6},{8,9},{9,8},{10,11... | collective-permute-start | bytes 1244168 | tf_op jit(solution)/shard_map/ppermute | solution.py:37
  19.5 28.6 %collective-permute-start = (bf16[2,3,24,1440]{3,2,1,0:T(8,128)(2,1)S(1)}, bf16[2,3,24,1440]{3,2,1,0:T(8,128)(2,1)S(1)}, u32[]{:S(2)}, u32[]{:S(2)}) collective-permute-start(bf16[2,3,24,1440]{3,2,1,0:T(8,128)(2,1)S(1)} %get-tuple-element.29), channel_id=1, source_target_pairs={{0,7},{1,2},{2,1},{3,4},{4,3},{5,6},{6,5},{7,0},{8,15},{9,10},{10,... | collective-permute-start | bytes 1244168 | tf_op jit(solution)/shard_map/ppermute | solution.py:38
  41.9 0.8 copy-start.9
  48.1 0.8 copy-start.8
  48.9 11.9 %copy-start.10 = (s32[160]{0:T(256)S(1)}, s32[160]{0:T(256)}, u32[]{:S(2)}) copy-start(s32[160]{0:T(256)} %param.13) | copy-start | bytes 1924
  54.5 12.8 %all-to-all-start = ((bf16[32,24,128]{2,1,0:T(8,128)(2,1)}), bf16[32,24,128]{2,1,0:T(8,128)(2,1)S(1)}, u32[]{:S(2)}, u32[]{:S(2)}) async-start(bf16[32,24,128]{2,1,0:T(8,128)(2,1)} %bitcast.44), calls=%async_computation | async-start | bytes 393216 | tf_op jit(solution)/shard_map/all_to_all | solution.py:425
  67.3 0.7 copy-start.3
  77.4 19.6 %copy-start.4 = (bf16[3,48,1440]{2,1,0:T(8,128)(2,1)S(1)}, bf16[3,48,1440]{2,1,0:T(8,128)(2,1)}, u32[]{:S(2)}) copy-start(bf16[3,48,1440]{2,1,0:T(8,128)(2,1)} %get-tuple-element.25.inner) | copy-start | bytes 1244164
  77.4 21.1 %copy-start.5 = (bf16[3,48,1440]{2,1,0:T(8,128)(2,1)S(1)}, bf16[3,48,1440]{2,1,0:T(8,128)(2,1)}, u32[]{:S(2)}) copy-start(bf16[3,48,1440]{2,1,0:T(8,128)(2,1)} %get-tuple-element.26.outer) | copy-start | bytes 1244164
  77.5 16.8 %all-to-all-start.2 = ((bf16[32,24,256]{2,1,0:T(8,128)(2,1)}), bf16[32,24,256]{2,1,0:T(8,128)(2,1)S(1)}, u32[]{:S(2)}, u32[]{:S(2)}) async-start(bf16[32,24,256]{2,1,0:T(8,128)(2,1)} %bitcast.43), calls=%async_computation.2 | async-start | bytes 786432 | tf_op jit(solution)/shard_map/all_to_all | solution.py:425
  94.2 31.4 %copy-start.2 = (bf16[32,24,256]{2,1,0:T(8,128)(2,1)}, bf16[32,24,256]{2,1,0:T(8,128)(2,1)S(1)}, u32[]{:S(2)}) copy-start(bf16[32,24,256]{2,1,0:T(8,128)(2,1)S(1)} %all-to-all-done.2) | copy-start | bytes 1179652
  94.2 42.2 %all-to-all-start.3 = ((bf16[32,40,256]{2,1,0:T(8,128)(2,1)}), bf16[32,40,256]{2,1,0:T(8,128)(2,1)S(1)}, u32[]{:S(2)}, u32[]{:S(2)}) async-start(bf16[32,40,256]{2,1,0:T(8,128)(2,1)} %bitcast.35), calls=%async_computation.3 | async-start | bytes 1310720 | tf_op jit(solution)/shard_map/all_to_all | solution.py:425
  97.0 28.6 %collective-permute-start.2 = (bf16[3,48,1440]{2,1,0:T(8,128)(2,1)S(1)}, bf16[3,48,1440]{2,1,0:T(8,128)(2,1)S(1)}, u32[]{:S(2)}, u32[]{:S(2)}) collective-permute-start(bf16[3,48,1440]{2,1,0:T(8,128)(2,1)S(1)} %copy-done.4), channel_id=1, source_target_pairs={{0,1},{1,0},{2,3},{3,2},{4,5},{5,4},{6,7},{7,6},{8,9},{9,8},{10,11... | collective-permute-start | bytes 1244168 | tf_op jit(solution)/shard_map/ppermute | solution.py:37
  98.6 27.0 %collective-permute-start.3 = (bf16[3,48,1440]{2,1,0:T(8,128)(2,1)S(1)}, bf16[3,48,1440]{2,1,0:T(8,128)(2,1)S(1)}, u32[]{:S(2)}, u32[]{:S(2)}) collective-permute-start(bf16[3,48,1440]{2,1,0:T(8,128)(2,1)S(1)} %copy-done.5), channel_id=1, source_target_pairs={{0,7},{1,2},{2,1},{3,4},{4,3},{5,6},{6,5},{7,0},{8,15},{9,10},{10,... | collective-permute-start | bytes 1244168 | tf_op jit(solution)/shard_map/ppermute | solution.py:38
  125.6 0.8 copy-start.6
  125.6 0.9 copy-start.7
  136.4 0.8 copy-start.1

commit v6 on v5

--- a/solution.py
+++ b/solution.py
@@ -30,13 +30,13 @@
     return table.reshape(nlon, 2 * span).astype(jnp.bfloat16)
 
 
-def partners(inner, outer):
+def partner(edge, pair):
     count = lax.axis_size("lat")
-    near = [(i, i ^ 1) for i in range(count)]
-    far = [(i, (i + (1 if i % 2 else -1)) % count) for i in range(count)]
-    one = lax.ppermute(inner, "lat", near)
-    other = lax.ppermute(outer, "lat", far)
-    return one, other
+    if pair:
+        steps = [(i, i ^ 1) for i in range(count)]
+    else:
+        steps = [(i, (i + (1 if i % 2 else -1)) % count) for i in range(count)]
+    return lax.ppermute(edge, "lat", steps)
 
 
 def place():
@@ -190,7 +190,7 @@
     return gaps * lax.rsqrt(gaps * gaps + smooth_width * smooth_width)
 
 
-def score_kernel(members, used, rows, halo, got, legendre, target, order, back, grads, spread, gather):
+def score_kernel(members, used, rows, halo, got, legendre, target, order, back, grads, spread, gather, picked):
     owners, groups, height, lanes = got.shape
     orders, nlat, degrees = legendre.shape
     slots = target.shape[1]
@@ -208,47 +208,68 @@
         first, second = (at, at + part) if t % 2 else (at + part, at)
         spread[first : first + part, :] = block[:part]
         spread[second : second + part, :] = block[part : 2 * part]
+    reorder = jnp.where(
+        lax.broadcasted_iota(jnp.int32, (degrees, degrees), 0) == order[...], 1.0, 0.0
+    )
+    picked[...] = reorder.astype(BF16)
     edge = halo * orders
     gather[:edge, :] = jnp.zeros((edge, ens * slots), F32)
     gather[edge + nlat * orders :, :] = jnp.zeros((edge, ens * slots), F32)
 
-    def one(m):
-        block = spread[pl.ds(m, nlat, stride=orders), :].astype(BF16)
-        leg = legendre[m]
-        coeff = lax.dot_general(
-            block, leg, (((0,), (0,)), ((), ())), preferred_element_type=F32
-        )
-        own = [coeff[k * slots : (k + 1) * slots] for k in range(ens)]
-        truth = target[m].astype(F32)
+    def score(values, truth):
+        own = [values[k * slots : (k + 1) * slots] for k in range(ens)]
         sums = [None] * ens
         for k in range(ens):
             for n in range(k + 1, ens):
                 sign = soft_sign(own[k] - own[n])
                 sums[k] = sign if sums[k] is None else sums[k] + sign
                 sums[n] = -sign if sums[n] is None else sums[n] - sign
-        grad = jnp.concatenate(
+        return jnp.concatenate(
             [
                 soft_sign(own[k] - truth) * (1.0 / ens) - sums[k] * (1.0 / (ens * (ens - 1)))
                 for k in range(ens)
             ],
             axis=0,
-        ).astype(BF16)
-        spec = lax.dot_general(
-            leg, grad, (((1,), (1,)), ((), ())), preferred_element_type=F32
         )
-        gather[pl.ds(edge + m, nlat, stride=orders), :] = spec
-        at = pl.multiple_of(m * ens * slots, 8)
-        ordered = jnp.dot(grad, order[...], preferred_element_type=F32)
-        for j in range(grads.shape[0]):
-            last = min(degrees, (j + 1) * 128)
-            grads[j, pl.ds(at, ens * slots), : last - j * 128] = ordered[:, j * 128 : last]
-
-    step = 4 if orders % 4 == 0 else 1
+
+    tail = degrees % 128
+    packs = tail > 0 and 128 % tail == 0 and orders % (128 // tail) == 0
+    step = 128 // tail if packs else 1
+    body = degrees - tail if packs else degrees
 
     @pl.loop(0, orders // step)
     def _(trip):
-        for j in range(step):
-            one(trip * step + j)
+        numbers = [trip * step + j for j in range(step)]
+        coeffs = [
+            lax.dot_general(
+                spread[pl.ds(m, nlat, stride=orders), :].astype(BF16),
+                legendre[m],
+                (((0,), (0,)), ((), ())),
+                preferred_element_type=F32,
+            )
+            for m in numbers
+        ]
+        truths = [target[m].astype(F32) for m in numbers]
+        scored = [score(x[:, :body], y[:, :body]) for x, y in zip(coeffs, truths)]
+        if packs:
+            rest = score(
+                jnp.concatenate([x[:, body:] for x in coeffs], axis=1),
+                jnp.concatenate([y[:, body:] for y in truths], axis=1),
+            )
+            scored = [
+                jnp.concatenate([x, rest[:, j * tail : (j + 1) * tail]], axis=1)
+                for j, x in enumerate(scored)
+            ]
+        for m, grad in zip(numbers, scored):
+            grad = grad.astype(BF16)
+            gather[pl.ds(edge + m, nlat, stride=orders), :] = lax.dot_general(
+                legendre[m], grad, (((1,), (1,)), ((), ())), preferred_element_type=F32
+            )
+            at = pl.multiple_of(m * ens * slots, 8)
+            ordered = jnp.dot(grad, picked[...], preferred_element_type=F32)
+            for j in range(grads.shape[0]):
+                last = min(degrees, (j + 1) * 128)
+                grads[j, pl.ds(at, ens * slots), : last - j * 128] = ordered[:, j * 128 : last]
 
     wide = back.shape[3]
     tall = (rows + 2 * halo) * orders
@@ -345,23 +366,36 @@
                 out[e, t, b * share : (b + 1) * share, :] = jnp.concatenate(pieces, axis=1).astype(BF16)
 
 
-def unpack_kernel(members, got, out):
+def unpack_kernel(members, got, out, swapped, pickers):
     _, groups, depth, lanes = got.shape
     _, chan_share, per_owner, _, orders = out.shape
     share = depth // members
-    row = lax.broadcasted_iota(jnp.int32, (groups * depth, orders), 0)
-    column = lax.broadcasted_iota(jnp.int32, (groups * depth, orders), 1)
-    block = got[0].reshape(groups * depth, lanes)
+    pair = 2 * per_owner
+
+    def iotas(shape):
+        return (lax.broadcasted_iota(jnp.int32, shape, d) for d in range(2))
+
+    @pl.when(pl.program_id(0) == 0)
+    def _():
+        row, column = iotas(swapped.shape)
+        wanted = ((row % 2) * chan_share + row // pair) * per_owner + (row % pair) // 2
+        swapped[...] = jnp.where(column == wanted, 1.0, 0.0).astype(BF16)
+        row, column = iotas(pickers.shape[1:])
+        start = (column // share) * depth + column % share
+        for b in range(members):
+            pickers[b] = jnp.where(row == start + b * share, 1.0, 0.0).astype(BF16)
+
+    turned = lax.dot_general(
+        swapped[...],
+        got[0].reshape(groups * depth, lanes),
+        (((1,), (1,)), ((), ())),
+        preferred_element_type=F32,
+    ).astype(BF16)
     for b in range(members):
-        wanted = (column // share) * depth + b * share + column % share
-        picker = jnp.where(row == wanted, 1.0, 0.0).astype(BF16)
-        lines = lax.dot_general(
-            block, picker, (((0,), (0,)), ((), ())), preferred_element_type=F32
-        )
+        lines = jnp.dot(turned, pickers[b], preferred_element_type=F32)
         for c in range(chan_share):
-            for r in range(2):
-                at = (r * chan_share + c) * per_owner
-                out[b, c, :, r, :] = lines[at : at + per_owner]
+            block = lines[c * pair : (c + 1) * pair]
+            out[b, c] = block.reshape(per_owner, 2, orders)
 
 
 def local(fields, depth_kernel, mix_weight, legendre, truth, degree_order):
@@ -386,10 +420,8 @@
     flags = place()
     own = fields.transpose(0, 2, 1, 3)
     odd = lat_at % 2
-    near, far = partners(
-        lax.dynamic_slice_in_dim(own, (1 - odd) * (rows - halo), halo, 1),
-        lax.dynamic_slice_in_dim(own, odd * (rows - halo), halo, 1),
-    )
+    inner = lax.dynamic_slice_in_dim(own, (1 - odd) * (rows - halo), halo, 1)
+    near = partner(inner, True)
 
     pick = np.zeros((2, members, ens_parts, height, chans), np.float32)
     for r in range(2):
@@ -436,15 +468,18 @@
         mix_weight,
         pick,
     )
-    legendre, partial = lax.optimization_barrier((legendre, partial))
-    order_legendre = lax.all_to_all(legendre, "lat", split_axis=1, concat_axis=0, tiled=True)
-    order_legendre = order_legendre.transpose(1, 0, 2)
     target = lax.dynamic_slice(
         truth, (ens_at * chan_share, 0, lat_at * share, 0), (chan_share, 2, share, degrees)
     )
     target = target.transpose(2, 1, 0, 3).reshape(share, used, degrees)
     target = jnp.pad(target, ((0, 0), (0, slots - used), (0, 0)))
-    reorder = (jnp.arange(degrees)[:, None] == degree_order[None, :]).astype(BF16)
+
+    slab = legendre.reshape(rows, groups, share * degrees).transpose(1, 0, 2)
+    line = math.gcd(rows * share * degrees, 128)
+    slab = slab.reshape(groups, rows * share * degrees // line, line)
+    late, partial = lax.optimization_barrier((own, partial))
+    outer = lax.dynamic_slice_in_dim(late, odd * (rows - halo), halo, 1)
+    far = partner(outer, False)
 
     def chunk(lines):
         return jax.ShapeDtypeStruct((ens_parts, groups, height, up(lines * share, 128)), BF16)
@@ -462,6 +497,9 @@
         table,
         mixer,
     )
+    slab, mixed = lax.optimization_barrier((slab, mixed))
+    slab = lax.all_to_all(slab, "lat", split_axis=0, concat_axis=0, tiled=True)
+    order_legendre = slab.reshape(nlat, share, degrees).transpose(1, 0, 2)
     sent, outer = call(
         functools.partial(far_kernel, share),
         (chunk(rows), edge),
@@ -476,8 +514,7 @@
         mixed,
     )
     got = swap(sent)
-    got, held = lax.optimization_barrier((got, outer))
-    near, far = partners(inner, held)
+    near, far = partner(inner, True), partner(outer, False)
     back, grads = call(
         functools.partial(score_kernel, members, used, rows, halo),
         (
@@ -487,12 +524,13 @@
         [
             pltpu.VMEM((nlat * share, ens * slots), F32),
             pltpu.VMEM(((nlat + 2 * halo) * share, ens * slots), F32),
+            pltpu.VMEM((degrees, degrees), BF16),
         ],
         work,
         got,
         order_legendre,
         target,
-        reorder,
+        degree_order.reshape(1, degrees),
     )
     returned = swap(back)
     packed = call(
@@ -533,6 +571,10 @@
         out_specs=pl.BlockSpec(
             (members, chan_share, per_owner, 2, orders), lambda e: (0, e, 0, 0, 0)
         ),
+        scratch_shapes=[
+            pltpu.VMEM((used * per_owner, owned.shape[3]), BF16),
+            pltpu.VMEM((members, groups * owned.shape[2], orders), BF16),
+        ],
         compiler_params=vmem,
         cost_estimate=pl.CostEstimate(flops=work, transcendentals=0, bytes_accessed=1),
         name="unpack",

time: 142 us -> 138 us (0.972)
  Pallas kernels: 47.2 us -> 44.5 us
    reshape x0 -> x3, local copies, waits for them, and re-layouts: none -> 3.2 us  [the longest x1 1.65 us: local(): slab = legendre.reshape(rows, groups, share * degrees).transpose(1, 0, 2)]
    pallas_call x7, Pallas kernels: 43 us -> 39.9 us  [call(): pl.pallas_call(body, out_shape=outs, in_specs=specs, scratch_shapes=scrat...]
    unnamed x25 -> x21, local copies, waits for them, and re-layouts: 6.29 us -> 3.86 us
    ppermute x4, starting transfers between devices: 10.3 us -> 12.3 us  [partner(): return lax.ppermute(edge, 'lat', steps)]
    all_to_all x3, starting transfers between devices: 10.7 us -> 8.84 us  [swap(): lax.all_to_all(flat, ('ens', 'lat'), split_axis=0, concat_axis=0, tiled=T...]
  transfers between devices with their start and end apart: 8 -> 8, of which waited for: 4 -> 6; matrix products, arithmetic and copies ran while one was open for 3% -> 4% of each run, Pallas kernels for 19% -> 20%
where the time goes in v6:
time: 138 us; the launch traced here: 137 us
  waiting for transfers between devices  53 us (38%)
  Pallas kernels  44.5 us (32%)
  starting transfers between devices  27.2 us (20%)
  local copies, waits for them, and re-layouts  10.6 us (8%)
    pallas_call x7, Pallas kernels, call(): pl.pallas_call(body, out_shape=outs, in_specs=specs, scratch_shapes=scrat...  39.9 us
    ppermute x4, waiting for transfers between devices, partner(): return lax.ppermute(edge, 'lat', steps)  38.8 us
    all_to_all x3, waiting for transfers between devices, swap(): lax.all_to_all(flat, ('ens', 'lat'), split_axis=0, concat_axis=0, tiled=T...  14.2 us
    ppermute x4, starting transfers between devices, partner(): return lax.ppermute(edge, 'lat', steps)  12.3 us
    all_to_all x3, starting transfers between devices, swap(): lax.all_to_all(flat, ('ens', 'lat'), split_axis=0, concat_axis=0, tiled=T...  8.84 us
    all_to_all x1, starting transfers between devices, local(): slab = lax.all_to_all(slab, 'lat', split_axis=0, concat_axis=0, tiled=True)  6.05 us
    pallas_call x1, Pallas kernels, local(): pl.pallas_call(functools.partial(unpack_kernel, members), out_shape=jax.S...  4.59 us
    unnamed x21, local copies, waits for them, and re-layouts  3.86 us
  transfers between devices with their start and end apart: 8, of which 6 were waited for; matrix products, arithmetic and copies ran while one was open for 4% of the time, Pallas kernels for 20%

profile of v6, /device:TPU:0, one launch (start us, length us, event | category | flops | bytes accessed | tf_op | source)
XLA Modules:
  0.0 136.7 jit_solution(3023446172141964604)
XLA Ops:
  0.6 1.1 dynamic-slice_bitcast_fusion
  1.7 3.1 %collective-permute-start.1 = (bf16[2,3,24,1440]{3,2,1,0:T(8,128)(2,1)S(1)}, bf16[2,3,24,1440]{3,2,1,0:T(8,128)(2,1)S(1)}, u32[]{:S(2)}, u32[]{:S(2)}) collective-permute-start(bf16[2,3,24,1440]{3,2,1,0:T(8,128)(2,1)S(1)} %dynamic-slice_bitcast_fusion), channel_id=1, source_target_pairs={{0,1},{1,0},{2,3},{3,2},{4,5},{5,4},{6,7},{7,6},{8,9},{9,8},{10,11... | collective-permute-start | bytes 1244168 | tf_op jit(solution)/shard_map/ppermute | solution.py:39
  4.8 6.5 %shard_map.95 = (f32[6,48,1440]{2,1,0:T(8,128)}, bf16[49,48,128]{2,1,0:T(8,128)(2,1)}, bf16[2,96,48]{2,1,0:T(8,128)(2,1)}) custom-call(bf16[2,6,24,1440]{3,2,1,0:T(8,128)(2,1)} %bitcast.24, f32[7,7,24]{2,1,0:T(8,128)} %bitcast.37, bf16[24,24]{1,0:T(8,128)(2,1)} %weight.1, bf16[2,2,96,24]{3,2,1,0:T(8,128)(2,1)} %constant.44.clone.pick), custom_call_target="tpu_custom_call" | custom-call | flops 40642560 | bytes 3317760 | tf_op jit(solution)/shard_map/pallas_call | solution.py:444
  11.2 1.6 %reshape.37 = bf16[6,8,3200]{2,1,0:T(8,128)(2,1)S(1)} reshape(bf16[6,160,160]{2,1,0:T(8,128)(2,1)} %param.11) | data formatting | bytes 614400 | tf_op jit(solution)/shard_map/reshape | solution.py:477
  13.6 1.4 %collective-permute-done.1.edge = bf16[2,3,24,1440]{3,2,1,0:T(8,128)(2,1)S(1)} collective-permute-done((bf16[2,3,24,1440]{3,2,1,0:T(8,128)(2,1)S(1)}, bf16[2,3,24,1440]{3,2,1,0:T(8,128)(2,1)S(1)}, u32[]{:S(2)}, u32[]{:S(2)}) %collective-permute-start.1) | collective-permute-done | bytes 414752 | tf_op jit(solution)/shard_map/ppermute | solution.py:39
  15.7 5.4 %shard_map.96 = (f32[3,96,256]{2,1,0:T(8,128)}, bf16[3,48,1440]{2,1,0:T(8,128)(2,1)}) custom-call(s32[2]{0:T(128)} %pad_add_fusion.flags, bf16[2,3,24,1440]{3,2,1,0:T(8,128)(2,1)} %copy-done.8, f32[6,48,1440]{2,1,0:T(8,128)} %get-tuple-element.17.partial, bf16[49,48,128]{2,1,0:T(8,128)(2,1)} %get-tuple-element.18.taps, ...), custom_call_target="tpu_custom_call" | custom-call | flops 20321280 | bytes 3317760 | tf_op jit(solution)/shard_map/pallas_call | solution.py:444
  21.9 6.1 %all-to-all-start.1 = ((bf16[8,150,128]{2,1,0:T(8,128)(2,1)}), bf16[8,150,128]{2,1,0:T(8,128)(2,1)S(1)}, u32[]{:S(2)}, u32[]{:S(2)}) async-start(bf16[8,150,128]{2,1,0:T(8,128)(2,1)} %copy.15), calls=%async_computation.1 | async-start | bytes 622592 | tf_op jit(solution)/shard_map/all_to_all | solution.py:501
  28.0 4.8 %collective-permute-start = (bf16[2,3,24,1440]{3,2,1,0:T(8,128)(2,1)S(1)}, bf16[2,3,24,1440]{3,2,1,0:T(8,128)(2,1)S(1)}, u32[]{:S(2)}, u32[]{:S(2)}) collective-permute-start(bf16[2,3,24,1440]{3,2,1,0:T(8,128)(2,1)S(1)} %constant_dynamic-slice_fusion.1), channel_id=1, source_target_pairs={{0,7},{1,2},{2,1},{3,4},{4,3},{5,6},{6,5},{7,0},{8,15},{9,10},{10,... | collective-permute-start | bytes 1244168 | tf_op jit(solution)/shard_map/ppermute | solution.py:39
  32.8 13.9 %collective-permute-done.edge = bf16[2,3,24,1440]{3,2,1,0:T(8,128)(2,1)S(1)} collective-permute-done((bf16[2,3,24,1440]{3,2,1,0:T(8,128)(2,1)S(1)}, bf16[2,3,24,1440]{3,2,1,0:T(8,128)(2,1)S(1)}, u32[]{:S(2)}, u32[]{:S(2)}) %collective-permute-start) | collective-permute-done | bytes 414752 | tf_op jit(solution)/shard_map/ppermute | solution.py:39
  47.4 5.6 %shard_map.97 = (bf16[4,8,24,128]{3,2,1,0:T(8,128)(2,1)}, bf16[3,48,1440]{2,1,0:T(8,128)(2,1)}) custom-call(s32[2]{0:T(128)} %pad_add_fusion.flags, bf16[2,3,24,1440]{3,2,1,0:T(8,128)(2,1)} %copy-done.9, f32[6,48,1440]{2,1,0:T(8,128)} %get-tuple-element.17.partial, bf16[49,48,128]{2,1,0:T(8,128)(2,1)} %get-tuple-element.18.taps, ...), custom_call_target="tpu_custom_call" | custom-call | flops 20321280 | bytes 3317760 | tf_op jit(solution)/shard_map/pallas_call | solution.py:444
  53.0 2.7 %all-to-all-start = ((bf16[32,24,128]{2,1,0:T(8,128)(2,1)}), bf16[32,24,128]{2,1,0:T(8,128)(2,1)S(1)}, u32[]{:S(2)}, u32[]{:S(2)}) async-start(bf16[32,24,128]{2,1,0:T(8,128)(2,1)} %bitcast.36), calls=%async_computation | async-start | bytes 393216 | tf_op jit(solution)/shard_map/all_to_all | solution.py:457
  55.7 1.0 constant_dynamic-slice_fusion
  59.0 4.9 %all-to-all-done = bf16[32,24,128]{2,1,0:T(8,128)(2,1)S(1)} async-done(((bf16[32,24,128]{2,1,0:T(8,128)(2,1)}), bf16[32,24,128]{2,1,0:T(8,128)(2,1)S(1)}, u32[]{:S(2)}, u32[]{:S(2)}) %all-to-all-start) | async-done | bytes 196640 | tf_op jit(solution)/shard_map/all_to_all | solution.py:457
  64.6 6.5 %shard_map.98 = (bf16[4,8,24,256]{3,2,1,0:T(8,128)(2,1)}, f32[2,2560,128]{2,1,0:T(8,128)}) custom-call(bf16[4,8,24,128]{3,2,1,0:T(8,128)(2,1)} %bitcast.33, bf16[20,48,160]{2,1,0:T(8,128)(2,1)} %bitcast.29, bf16[20,16,160]{2,1,0:T(8,128)(2,1)} %pad.4.target, s32[1,160]{1,0:T(1,128)} %bitcast.39), custom_call_target="tpu_custom_call" | custom-call | flops 40642560 | bytes 3317760 | tf_op jit(solution)/shard_map/pallas_call | solution.py:444
  71.1 3.3 %all-to-all-start.2 = ((bf16[32,24,256]{2,1,0:T(8,128)(2,1)}), bf16[32,24,256]{2,1,0:T(8,128)(2,1)S(1)}, u32[]{:S(2)}, u32[]{:S(2)}) async-start(bf16[32,24,256]{2,1,0:T(8,128)(2,1)} %bitcast.35), calls=%async_computation.2 | async-start | bytes 786432 | tf_op jit(solution)/shard_map/all_to_all | solution.py:457
  74.5 4.2 %shard_map.101 = bf16[4,8,40,256]{3,2,1,0:T(8,128)(2,1)} custom-call(f32[2,2560,128]{2,1,0:T(8,128)} %get-tuple-element.27.grads), custom_call_target="tpu_custom_call" | custom-call | flops 40642560 | bytes 3317760 | tf_op jit(solution)/shard_map/pallas_call | solution.py:444
  78.6 9.2 %all-to-all-done.2 = bf16[32,24,256]{2,1,0:T(8,128)(2,1)S(1)} async-done(((bf16[32,24,256]{2,1,0:T(8,128)(2,1)}), bf16[32,24,256]{2,1,0:T(8,128)(2,1)S(1)}, u32[]{:S(2)}, u32[]{:S(2)}) %all-to-all-start.2) | async-done | bytes 393248 | tf_op jit(solution)/shard_map/all_to_all | solution.py:457
  87.9 2.8 %all-to-all-start.3 = ((bf16[32,40,256]{2,1,0:T(8,128)(2,1)}), bf16[32,40,256]{2,1,0:T(8,128)(2,1)S(1)}, u32[]{:S(2)}, u32[]{:S(2)}) async-start(bf16[32,40,256]{2,1,0:T(8,128)(2,1)} %bitcast.27), calls=%async_computation.3 | async-start | bytes 1310720 | tf_op jit(solution)/shard_map/all_to_all | solution.py:457
  90.7 4.4 %collective-permute-start.3 = (bf16[3,48,1440]{2,1,0:T(8,128)(2,1)S(1)}, bf16[3,48,1440]{2,1,0:T(8,128)(2,1)S(1)}, u32[]{:S(2)}, u32[]{:S(2)}) collective-permute-start(bf16[3,48,1440]{2,1,0:T(8,128)(2,1)S(1)} %copy-done.5), channel_id=1, source_target_pairs={{0,7},{1,2},{2,1},{3,4},{4,3},{5,6},{6,5},{7,0},{8,15},{9,10},{10,... | collective-permute-start | bytes 1244168 | tf_op jit(solution)/shard_map/ppermute | solution.py:39
  95.2 1.9 %shard_map.99.taps = bf16[49,48,128]{2,1,0:T(8,128)(2,1)} custom-call(f32[7,7,24]{2,1,0:T(8,128)} %bitcast.38), custom_call_target="tpu_custom_call" | custom-call | flops 5080320 | bytes 3317760 | tf_op jit(solution)/shard_map/pallas_call | solution.py:444
  97.0 19.2 %collective-permute-done.3.far = bf16[3,48,1440]{2,1,0:T(8,128)(2,1)S(1)} collective-permute-done((bf16[3,48,1440]{2,1,0:T(8,128)(2,1)S(1)}, bf16[3,48,1440]{2,1,0:T(8,128)(2,1)S(1)}, u32[]{:S(2)}, u32[]{:S(2)}) %collective-permute-start.3) | collective-permute-done | bytes 414752 | tf_op jit(solution)/shard_map/ppermute | solution.py:39
  116.3 4.4 %collective-permute-done.2.near = bf16[3,48,1440]{2,1,0:T(8,128)(2,1)S(1)} collective-permute-done((bf16[3,48,1440]{2,1,0:T(8,128)(2,1)S(1)}, bf16[3,48,1440]{2,1,0:T(8,128)(2,1)S(1)}, u32[]{:S(2)}, u32[]{:S(2)}) %collective-permute-start.2) | collective-permute-done | bytes 414752 | tf_op jit(solution)/shard_map/ppermute | solution.py:39
  121.4 9.9 %shard_map.100 = bf16[2,6,24,1440]{3,2,1,0:T(8,128)(2,1)} custom-call(s32[2]{0:T(128)} %pad_add_fusion.flags, bf16[4,8,24,256]{3,2,1,0:T(8,128)(2,1)} %bitcast.30, bf16[3,48,1440]{2,1,0:T(8,128)(2,1)} %copy-done.7, bf16[3,48,1440]{2,1,0:T(8,128)(2,1)} %copy-done.6, bf16[3,48,1440]{2,1,0:T(8,128)(2,1)} %get-tuple-element.25.inner, ...), custom_call_target="tpu_custom_call" | custom-call | flops 40642560 | bytes 3317760 | tf_op jit(solution)/shard_map/pallas_call | solution.py:444
  132.1 4.6 %unpack.1 = f32[2,24,20,2,160]{4,3,2,1,0:T(2,128)} custom-call(bf16[4,8,40,256]{3,2,1,0:T(8,128)(2,1)} %bitcast.26), custom_call_target="tpu_custom_call" | custom-call | flops 40642560 | bytes 1 | tf_op jit(solution)/shard_map/unpack/pallas_call | solution.py:566
  (31 shorter events, 7.6 us)
Async XLA Ops:
  1.7 13.2 %collective-permute-start.1 = (bf16[2,3,24,1440]{3,2,1,0:T(8,128)(2,1)S(1)}, bf16[2,3,24,1440]{3,2,1,0:T(8,128)(2,1)S(1)}, u32[]{:S(2)}, u32[]{:S(2)}) collective-permute-start(bf16[2,3,24,1440]{3,2,1,0:T(8,128)(2,1)S(1)} %dynamic-slice_bitcast_fusion), channel_id=1, source_target_pairs={{0,1},{1,0},{2,3},{3,2},{4,5},{5,4},{6,7},{7,6},{8,9},{9,8},{10,11... | collective-permute-start | bytes 1244168 | tf_op jit(solution)/shard_map/ppermute | solution.py:39
  14.9 0.8 copy-start.8
  15.7 12.2 %copy-start = (bf16[2,24,6,1440]{3,1,2,0:T(8,128)(2,1)S(1)}, bf16[2,24,6,1440]{3,1,2,0:T(8,128)(2,1)}, u32[]{:S(2)}) copy-start(bf16[2,24,6,1440]{3,1,2,0:T(8,128)(2,1)} %param.8) | copy-start | bytes 2488324
  21.9 31.1 %all-to-all-start.1 = ((bf16[8,150,128]{2,1,0:T(8,128)(2,1)}), bf16[8,150,128]{2,1,0:T(8,128)(2,1)S(1)}, u32[]{:S(2)}, u32[]{:S(2)}) async-start(bf16[8,150,128]{2,1,0:T(8,128)(2,1)} %copy.15), calls=%async_computation.1 | async-start | bytes 622592 | tf_op jit(solution)/shard_map/all_to_all | solution.py:501
  28.0 18.6 %collective-permute-start = (bf16[2,3,24,1440]{3,2,1,0:T(8,128)(2,1)S(1)}, bf16[2,3,24,1440]{3,2,1,0:T(8,128)(2,1)S(1)}, u32[]{:S(2)}, u32[]{:S(2)}) collective-permute-start(bf16[2,3,24,1440]{3,2,1,0:T(8,128)(2,1)S(1)} %constant_dynamic-slice_fusion.1), channel_id=1, source_target_pairs={{0,7},{1,2},{2,1},{3,4},{4,3},{5,6},{6,5},{7,0},{8,15},{9,10},{10,... | collective-permute-start | bytes 1244168 | tf_op jit(solution)/shard_map/ppermute | solution.py:39
  46.6 0.8 copy-start.9
  53.0 11.0 %all-to-all-start = ((bf16[32,24,128]{2,1,0:T(8,128)(2,1)}), bf16[32,24,128]{2,1,0:T(8,128)(2,1)S(1)}, u32[]{:S(2)}, u32[]{:S(2)}) async-start(bf16[32,24,128]{2,1,0:T(8,128)(2,1)} %bitcast.36), calls=%async_computation | async-start | bytes 393216 | tf_op jit(solution)/shard_map/all_to_all | solution.py:457
  63.9 0.7 copy-start.3
  71.1 19.6 %copy-start.5 = (bf16[3,48,1440]{2,1,0:T(8,128)(2,1)S(1)}, bf16[3,48,1440]{2,1,0:T(8,128)(2,1)}, u32[]{:S(2)}) copy-start(bf16[3,48,1440]{2,1,0:T(8,128)(2,1)} %get-tuple-element.26.outer) | copy-start | bytes 1244164
  71.1 24.0 %copy-start.4 = (bf16[3,48,1440]{2,1,0:T(8,128)(2,1)S(1)}, bf16[3,48,1440]{2,1,0:T(8,128)(2,1)}, u32[]{:S(2)}) copy-start(bf16[3,48,1440]{2,1,0:T(8,128)(2,1)} %get-tuple-element.25.inner) | copy-start | bytes 1244164
  71.1 16.8 %all-to-all-start.2 = ((bf16[32,24,256]{2,1,0:T(8,128)(2,1)}), bf16[32,24,256]{2,1,0:T(8,128)(2,1)S(1)}, u32[]{:S(2)}, u32[]{:S(2)}) async-start(bf16[32,24,256]{2,1,0:T(8,128)(2,1)} %bitcast.35), calls=%async_computation.2 | async-start | bytes 786432 | tf_op jit(solution)/shard_map/all_to_all | solution.py:457
  87.9 32.7 %copy-start.2 = (bf16[32,24,256]{2,1,0:T(8,128)(2,1)}, bf16[32,24,256]{2,1,0:T(8,128)(2,1)S(1)}, u32[]{:S(2)}) copy-start(bf16[32,24,256]{2,1,0:T(8,128)(2,1)S(1)} %all-to-all-done.2) | copy-start | bytes 1179652
  87.9 43.4 %all-to-all-start.3 = ((bf16[32,40,256]{2,1,0:T(8,128)(2,1)}), bf16[32,40,256]{2,1,0:T(8,128)(2,1)S(1)}, u32[]{:S(2)}, u32[]{:S(2)}) async-start(bf16[32,40,256]{2,1,0:T(8,128)(2,1)} %bitcast.27), calls=%async_computation.3 | async-start | bytes 1310720 | tf_op jit(solution)/shard_map/all_to_all | solution.py:457
  90.7 25.6 %collective-permute-start.3 = (bf16[3,48,1440]{2,1,0:T(8,128)(2,1)S(1)}, bf16[3,48,1440]{2,1,0:T(8,128)(2,1)S(1)}, u32[]{:S(2)}, u32[]{:S(2)}) collective-permute-start(bf16[3,48,1440]{2,1,0:T(8,128)(2,1)S(1)} %copy-done.5), channel_id=1, source_target_pairs={{0,7},{1,2},{2,1},{3,4},{4,3},{5,6},{6,5},{7,0},{8,15},{9,10},{10,... | collective-permute-start | bytes 1244168 | tf_op jit(solution)/shard_map/ppermute | solution.py:39
  95.1 25.5 %collective-permute-start.2 = (bf16[3,48,1440]{2,1,0:T(8,128)(2,1)S(1)}, bf16[3,48,1440]{2,1,0:T(8,128)(2,1)S(1)}, u32[]{:S(2)}, u32[]{:S(2)}) collective-permute-start(bf16[3,48,1440]{2,1,0:T(8,128)(2,1)S(1)} %copy-done.4), channel_id=1, source_target_pairs={{0,1},{1,0},{2,3},{3,2},{4,5},{5,4},{6,7},{7,6},{8,9},{9,8},{10,11... | collective-permute-start | bytes 1244168 | tf_op jit(solution)/shard_map/ppermute | solution.py:39
  116.3 4.4 %copy-start.6 = (bf16[3,48,1440]{2,1,0:T(8,128)(2,1)}, bf16[3,48,1440]{2,1,0:T(8,128)(2,1)S(1)}, u32[]{:S(2)}) copy-start(bf16[3,48,1440]{2,1,0:T(8,128)(2,1)S(1)} %collective-permute-done.3.far) | copy-start | bytes 1244164
  120.6 0.8 copy-start.7
  131.3 0.9 copy-start.1

commit v7 on v6

--- a/solution.py
+++ b/solution.py
@@ -366,36 +366,33 @@
                 out[e, t, b * share : (b + 1) * share, :] = jnp.concatenate(pieces, axis=1).astype(BF16)
 
 
-def unpack_kernel(members, got, out, swapped, pickers):
-    _, groups, depth, lanes = got.shape
-    _, chan_share, per_owner, _, orders = out.shape
-    share = depth // members
+def unpack_kernel(members, got, out):
+    owners, groups, depth, lanes = got.shape
+    _, chans, per_owner, _, orders = out.shape
+    share, chan_share = depth // members, chans // owners
     pair = 2 * per_owner
 
     def iotas(shape):
         return (lax.broadcasted_iota(jnp.int32, shape, d) for d in range(2))
 
-    @pl.when(pl.program_id(0) == 0)
-    def _():
-        row, column = iotas(swapped.shape)
-        wanted = ((row % 2) * chan_share + row // pair) * per_owner + (row % pair) // 2
-        swapped[...] = jnp.where(column == wanted, 1.0, 0.0).astype(BF16)
-        row, column = iotas(pickers.shape[1:])
-        start = (column // share) * depth + column % share
+    row, column = iotas((chan_share * pair, lanes))
+    wanted = ((row % 2) * chan_share + row // pair) * per_owner + (row % pair) // 2
+    swapped = jnp.where(column == wanted, 1.0, 0.0).astype(BF16)
+    row, column = iotas((groups * depth, orders))
+    start = (column // share) * depth + column % share
+    pickers = [jnp.where(row == start + b * share, 1.0, 0.0).astype(BF16) for b in range(members)]
+    for e in range(owners):
+        turned = lax.dot_general(
+            swapped,
+            got[e].reshape(groups * depth, lanes),
+            (((1,), (1,)), ((), ())),
+            preferred_element_type=F32,
+        ).astype(BF16)
         for b in range(members):
-            pickers[b] = jnp.where(row == start + b * share, 1.0, 0.0).astype(BF16)
-
-    turned = lax.dot_general(
-        swapped[...],
-        got[0].reshape(groups * depth, lanes),
-        (((1,), (1,)), ((), ())),
-        preferred_element_type=F32,
-    ).astype(BF16)
-    for b in range(members):
-        lines = jnp.dot(turned, pickers[b], preferred_element_type=F32)
-        for c in range(chan_share):
-            block = lines[c * pair : (c + 1) * pair]
-            out[b, c] = block.reshape(per_owner, 2, orders)
+            lines = jnp.dot(turned, pickers[b], preferred_element_type=F32)
+            for c in range(chan_share):
+                block = lines[c * pair : (c + 1) * pair]
+                out[b, e * chan_share + c] = block.reshape(per_owner, 2, orders)
 
 
 def local(fields, depth_kernel, mix_weight, legendre, truth, degree_order):
@@ -563,22 +560,13 @@
         mixer,
         table,
     )
-    score_grad = pl.pallas_call(
+    score_grad = call(
         functools.partial(unpack_kernel, members),
-        out_shape=jax.ShapeDtypeStruct((members, chans, per_owner, 2, orders), F32),
-        grid=(ens_parts,),
-        in_specs=[pl.BlockSpec((1,) + owned.shape[1:], lambda e: (e, 0, 0, 0))],
-        out_specs=pl.BlockSpec(
-            (members, chan_share, per_owner, 2, orders), lambda e: (0, e, 0, 0, 0)
-        ),
-        scratch_shapes=[
-            pltpu.VMEM((used * per_owner, owned.shape[3]), BF16),
-            pltpu.VMEM((members, groups * owned.shape[2], orders), BF16),
-        ],
-        compiler_params=vmem,
-        cost_estimate=pl.CostEstimate(flops=work, transcendentals=0, bytes_accessed=1),
-        name="unpack",
-    )(owned)
+        jax.ShapeDtypeStruct((members, chans, per_owner, 2, orders), F32),
+        [],
+        work,
+        owned,
+    )
     return grad_fields.transpose(0, 2, 1, 3), score_grad.transpose(0, 1, 3, 4, 2)
 
 

time: 138 us -> 137 us (level)
    pallas_call x1 -> x0, Pallas kernels: 4.59 us -> none  [local(): pl.pallas_call(functools.partial(unpack_kernel, members), out_shape=jax.S...]
    pallas_call x7 -> x8, Pallas kernels: 39.9 us -> 43.6 us  [call(): pl.pallas_call(body, out_shape=outs, in_specs=specs, scratch_shapes=scrat...]
  transfers between devices with their start and end apart: 8 -> 8, of which waited for: 6 -> 6; matrix products, arithmetic and copies ran while one was open for 4% -> 4% of each run, Pallas kernels for 20% -> 21%
where the time goes in v7:
time: 137 us; the launch traced here: 136 us
  waiting for transfers between devices  53 us (39%)
  Pallas kernels  43.6 us (32%)
  starting transfers between devices  27.2 us (20%)
  local copies, waits for them, and re-layouts  10.6 us (8%)
    pallas_call x8, Pallas kernels, call(): pl.pallas_call(body, out_shape=outs, in_specs=specs, scratch_shapes=scrat...  43.6 us
    ppermute x4, waiting for transfers between devices, partner(): return lax.ppermute(edge, 'lat', steps)  38.8 us
    all_to_all x3, waiting for transfers between devices, swap(): lax.all_to_all(flat, ('ens', 'lat'), split_axis=0, concat_axis=0, tiled=T...  14.2 us
    ppermute x4, starting transfers between devices, partner(): return lax.ppermute(edge, 'lat', steps)  12.3 us
    all_to_all x3, starting transfers between devices, swap(): lax.all_to_all(flat, ('ens', 'lat'), split_axis=0, concat_axis=0, tiled=T...  8.84 us
    all_to_all x1, starting transfers between devices, local(): slab = lax.all_to_all(slab, 'lat', split_axis=0, concat_axis=0, tiled=True)  6.05 us
    unnamed x21, local copies, waits for them, and re-layouts  3.86 us
  transfers between devices with their start and end apart: 8, of which 6 were waited for; matrix products, arithmetic and copies ran while one was open for 4% of the time, Pallas kernels for 21%

profile of v7, /device:TPU:0, one launch (start us, length us, event | category | flops | bytes accessed | tf_op | source)
XLA Modules:
  0.0 135.8 jit_solution(17454147029518566288)
XLA Ops:
  0.6 1.1 dynamic-slice_bitcast_fusion
  1.7 3.1 %collective-permute-start.1 = (bf16[2,3,24,1440]{3,2,1,0:T(8,128)(2,1)S(1)}, bf16[2,3,24,1440]{3,2,1,0:T(8,128)(2,1)S(1)}, u32[]{:S(2)}, u32[]{:S(2)}) collective-permute-start(bf16[2,3,24,1440]{3,2,1,0:T(8,128)(2,1)S(1)} %dynamic-slice_bitcast_fusion), channel_id=1, source_target_pairs={{0,1},{1,0},{2,3},{3,2},{4,5},{5,4},{6,7},{7,6},{8,9},{9,8},{10,11... | collective-permute-start | bytes 1244168 | tf_op jit(solution)/shard_map/ppermute | solution.py:39
  4.8 6.5 %shard_map.95 = (f32[6,48,1440]{2,1,0:T(8,128)}, bf16[49,48,128]{2,1,0:T(8,128)(2,1)}, bf16[2,96,48]{2,1,0:T(8,128)(2,1)}) custom-call(bf16[2,6,24,1440]{3,2,1,0:T(8,128)(2,1)} %bitcast.24, f32[7,7,24]{2,1,0:T(8,128)} %bitcast.37, bf16[24,24]{1,0:T(8,128)(2,1)} %weight.1, bf16[2,2,96,24]{3,2,1,0:T(8,128)(2,1)} %constant.44.clone.pick), custom_call_target="tpu_custom_call" | custom-call | flops 40642560 | bytes 3317760 | tf_op jit(solution)/shard_map/pallas_call | solution.py:441
  11.2 1.6 %reshape.37 = bf16[6,8,3200]{2,1,0:T(8,128)(2,1)S(1)} reshape(bf16[6,160,160]{2,1,0:T(8,128)(2,1)} %param.11) | data formatting | bytes 614400 | tf_op jit(solution)/shard_map/reshape | solution.py:474
  13.6 1.4 %collective-permute-done.1.edge = bf16[2,3,24,1440]{3,2,1,0:T(8,128)(2,1)S(1)} collective-permute-done((bf16[2,3,24,1440]{3,2,1,0:T(8,128)(2,1)S(1)}, bf16[2,3,24,1440]{3,2,1,0:T(8,128)(2,1)S(1)}, u32[]{:S(2)}, u32[]{:S(2)}) %collective-permute-start.1) | collective-permute-done | bytes 414752 | tf_op jit(solution)/shard_map/ppermute | solution.py:39
  15.7 5.4 %shard_map.96 = (f32[3,96,256]{2,1,0:T(8,128)}, bf16[3,48,1440]{2,1,0:T(8,128)(2,1)}) custom-call(s32[2]{0:T(128)} %pad_add_fusion.flags, bf16[2,3,24,1440]{3,2,1,0:T(8,128)(2,1)} %copy-done.8, f32[6,48,1440]{2,1,0:T(8,128)} %get-tuple-element.17.partial, bf16[49,48,128]{2,1,0:T(8,128)(2,1)} %get-tuple-element.18.taps, ...), custom_call_target="tpu_custom_call" | custom-call | flops 20321280 | bytes 3317760 | tf_op jit(solution)/shard_map/pallas_call | solution.py:441
  21.9 6.1 %all-to-all-start.1 = ((bf16[8,150,128]{2,1,0:T(8,128)(2,1)}), bf16[8,150,128]{2,1,0:T(8,128)(2,1)S(1)}, u32[]{:S(2)}, u32[]{:S(2)}) async-start(bf16[8,150,128]{2,1,0:T(8,128)(2,1)} %copy.15), calls=%async_computation.1 | async-start | bytes 622592 | tf_op jit(solution)/shard_map/all_to_all | solution.py:498
  28.0 4.8 %collective-permute-start = (bf16[2,3,24,1440]{3,2,1,0:T(8,128)(2,1)S(1)}, bf16[2,3,24,1440]{3,2,1,0:T(8,128)(2,1)S(1)}, u32[]{:S(2)}, u32[]{:S(2)}) collective-permute-start(bf16[2,3,24,1440]{3,2,1,0:T(8,128)(2,1)S(1)} %constant_dynamic-slice_fusion.1), channel_id=1, source_target_pairs={{0,7},{1,2},{2,1},{3,4},{4,3},{5,6},{6,5},{7,0},{8,15},{9,10},{10,... | collective-permute-start | bytes 1244168 | tf_op jit(solution)/shard_map/ppermute | solution.py:39
  32.8 13.9 %collective-permute-done.edge = bf16[2,3,24,1440]{3,2,1,0:T(8,128)(2,1)S(1)} collective-permute-done((bf16[2,3,24,1440]{3,2,1,0:T(8,128)(2,1)S(1)}, bf16[2,3,24,1440]{3,2,1,0:T(8,128)(2,1)S(1)}, u32[]{:S(2)}, u32[]{:S(2)}) %collective-permute-start) | collective-permute-done | bytes 414752 | tf_op jit(solution)/shard_map/ppermute | solution.py:39
  47.4 5.6 %shard_map.97 = (bf16[4,8,24,128]{3,2,1,0:T(8,128)(2,1)}, bf16[3,48,1440]{2,1,0:T(8,128)(2,1)}) custom-call(s32[2]{0:T(128)} %pad_add_fusion.flags, bf16[2,3,24,1440]{3,2,1,0:T(8,128)(2,1)} %copy-done.9, f32[6,48,1440]{2,1,0:T(8,128)} %get-tuple-element.17.partial, bf16[49,48,128]{2,1,0:T(8,128)(2,1)} %get-tuple-element.18.taps, ...), custom_call_target="tpu_custom_call" | custom-call | flops 20321280 | bytes 3317760 | tf_op jit(solution)/shard_map/pallas_call | solution.py:441
  53.0 2.7 %all-to-all-start = ((bf16[32,24,128]{2,1,0:T(8,128)(2,1)}), bf16[32,24,128]{2,1,0:T(8,128)(2,1)S(1)}, u32[]{:S(2)}, u32[]{:S(2)}) async-start(bf16[32,24,128]{2,1,0:T(8,128)(2,1)} %bitcast.36), calls=%async_computation | async-start | bytes 393216 | tf_op jit(solution)/shard_map/all_to_all | solution.py:454
  55.7 1.0 constant_dynamic-slice_fusion
  59.0 4.9 %all-to-all-done = bf16[32,24,128]{2,1,0:T(8,128)(2,1)S(1)} async-done(((bf16[32,24,128]{2,1,0:T(8,128)(2,1)}), bf16[32,24,128]{2,1,0:T(8,128)(2,1)S(1)}, u32[]{:S(2)}, u32[]{:S(2)}) %all-to-all-start) | async-done | bytes 196640 | tf_op jit(solution)/shard_map/all_to_all | solution.py:454
  64.6 6.5 %shard_map.98 = (bf16[4,8,24,256]{3,2,1,0:T(8,128)(2,1)}, f32[2,2560,128]{2,1,0:T(8,128)}) custom-call(bf16[4,8,24,128]{3,2,1,0:T(8,128)(2,1)} %bitcast.33, bf16[20,48,160]{2,1,0:T(8,128)(2,1)} %bitcast.29, bf16[20,16,160]{2,1,0:T(8,128)(2,1)} %pad.4.target, s32[1,160]{1,0:T(1,128)} %bitcast.39), custom_call_target="tpu_custom_call" | custom-call | flops 40642560 | bytes 3317760 | tf_op jit(solution)/shard_map/pallas_call | solution.py:441
  71.1 3.3 %all-to-all-start.2 = ((bf16[32,24,256]{2,1,0:T(8,128)(2,1)}), bf16[32,24,256]{2,1,0:T(8,128)(2,1)S(1)}, u32[]{:S(2)}, u32[]{:S(2)}) async-start(bf16[32,24,256]{2,1,0:T(8,128)(2,1)} %bitcast.35), calls=%async_computation.2 | async-start | bytes 786432 | tf_op jit(solution)/shard_map/all_to_all | solution.py:454
  74.5 4.2 %shard_map.101 = bf16[4,8,40,256]{3,2,1,0:T(8,128)(2,1)} custom-call(f32[2,2560,128]{2,1,0:T(8,128)} %get-tuple-element.27.grads), custom_call_target="tpu_custom_call" | custom-call | flops 40642560 | bytes 3317760 | tf_op jit(solution)/shard_map/pallas_call | solution.py:441
  78.6 9.2 %all-to-all-done.2 = bf16[32,24,256]{2,1,0:T(8,128)(2,1)S(1)} async-done(((bf16[32,24,256]{2,1,0:T(8,128)(2,1)}), bf16[32,24,256]{2,1,0:T(8,128)(2,1)S(1)}, u32[]{:S(2)}, u32[]{:S(2)}) %all-to-all-start.2) | async-done | bytes 393248 | tf_op jit(solution)/shard_map/all_to_all | solution.py:454
  87.9 2.8 %all-to-all-start.3 = ((bf16[32,40,256]{2,1,0:T(8,128)(2,1)}), bf16[32,40,256]{2,1,0:T(8,128)(2,1)S(1)}, u32[]{:S(2)}, u32[]{:S(2)}) async-start(bf16[32,40,256]{2,1,0:T(8,128)(2,1)} %bitcast.27), calls=%async_computation.3 | async-start | bytes 1310720 | tf_op jit(solution)/shard_map/all_to_all | solution.py:454
  90.7 4.4 %collective-permute-start.3 = (bf16[3,48,1440]{2,1,0:T(8,128)(2,1)S(1)}, bf16[3,48,1440]{2,1,0:T(8,128)(2,1)S(1)}, u32[]{:S(2)}, u32[]{:S(2)}) collective-permute-start(bf16[3,48,1440]{2,1,0:T(8,128)(2,1)S(1)} %copy-done.5), channel_id=1, source_target_pairs={{0,7},{1,2},{2,1},{3,4},{4,3},{5,6},{6,5},{7,0},{8,15},{9,10},{10,... | collective-permute-start | bytes 1244168 | tf_op jit(solution)/shard_map/ppermute | solution.py:39
  95.2 1.9 %shard_map.99.taps = bf16[49,48,128]{2,1,0:T(8,128)(2,1)} custom-call(f32[7,7,24]{2,1,0:T(8,128)} %bitcast.38), custom_call_target="tpu_custom_call" | custom-call | flops 5080320 | bytes 3317760 | tf_op jit(solution)/shard_map/pallas_call | solution.py:441
  97.0 19.2 %collective-permute-done.3.far = bf16[3,48,1440]{2,1,0:T(8,128)(2,1)S(1)} collective-permute-done((bf16[3,48,1440]{2,1,0:T(8,128)(2,1)S(1)}, bf16[3,48,1440]{2,1,0:T(8,128)(2,1)S(1)}, u32[]{:S(2)}, u32[]{:S(2)}) %collective-permute-start.3) | collective-permute-done | bytes 414752 | tf_op jit(solution)/shard_map/ppermute | solution.py:39
  116.3 4.4 %collective-permute-done.2.near = bf16[3,48,1440]{2,1,0:T(8,128)(2,1)S(1)} collective-permute-done((bf16[3,48,1440]{2,1,0:T(8,128)(2,1)S(1)}, bf16[3,48,1440]{2,1,0:T(8,128)(2,1)S(1)}, u32[]{:S(2)}, u32[]{:S(2)}) %collective-permute-start.2) | collective-permute-done | bytes 414752 | tf_op jit(solution)/shard_map/ppermute | solution.py:39
  121.4 9.9 %shard_map.100 = bf16[2,6,24,1440]{3,2,1,0:T(8,128)(2,1)} custom-call(s32[2]{0:T(128)} %pad_add_fusion.flags, bf16[4,8,24,256]{3,2,1,0:T(8,128)(2,1)} %bitcast.30, bf16[3,48,1440]{2,1,0:T(8,128)(2,1)} %copy-done.7, bf16[3,48,1440]{2,1,0:T(8,128)(2,1)} %copy-done.6, bf16[3,48,1440]{2,1,0:T(8,128)(2,1)} %get-tuple-element.25.inner, ...), custom_call_target="tpu_custom_call" | custom-call | flops 40642560 | bytes 3317760 | tf_op jit(solution)/shard_map/pallas_call | solution.py:441
  132.1 3.7 %shard_map.102 = f32[2,24,20,2,160]{4,3,2,1,0:T(2,128)} custom-call(bf16[4,8,40,256]{3,2,1,0:T(8,128)(2,1)} %bitcast.26), custom_call_target="tpu_custom_call" | custom-call | flops 40642560 | bytes 3317760 | tf_op jit(solution)/shard_map/pallas_call | solution.py:441
  (31 shorter events, 7.6 us)
Async XLA Ops:
  1.7 13.2 %collective-permute-start.1 = (bf16[2,3,24,1440]{3,2,1,0:T(8,128)(2,1)S(1)}, bf16[2,3,24,1440]{3,2,1,0:T(8,128)(2,1)S(1)}, u32[]{:S(2)}, u32[]{:S(2)}) collective-permute-start(bf16[2,3,24,1440]{3,2,1,0:T(8,128)(2,1)S(1)} %dynamic-slice_bitcast_fusion), channel_id=1, source_target_pairs={{0,1},{1,0},{2,3},{3,2},{4,5},{5,4},{6,7},{7,6},{8,9},{9,8},{10,11... | collective-permute-start | bytes 1244168 | tf_op jit(solution)/shard_map/ppermute | solution.py:39
  14.9 0.8 copy-start.8
  15.7 12.2 %copy-start = (bf16[2,24,6,1440]{3,1,2,0:T(8,128)(2,1)S(1)}, bf16[2,24,6,1440]{3,1,2,0:T(8,128)(2,1)}, u32[]{:S(2)}) copy-start(bf16[2,24,6,1440]{3,1,2,0:T(8,128)(2,1)} %param.8) | copy-start | bytes 2488324
  21.9 31.1 %all-to-all-start.1 = ((bf16[8,150,128]{2,1,0:T(8,128)(2,1)}), bf16[8,150,128]{2,1,0:T(8,128)(2,1)S(1)}, u32[]{:S(2)}, u32[]{:S(2)}) async-start(bf16[8,150,128]{2,1,0:T(8,128)(2,1)} %copy.15), calls=%async_computation.1 | async-start | bytes 622592 | tf_op jit(solution)/shard_map/all_to_all | solution.py:498
  28.0 18.6 %collective-permute-start = (bf16[2,3,24,1440]{3,2,1,0:T(8,128)(2,1)S(1)}, bf16[2,3,24,1440]{3,2,1,0:T(8,128)(2,1)S(1)}, u32[]{:S(2)}, u32[]{:S(2)}) collective-permute-start(bf16[2,3,24,1440]{3,2,1,0:T(8,128)(2,1)S(1)} %constant_dynamic-slice_fusion.1), channel_id=1, source_target_pairs={{0,7},{1,2},{2,1},{3,4},{4,3},{5,6},{6,5},{7,0},{8,15},{9,10},{10,... | collective-permute-start | bytes 1244168 | tf_op jit(solution)/shard_map/ppermute | solution.py:39
  46.6 0.8 copy-start.9
  53.0 11.0 %all-to-all-start = ((bf16[32,24,128]{2,1,0:T(8,128)(2,1)}), bf16[32,24,128]{2,1,0:T(8,128)(2,1)S(1)}, u32[]{:S(2)}, u32[]{:S(2)}) async-start(bf16[32,24,128]{2,1,0:T(8,128)(2,1)} %bitcast.36), calls=%async_computation | async-start | bytes 393216 | tf_op jit(solution)/shard_map/all_to_all | solution.py:454
  63.9 0.7 copy-start.3
  71.1 19.6 %copy-start.5 = (bf16[3,48,1440]{2,1,0:T(8,128)(2,1)S(1)}, bf16[3,48,1440]{2,1,0:T(8,128)(2,1)}, u32[]{:S(2)}) copy-start(bf16[3,48,1440]{2,1,0:T(8,128)(2,1)} %get-tuple-element.26.outer) | copy-start | bytes 1244164
  71.1 24.0 %copy-start.4 = (bf16[3,48,1440]{2,1,0:T(8,128)(2,1)S(1)}, bf16[3,48,1440]{2,1,0:T(8,128)(2,1)}, u32[]{:S(2)}) copy-start(bf16[3,48,1440]{2,1,0:T(8,128)(2,1)} %get-tuple-element.25.inner) | copy-start | bytes 1244164
  71.1 16.8 %all-to-all-start.2 = ((bf16[32,24,256]{2,1,0:T(8,128)(2,1)}), bf16[32,24,256]{2,1,0:T(8,128)(2,1)S(1)}, u32[]{:S(2)}, u32[]{:S(2)}) async-start(bf16[32,24,256]{2,1,0:T(8,128)(2,1)} %bitcast.35), calls=%async_computation.2 | async-start | bytes 786432 | tf_op jit(solution)/shard_map/all_to_all | solution.py:454
  87.9 32.7 %copy-start.2 = (bf16[32,24,256]{2,1,0:T(8,128)(2,1)}, bf16[32,24,256]{2,1,0:T(8,128)(2,1)S(1)}, u32[]{:S(2)}) copy-start(bf16[32,24,256]{2,1,0:T(8,128)(2,1)S(1)} %all-to-all-done.2) | copy-start | bytes 1179652
  87.9 43.4 %all-to-all-start.3 = ((bf16[32,40,256]{2,1,0:T(8,128)(2,1)}), bf16[32,40,256]{2,1,0:T(8,128)(2,1)S(1)}, u32[]{:S(2)}, u32[]{:S(2)}) async-start(bf16[32,40,256]{2,1,0:T(8,128)(2,1)} %bitcast.27), calls=%async_computation.3 | async-start | bytes 1310720 | tf_op jit(solution)/shard_map/all_to_all | solution.py:454
  90.7 25.6 %collective-permute-start.3 = (bf16[3,48,1440]{2,1,0:T(8,128)(2,1)S(1)}, bf16[3,48,1440]{2,1,0:T(8,128)(2,1)S(1)}, u32[]{:S(2)}, u32[]{:S(2)}) collective-permute-start(bf16[3,48,1440]{2,1,0:T(8,128)(2,1)S(1)} %copy-done.5), channel_id=1, source_target_pairs={{0,7},{1,2},{2,1},{3,4},{4,3},{5,6},{6,5},{7,0},{8,15},{9,10},{10,... | collective-permute-start | bytes 1244168 | tf_op jit(solution)/shard_map/ppermute | solution.py:39
  95.1 25.5 %collective-permute-start.2 = (bf16[3,48,1440]{2,1,0:T(8,128)(2,1)S(1)}, bf16[3,48,1440]{2,1,0:T(8,128)(2,1)S(1)}, u32[]{:S(2)}, u32[]{:S(2)}) collective-permute-start(bf16[3,48,1440]{2,1,0:T(8,128)(2,1)S(1)} %copy-done.4), channel_id=1, source_target_pairs={{0,1},{1,0},{2,3},{3,2},{4,5},{5,4},{6,7},{7,6},{8,9},{9,8},{10,11... | collective-permute-start | bytes 1244168 | tf_op jit(solution)/shard_map/ppermute | solution.py:39
  116.3 4.4 %copy-start.6 = (bf16[3,48,1440]{2,1,0:T(8,128)(2,1)}, bf16[3,48,1440]{2,1,0:T(8,128)(2,1)S(1)}, u32[]{:S(2)}) copy-start(bf16[3,48,1440]{2,1,0:T(8,128)(2,1)S(1)} %collective-permute-done.3.far) | copy-start | bytes 1244164
  120.6 0.8 copy-start.7
  131.3 0.9 copy-start.1

commit v8 on v7

--- a/solution.py
+++ b/solution.py
@@ -30,12 +30,14 @@
     return table.reshape(nlon, 2 * span).astype(jnp.bfloat16)
 
 
-def partner(edge, pair):
-    count = lax.axis_size("lat")
-    if pair:
-        steps = [(i, i ^ 1) for i in range(count)]
-    else:
-        steps = [(i, (i + (1 if i % 2 else -1)) % count) for i in range(count)]
+def pairs_of(count, shift):
+    return [[i, (i + 1) % count] for i in range(shift, count, 2)]
+
+
+def partner(edge, near):
+    steps = []
+    for one, other in pairs_of(lax.axis_size("lat"), 0 if near else 1):
+        steps += [(one, other), (other, one)]
     return lax.ppermute(edge, "lat", steps)
 
 
@@ -162,7 +164,8 @@
 
 
 def near_kernel(flags, edge, partial, taps, table, mixer, mixed, slope, padded, act):
-    lines = finish_rows(flags[0] == 1, None, edge, partial, taps, table, mixer, slope, padded, act)
+    odd = flags[0]
+    lines = finish_rows(odd == 1, None, edge.at[1 - odd], partial, taps, table, mixer, slope, padded, act)
     for j, line in enumerate(lines):
         mixed[j] = line
 
@@ -417,8 +420,9 @@
     flags = place()
     own = fields.transpose(0, 2, 1, 3)
     odd = lat_at % 2
-    inner = lax.dynamic_slice_in_dim(own, (1 - odd) * (rows - halo), halo, 1)
-    near = partner(inner, True)
+    ends = jnp.stack([own[:, :halo], own[:, rows - halo :]])
+    near = lax.all_to_all(ends, "lat", split_axis=0, concat_axis=0, tiled=True, axis_index_groups=pairs_of(groups, 0))
+    far = partner(lax.dynamic_slice_in_dim(own, odd * (rows - halo), halo, 1), False)
 
     pick = np.zeros((2, members, ens_parts, height, chans), np.float32)
     for r in range(2):
@@ -474,9 +478,6 @@
     slab = legendre.reshape(rows, groups, share * degrees).transpose(1, 0, 2)
     line = math.gcd(rows * share * degrees, 128)
     slab = slab.reshape(groups, rows * share * degrees // line, line)
-    late, partial = lax.optimization_barrier((own, partial))
-    outer = lax.dynamic_slice_in_dim(late, odd * (rows - halo), halo, 1)
-    far = partner(outer, False)
 
     def chunk(lines):
         return jax.ShapeDtypeStruct((ens_parts, groups, height, up(lines * share, 128)), BF16)
@@ -511,7 +512,8 @@
         mixed,
     )
     got = swap(sent)
-    near, far = partner(inner, True), partner(outer, False)
+    got, held = lax.optimization_barrier((got, outer))
+    near, far = partner(inner, True), partner(held, False)
     back, grads = call(
         functools.partial(score_kernel, members, used, rows, halo),
         (

time: 137 us -> 142 us (1.036)
  starting transfers between devices: 27.2 us -> 30.8 us
  waiting for transfers between devices: 53 us -> 55.2 us
    ppermute x4 -> x3, waiting for transfers between devices: 38.8 us -> 21.7 us  [partner(): return lax.ppermute(edge, 'lat', steps)]
    all_to_all x0 -> x1, waiting for transfers between devices: none -> 8.5 us  [local(): lax.all_to_all(ends, 'lat', split_axis=0, concat_axis=0, tiled=True, axis...]
    all_to_all x1, waiting for transfers between devices: 0.01 us -> 8.28 us  [local(): slab = lax.all_to_all(slab, 'lat', split_axis=0, concat_axis=0, tiled=True)]
    all_to_all x0 -> x1, starting transfers between devices: none -> 4.26 us  [local(): lax.all_to_all(ends, 'lat', split_axis=0, concat_axis=0, tiled=True, axis...]
    all_to_all x3, starting transfers between devices: 8.84 us -> 11.5 us  [swap(): lax.all_to_all(flat, ('ens', 'lat'), split_axis=0, concat_axis=0, tiled=T...]
    all_to_all x3, waiting for transfers between devices: 14.2 us -> 16.7 us  [swap(): lax.all_to_all(flat, ('ens', 'lat'), split_axis=0, concat_axis=0, tiled=T...]
    all_to_all x1, starting transfers between devices: 6.05 us -> 4.17 us  [local(): slab = lax.all_to_all(slab, 'lat', split_axis=0, concat_axis=0, tiled=True)]
    ppermute x4 -> x3, starting transfers between devices: 12.3 us -> 10.9 us  [partner(): return lax.ppermute(edge, 'lat', steps)]
  transfers between devices with their start and end apart: 8 -> 8, of which waited for: 6 -> 5; matrix products, arithmetic and copies ran while one was open for 4% -> 3% of each run, Pallas kernels for 21% -> 20%
where the time goes in v8:
time: 142 us
  waiting for transfers between devices  55.2 us (39%)
  Pallas kernels  43.7 us (31%)
  starting transfers between devices  30.8 us (22%)
  local copies, waits for them, and re-layouts  9.47 us (7%)
  other arithmetic  1.57 us (1%)
    pallas_call x8, Pallas kernels, call(): pl.pallas_call(body, out_shape=outs, in_specs=specs, scratch_shapes=scrat...  43.7 us
    ppermute x3, waiting for transfers between devices, partner(): return lax.ppermute(edge, 'lat', steps)  21.7 us
    all_to_all x3, waiting for transfers between devices, swap(): lax.all_to_all(flat, ('ens', 'lat'), split_axis=0, concat_axis=0, tiled=T...  16.7 us
    all_to_all x3, starting transfers between devices, swap(): lax.all_to_all(flat, ('ens', 'lat'), split_axis=0, concat_axis=0, tiled=T...  11.5 us
    ppermute x3, starting transfers between devices, partner(): return lax.ppermute(edge, 'lat', steps)  10.9 us
    all_to_all x1, waiting for transfers between devices, local(): lax.all_to_all(ends, 'lat', split_axis=0, concat_axis=0, tiled=True, axis...  8.5 us
    all_to_all x1, waiting for transfers between devices, local(): slab = lax.all_to_all(slab, 'lat', split_axis=0, concat_axis=0, tiled=True)  8.28 us
    all_to_all x1, starting transfers between devices, local(): lax.all_to_all(ends, 'lat', split_axis=0, concat_axis=0, tiled=True, axis...  4.26 us
  transfers between devices with their start and end apart: 8, of which 5 were waited for; matrix products, arithmetic and copies ran while one was open for 3% of the time, Pallas kernels for 20%

profile of v8, /device:TPU:0, one launch (start us, length us, event | category | flops | bytes accessed | tf_op | source)
XLA Modules:
  0.0 141.5 jit_solution(17547897243011350366)
XLA Ops:
  0.6 1.3 slice_bitcast_fusion.1
  1.9 1.0 pad_maximum_fusion
  2.9 4.3 %all-to-all-start = ((bf16[2,2,3,24,1440]{4,3,2,1,0:T(8,128)(2,1)}), bf16[2,2,3,24,1440]{4,3,2,1,0:T(8,128)(2,1)S(1)}, u32[]{:S(2)}, u32[]{:S(2)}) async-start(bf16[2,2,3,24,1440]{4,3,2,1,0:T(8,128)(2,1)} %pad_maximum_fusion), calls=%async_computation | async-start | bytes 1769472 | tf_op jit(solution)/shard_map/all_to_all | solution.py:424
  7.2 5.9 %collective-permute-start = (bf16[2,3,24,1440]{3,2,1,0:T(8,128)(2,1)S(1)}, bf16[2,3,24,1440]{3,2,1,0:T(8,128)(2,1)S(1)}, u32[]{:S(2)}, u32[]{:S(2)}) collective-permute-start(bf16[2,3,24,1440]{3,2,1,0:T(8,128)(2,1)S(1)} %dynamic-slice_bitcast_fusion), channel_id=1, source_target_pairs={{1,2},{2,1},{3,4},{4,3},{5,6},{6,5},{7,0},{0,7},{9,10},{10,9},{11,... | collective-permute-start | bytes 1244168 | tf_op jit(solution)/shard_map/ppermute | solution.py:41
  13.8 6.5 %shard_map.95 = (f32[6,48,1440]{2,1,0:T(8,128)}, bf16[49,48,128]{2,1,0:T(8,128)(2,1)}, bf16[2,96,48]{2,1,0:T(8,128)(2,1)}) custom-call(bf16[2,6,24,1440]{3,2,1,0:T(8,128)(2,1)} %bitcast.29, f32[7,7,24]{2,1,0:T(8,128)} %bitcast.41, bf16[24,24]{1,0:T(8,128)(2,1)} %weight.1, bf16[2,2,96,24]{3,2,1,0:T(8,128)(2,1)} %constant.43.clone.pick), custom_call_target="tpu_custom_call" | custom-call | flops 40642560 | bytes 3317760 | tf_op jit(solution)/shard_map/pallas_call | solution.py:445
  20.8 8.5 %all-to-all-done.edge = bf16[2,2,3,24,1440]{4,3,2,1,0:T(8,128)(2,1)S(1)} async-done(((bf16[2,2,3,24,1440]{4,3,2,1,0:T(8,128)(2,1)}), bf16[2,2,3,24,1440]{4,3,2,1,0:T(8,128)(2,1)S(1)}, u32[]{:S(2)}, u32[]{:S(2)}) %all-to-all-start) | async-done | bytes 829472 | tf_op jit(solution)/shard_map/all_to_all | solution.py:424
  30.2 5.5 %shard_map.96 = (f32[3,96,256]{2,1,0:T(8,128)}, bf16[3,48,1440]{2,1,0:T(8,128)(2,1)}) custom-call(s32[2]{0:T(128)} %pad_add_fusion.flags, bf16[2,2,3,24,1440]{4,3,2,1,0:T(8,128)(2,1)} %copy-done.1, f32[6,48,1440]{2,1,0:T(8,128)} %get-tuple-element.15.partial, bf16[49,48,128]{2,1,0:T(8,128)(2,1)} %get-tuple-element.16.taps, ...), custom_call_target="tpu_custom_call" | custom-call | flops 20321280 | bytes 3317760 | tf_op jit(solution)/shard_map/pallas_call | solution.py:445
  36.5 5.6 %shard_map.97 = (bf16[4,8,24,128]{3,2,1,0:T(8,128)(2,1)}, bf16[3,48,1440]{2,1,0:T(8,128)(2,1)}) custom-call(s32[2]{0:T(128)} %pad_add_fusion.flags, bf16[2,3,24,1440]{3,2,1,0:T(8,128)(2,1)} %copy-done.10, f32[6,48,1440]{2,1,0:T(8,128)} %get-tuple-element.15.partial, bf16[49,48,128]{2,1,0:T(8,128)(2,1)} %get-tuple-element.16.taps, ...), custom_call_target="tpu_custom_call" | custom-call | flops 20321280 | bytes 3317760 | tf_op jit(solution)/shard_map/pallas_call | solution.py:445
  42.1 5.1 %all-to-all-start.1 = ((bf16[32,24,128]{2,1,0:T(8,128)(2,1)}), bf16[32,24,128]{2,1,0:T(8,128)(2,1)S(1)}, u32[]{:S(2)}, u32[]{:S(2)}) async-start(bf16[32,24,128]{2,1,0:T(8,128)(2,1)} %bitcast.40), calls=%async_computation.1 | async-start | bytes 393216 | tf_op jit(solution)/shard_map/all_to_all | solution.py:458
  48.0 7.5 %all-to-all-done.1 = bf16[32,24,128]{2,1,0:T(8,128)(2,1)S(1)} async-done(((bf16[32,24,128]{2,1,0:T(8,128)(2,1)}), bf16[32,24,128]{2,1,0:T(8,128)(2,1)S(1)}, u32[]{:S(2)}, u32[]{:S(2)}) %all-to-all-start.1) | async-done | bytes 196640 | tf_op jit(solution)/shard_map/all_to_all | solution.py:458
  55.5 4.2 %all-to-all-start.2 = ((bf16[8,150,128]{2,1,0:T(8,128)(2,1)}), bf16[8,150,128]{2,1,0:T(8,128)(2,1)S(1)}, u32[]{:S(2)}, u32[]{:S(2)}) async-start(bf16[8,150,128]{2,1,0:T(8,128)(2,1)} %copy.15), calls=%async_computation.2 | async-start | bytes 622592 | tf_op jit(solution)/shard_map/all_to_all | solution.py:499
  59.6 1.0 constant_dynamic-slice_fusion
  61.4 8.3 %all-to-all-done.2 = bf16[8,150,128]{2,1,0:T(8,128)(2,1)S(1)} async-done(((bf16[8,150,128]{2,1,0:T(8,128)(2,1)}), bf16[8,150,128]{2,1,0:T(8,128)(2,1)S(1)}, u32[]{:S(2)}, u32[]{:S(2)}) %all-to-all-start.2) | async-done | bytes 307232 | tf_op jit(solution)/shard_map/all_to_all | solution.py:499
  71.2 6.5 %shard_map.98 = (bf16[4,8,24,256]{3,2,1,0:T(8,128)(2,1)}, f32[2,2560,128]{2,1,0:T(8,128)}) custom-call(bf16[4,8,24,128]{3,2,1,0:T(8,128)(2,1)} %bitcast.37, bf16[20,48,160]{2,1,0:T(8,128)(2,1)} %bitcast.33, bf16[20,16,160]{2,1,0:T(8,128)(2,1)} %pad.4.target, s32[1,160]{1,0:T(1,128)} %bitcast.43), custom_call_target="tpu_custom_call" | custom-call | flops 40642560 | bytes 3317760 | tf_op jit(solution)/shard_map/pallas_call | solution.py:445
  77.7 3.6 %all-to-all-start.3 = ((bf16[32,24,256]{2,1,0:T(8,128)(2,1)}), bf16[32,24,256]{2,1,0:T(8,128)(2,1)S(1)}, u32[]{:S(2)}, u32[]{:S(2)}) async-start(bf16[32,24,256]{2,1,0:T(8,128)(2,1)} %bitcast.39), calls=%async_computation.3 | async-start | bytes 786432 | tf_op jit(solution)/shard_map/all_to_all | solution.py:458
  81.3 4.2 %shard_map.101 = bf16[4,8,40,256]{3,2,1,0:T(8,128)(2,1)} custom-call(f32[2,2560,128]{2,1,0:T(8,128)} %get-tuple-element.27.grads), custom_call_target="tpu_custom_call" | custom-call | flops 40642560 | bytes 3317760 | tf_op jit(solution)/shard_map/pallas_call | solution.py:445
  85.5 9.2 %all-to-all-done.3 = bf16[32,24,256]{2,1,0:T(8,128)(2,1)S(1)} async-done(((bf16[32,24,256]{2,1,0:T(8,128)(2,1)}), bf16[32,24,256]{2,1,0:T(8,128)(2,1)S(1)}, u32[]{:S(2)}, u32[]{:S(2)}) %all-to-all-start.3) | async-done | bytes 393248 | tf_op jit(solution)/shard_map/all_to_all | solution.py:458
  94.8 2.8 %all-to-all-start.4 = ((bf16[32,40,256]{2,1,0:T(8,128)(2,1)}), bf16[32,40,256]{2,1,0:T(8,128)(2,1)S(1)}, u32[]{:S(2)}, u32[]{:S(2)}) async-start(bf16[32,40,256]{2,1,0:T(8,128)(2,1)} %bitcast.31), calls=%async_computation.4 | async-start | bytes 1310720 | tf_op jit(solution)/shard_map/all_to_all | solution.py:458
  97.6 1.5 %collective-permute-start.1 = (bf16[3,48,1440]{2,1,0:T(8,128)(2,1)S(1)}, bf16[3,48,1440]{2,1,0:T(8,128)(2,1)S(1)}, u32[]{:S(2)}, u32[]{:S(2)}) collective-permute-start(bf16[3,48,1440]{2,1,0:T(8,128)(2,1)S(1)} %copy-done.6), channel_id=1, source_target_pairs={{0,1},{1,0},{2,3},{3,2},{4,5},{5,4},{6,7},{7,6},{8,9},{9,8},{10,11... | collective-permute-start | bytes 1244168 | tf_op jit(solution)/shard_map/ppermute | solution.py:41
  99.1 3.4 %collective-permute-start.2 = (bf16[3,48,1440]{2,1,0:T(8,128)(2,1)S(1)}, bf16[3,48,1440]{2,1,0:T(8,128)(2,1)S(1)}, u32[]{:S(2)}, u32[]{:S(2)}) collective-permute-start(bf16[3,48,1440]{2,1,0:T(8,128)(2,1)S(1)} %copy-done.7), channel_id=1, source_target_pairs={{1,2},{2,1},{3,4},{4,3},{5,6},{6,5},{7,0},{0,7},{9,10},{10,9},{11,... | collective-permute-start | bytes 1244168 | tf_op jit(solution)/shard_map/ppermute | solution.py:41
  102.6 1.9 %shard_map.99.taps = bf16[49,48,128]{2,1,0:T(8,128)(2,1)} custom-call(f32[7,7,24]{2,1,0:T(8,128)} %bitcast.42), custom_call_target="tpu_custom_call" | custom-call | flops 5080320 | bytes 3317760 | tf_op jit(solution)/shard_map/pallas_call | solution.py:445
  104.4 21.7 %collective-permute-done.1.near = bf16[3,48,1440]{2,1,0:T(8,128)(2,1)S(1)} collective-permute-done((bf16[3,48,1440]{2,1,0:T(8,128)(2,1)S(1)}, bf16[3,48,1440]{2,1,0:T(8,128)(2,1)S(1)}, u32[]{:S(2)}, u32[]{:S(2)}) %collective-permute-start.1) | collective-permute-done | bytes 414752 | tf_op jit(solution)/shard_map/ppermute | solution.py:41
  127.1 9.9 %shard_map.100 = bf16[2,6,24,1440]{3,2,1,0:T(8,128)(2,1)} custom-call(s32[2]{0:T(128)} %pad_add_fusion.flags, bf16[4,8,24,256]{3,2,1,0:T(8,128)(2,1)} %bitcast.34, bf16[3,48,1440]{2,1,0:T(8,128)(2,1)} %copy-done.8, bf16[3,48,1440]{2,1,0:T(8,128)(2,1)} %copy-done.9, bf16[3,48,1440]{2,1,0:T(8,128)(2,1)} %get-tuple-element.25.inner, ...), custom_call_target="tpu_custom_call" | custom-call | flops 40642560 | bytes 3317760 | tf_op jit(solution)/shard_map/pallas_call | solution.py:445
  137.8 3.7 %shard_map.102 = f32[2,24,20,2,160]{4,3,2,1,0:T(2,128)} custom-call(bf16[4,8,40,256]{3,2,1,0:T(8,128)(2,1)} %bitcast.30), custom_call_target="tpu_custom_call" | custom-call | flops 40642560 | bytes 3317760 | tf_op jit(solution)/shard_map/pallas_call | solution.py:445
  (34 shorter events, 7.8 us)
Async XLA Ops:
  0.6 6.6 %copy-start = (bf16[2,24,6,1440]{3,1,2,0:T(8,128)(2,1)S(1)}, bf16[2,24,6,1440]{3,1,2,0:T(8,128)(2,1)}, u32[]{:S(2)}) copy-start(bf16[2,24,6,1440]{3,1,2,0:T(8,128)(2,1)} %param.8) | copy-start | bytes 2488324
  1.9 11.2 %copy-start.5 = (bf16[6,160,160]{2,1,0:T(8,128)(2,1)S(1)}, bf16[6,160,160]{2,1,0:T(8,128)(2,1)}, u32[]{:S(2)}) copy-start(bf16[6,160,160]{2,1,0:T(8,128)(2,1)} %param.11) | copy-start | bytes 921604
  2.9 26.4 %all-to-all-start = ((bf16[2,2,3,24,1440]{4,3,2,1,0:T(8,128)(2,1)}), bf16[2,2,3,24,1440]{4,3,2,1,0:T(8,128)(2,1)S(1)}, u32[]{:S(2)}, u32[]{:S(2)}) async-start(bf16[2,2,3,24,1440]{4,3,2,1,0:T(8,128)(2,1)} %pad_maximum_fusion), calls=%async_computation | async-start | bytes 1769472 | tf_op jit(solution)/shard_map/all_to_all | solution.py:424
  7.2 28.5 %collective-permute-start = (bf16[2,3,24,1440]{3,2,1,0:T(8,128)(2,1)S(1)}, bf16[2,3,24,1440]{3,2,1,0:T(8,128)(2,1)S(1)}, u32[]{:S(2)}, u32[]{:S(2)}) collective-permute-start(bf16[2,3,24,1440]{3,2,1,0:T(8,128)(2,1)S(1)} %dynamic-slice_bitcast_fusion), channel_id=1, source_target_pairs={{1,2},{2,1},{3,4},{4,3},{5,6},{6,5},{7,0},{0,7},{9,10},{10,9},{11,... | collective-permute-start | bytes 1244168 | tf_op jit(solution)/shard_map/ppermute | solution.py:41
  29.3 0.9 copy-start.1
  35.7 0.8 copy-start.10
  42.1 13.4 %all-to-all-start.1 = ((bf16[32,24,128]{2,1,0:T(8,128)(2,1)}), bf16[32,24,128]{2,1,0:T(8,128)(2,1)S(1)}, u32[]{:S(2)}, u32[]{:S(2)}) async-start(bf16[32,24,128]{2,1,0:T(8,128)(2,1)} %bitcast.40), calls=%async_computation.1 | async-start | bytes 393216 | tf_op jit(solution)/shard_map/all_to_all | solution.py:458
  55.5 15.7 %copy-start.4 = (bf16[32,24,128]{2,1,0:T(8,128)(2,1)}, bf16[32,24,128]{2,1,0:T(8,128)(2,1)S(1)}, u32[]{:S(2)}) copy-start(bf16[32,24,128]{2,1,0:T(8,128)(2,1)S(1)} %all-to-all-done.1) | copy-start | bytes 589828
  55.5 14.2 %all-to-all-start.2 = ((bf16[8,150,128]{2,1,0:T(8,128)(2,1)}), bf16[8,150,128]{2,1,0:T(8,128)(2,1)S(1)}, u32[]{:S(2)}, u32[]{:S(2)}) async-start(bf16[8,150,128]{2,1,0:T(8,128)(2,1)} %copy.15), calls=%async_computation.2 | async-start | bytes 622592 | tf_op jit(solution)/shard_map/all_to_all | solution.py:499
  77.7 19.9 %copy-start.6 = (bf16[3,48,1440]{2,1,0:T(8,128)(2,1)S(1)}, bf16[3,48,1440]{2,1,0:T(8,128)(2,1)}, u32[]{:S(2)}) copy-start(bf16[3,48,1440]{2,1,0:T(8,128)(2,1)} %get-tuple-element.25.inner) | copy-start | bytes 1244164
  77.7 21.4 %copy-start.7 = (bf16[3,48,1440]{2,1,0:T(8,128)(2,1)S(1)}, bf16[3,48,1440]{2,1,0:T(8,128)(2,1)}, u32[]{:S(2)}) copy-start(bf16[3,48,1440]{2,1,0:T(8,128)(2,1)} %get-tuple-element.26.outer) | copy-start | bytes 1244164
  77.7 17.1 %all-to-all-start.3 = ((bf16[32,24,256]{2,1,0:T(8,128)(2,1)}), bf16[32,24,256]{2,1,0:T(8,128)(2,1)S(1)}, u32[]{:S(2)}, u32[]{:S(2)}) async-start(bf16[32,24,256]{2,1,0:T(8,128)(2,1)} %bitcast.39), calls=%async_computation.3 | async-start | bytes 786432 | tf_op jit(solution)/shard_map/all_to_all | solution.py:458
  94.8 31.4 %copy-start.3 = (bf16[32,24,256]{2,1,0:T(8,128)(2,1)}, bf16[32,24,256]{2,1,0:T(8,128)(2,1)S(1)}, u32[]{:S(2)}) copy-start(bf16[32,24,256]{2,1,0:T(8,128)(2,1)S(1)} %all-to-all-done.3) | copy-start | bytes 1179652
  94.8 42.2 %all-to-all-start.4 = ((bf16[32,40,256]{2,1,0:T(8,128)(2,1)}), bf16[32,40,256]{2,1,0:T(8,128)(2,1)S(1)}, u32[]{:S(2)}, u32[]{:S(2)}) async-start(bf16[32,40,256]{2,1,0:T(8,128)(2,1)} %bitcast.31), calls=%async_computation.4 | async-start | bytes 1310720 | tf_op jit(solution)/shard_map/all_to_all | solution.py:458
  97.6 28.6 %collective-permute-start.1 = (bf16[3,48,1440]{2,1,0:T(8,128)(2,1)S(1)}, bf16[3,48,1440]{2,1,0:T(8,128)(2,1)S(1)}, u32[]{:S(2)}, u32[]{:S(2)}) collective-permute-start(bf16[3,48,1440]{2,1,0:T(8,128)(2,1)S(1)} %copy-done.6), channel_id=1, source_target_pairs={{0,1},{1,0},{2,3},{3,2},{4,5},{5,4},{6,7},{7,6},{8,9},{9,8},{10,11... | collective-permute-start | bytes 1244168 | tf_op jit(solution)/shard_map/ppermute | solution.py:41
  99.1 27.0 %collective-permute-start.2 = (bf16[3,48,1440]{2,1,0:T(8,128)(2,1)S(1)}, bf16[3,48,1440]{2,1,0:T(8,128)(2,1)S(1)}, u32[]{:S(2)}, u32[]{:S(2)}) collective-permute-start(bf16[3,48,1440]{2,1,0:T(8,128)(2,1)S(1)} %copy-done.7), channel_id=1, source_target_pairs={{1,2},{2,1},{3,4},{4,3},{5,6},{6,5},{7,0},{0,7},{9,10},{10,9},{11,... | collective-permute-start | bytes 1244168 | tf_op jit(solution)/shard_map/ppermute | solution.py:41
  126.1 0.8 copy-start.8
  126.1 0.9 copy-start.9
  137.0 0.8 copy-start.2

commit v9 on v7

--- a/solution.py
+++ b/solution.py
@@ -30,13 +30,13 @@
     return table.reshape(nlon, 2 * span).astype(jnp.bfloat16)
 
 
-def partner(edge, pair):
+def partners(inner, outer):
     count = lax.axis_size("lat")
-    if pair:
-        steps = [(i, i ^ 1) for i in range(count)]
-    else:
-        steps = [(i, (i + (1 if i % 2 else -1)) % count) for i in range(count)]
-    return lax.ppermute(edge, "lat", steps)
+    near = [(i, i ^ 1) for i in range(count)]
+    far = [(i, (i + (1 if i % 2 else -1)) % count) for i in range(count)]
+    one = lax.ppermute(inner, "lat", near)
+    other = lax.ppermute(outer, "lat", far)
+    return one, other
 
 
 def place():
@@ -417,8 +417,10 @@
     flags = place()
     own = fields.transpose(0, 2, 1, 3)
     odd = lat_at % 2
-    inner = lax.dynamic_slice_in_dim(own, (1 - odd) * (rows - halo), halo, 1)
-    near = partner(inner, True)
+    near, far = partners(
+        lax.dynamic_slice_in_dim(own, (1 - odd) * (rows - halo), halo, 1),
+        lax.dynamic_slice_in_dim(own, odd * (rows - halo), halo, 1),
+    )
 
     pick = np.zeros((2, members, ens_parts, height, chans), np.float32)
     for r in range(2):
@@ -474,9 +476,6 @@
     slab = legendre.reshape(rows, groups, share * degrees).transpose(1, 0, 2)
     line = math.gcd(rows * share * degrees, 128)
     slab = slab.reshape(groups, rows * share * degrees // line, line)
-    late, partial = lax.optimization_barrier((own, partial))
-    outer = lax.dynamic_slice_in_dim(late, odd * (rows - halo), halo, 1)
-    far = partner(outer, False)
 
     def chunk(lines):
         return jax.ShapeDtypeStruct((ens_parts, groups, height, up(lines * share, 128)), BF16)
@@ -511,7 +510,7 @@
         mixed,
     )
     got = swap(sent)
-    near, far = partner(inner, True), partner(outer, False)
+    near, far = partners(inner, outer)
     back, grads = call(
         functools.partial(score_kernel, members, used, rows, halo),
         (

time: 137 us -> 137 us (level)
    unnamed x21 -> x19, local copies, waits for them, and re-layouts: 3.86 us -> 3.86 us
where the time goes in v9:
time: 137 us; the launch traced here: 136 us
  waiting for transfers between devices  53.1 us (39%)
  Pallas kernels  43.6 us (32%)
  starting transfers between devices  27.1 us (20%)
  local copies, waits for them, and re-layouts  10.7 us (8%)
    pallas_call x8, Pallas kernels, call(): pl.pallas_call(body, out_shape=outs, in_specs=specs, scratch_shapes=scrat...  43.6 us
    ppermute x2, waiting for transfers between devices, partners(): other = lax.ppermute(outer, 'lat', far)  33.2 us
    all_to_all x3, waiting for transfers between devices, swap(): lax.all_to_all(flat, ('ens', 'lat'), split_axis=0, concat_axis=0, tiled=T...  14.2 us
    ppermute x2, starting transfers between devices, partners(): other = lax.ppermute(outer, 'lat', far)  9.17 us
    all_to_all x3, starting transfers between devices, swap(): lax.all_to_all(flat, ('ens', 'lat'), split_axis=0, concat_axis=0, tiled=T...  8.85 us
    all_to_all x1, starting transfers between devices, local(): slab = lax.all_to_all(slab, 'lat', split_axis=0, concat_axis=0, tiled=True)  6.05 us
    ppermute x2, waiting for transfers between devices, partners(): one = lax.ppermute(inner, 'lat', near)  5.74 us
    unnamed x19, local copies, waits for them, and re-layouts  3.86 us
  transfers between devices with their start and end apart: 8, of which 6 were waited for; matrix products, arithmetic and copies ran while one was open for 4% of the time, Pallas kernels for 21%

profile of v9, /device:TPU:0, one launch (start us, length us, event | category | flops | bytes accessed | tf_op | source)
XLA Modules:
  0.0 135.9 jit_solution(11441264505381041530)
XLA Ops:
  0.7 1.2 dynamic-slice_bitcast_fusion
  1.9 3.1 %collective-permute-start.1 = (bf16[2,3,24,1440]{3,2,1,0:T(8,128)(2,1)S(1)}, bf16[2,3,24,1440]{3,2,1,0:T(8,128)(2,1)S(1)}, u32[]{:S(2)}, u32[]{:S(2)}) collective-permute-start(bf16[2,3,24,1440]{3,2,1,0:T(8,128)(2,1)S(1)} %get-tuple-element.24), channel_id=1, source_target_pairs={{0,1},{1,0},{2,3},{3,2},{4,5},{5,4},{6,7},{7,6},{8,9},{9,8},{10,11... | collective-permute-start | bytes 1244168 | tf_op jit(solution)/shard_map/ppermute | solution.py:37
  4.9 1.6 %reshape.37 = bf16[6,8,3200]{2,1,0:T(8,128)(2,1)S(1)} reshape(bf16[6,160,160]{2,1,0:T(8,128)(2,1)} %param.11) | data formatting | bytes 614400 | tf_op jit(solution)/shard_map/reshape | solution.py:476
  6.6 6.5 %shard_map.95 = (f32[6,48,1440]{2,1,0:T(8,128)}, bf16[49,48,128]{2,1,0:T(8,128)(2,1)}, bf16[2,96,48]{2,1,0:T(8,128)(2,1)}) custom-call(bf16[2,6,24,1440]{3,2,1,0:T(8,128)(2,1)} %bitcast.26, f32[7,7,24]{2,1,0:T(8,128)} %bitcast.38, bf16[24,24]{1,0:T(8,128)(2,1)} %weight.1, bf16[2,2,96,24]{3,2,1,0:T(8,128)(2,1)} %constant.44.clone.pick), custom_call_target="tpu_custom_call" | custom-call | flops 40642560 | bytes 3317760 | tf_op jit(solution)/shard_map/pallas_call | solution.py:443
  13.7 1.4 %collective-permute-done.1.edge = bf16[2,3,24,1440]{3,2,1,0:T(8,128)(2,1)S(1)} collective-permute-done((bf16[2,3,24,1440]{3,2,1,0:T(8,128)(2,1)S(1)}, bf16[2,3,24,1440]{3,2,1,0:T(8,128)(2,1)S(1)}, u32[]{:S(2)}, u32[]{:S(2)}) %collective-permute-start.1) | collective-permute-done | bytes 414752 | tf_op jit(solution)/shard_map/ppermute | solution.py:37
  15.9 5.4 %shard_map.96 = (f32[3,96,256]{2,1,0:T(8,128)}, bf16[3,48,1440]{2,1,0:T(8,128)(2,1)}) custom-call(s32[2]{0:T(128)} %pad_add_fusion.flags, bf16[2,3,24,1440]{3,2,1,0:T(8,128)(2,1)} %copy-done.7, f32[6,48,1440]{2,1,0:T(8,128)} %get-tuple-element.13.partial, bf16[49,48,128]{2,1,0:T(8,128)(2,1)} %get-tuple-element.14.taps, ...), custom_call_target="tpu_custom_call" | custom-call | flops 20321280 | bytes 3317760 | tf_op jit(solution)/shard_map/pallas_call | solution.py:443
  22.0 6.1 %all-to-all-start.1 = ((bf16[8,150,128]{2,1,0:T(8,128)(2,1)}), bf16[8,150,128]{2,1,0:T(8,128)(2,1)S(1)}, u32[]{:S(2)}, u32[]{:S(2)}) async-start(bf16[8,150,128]{2,1,0:T(8,128)(2,1)} %copy.15), calls=%async_computation.1 | async-start | bytes 622592 | tf_op jit(solution)/shard_map/all_to_all | solution.py:497
  28.0 4.7 %collective-permute-start = (bf16[2,3,24,1440]{3,2,1,0:T(8,128)(2,1)S(1)}, bf16[2,3,24,1440]{3,2,1,0:T(8,128)(2,1)S(1)}, u32[]{:S(2)}, u32[]{:S(2)}) collective-permute-start(bf16[2,3,24,1440]{3,2,1,0:T(8,128)(2,1)S(1)} %get-tuple-element.25), channel_id=1, source_target_pairs={{0,7},{1,2},{2,1},{3,4},{4,3},{5,6},{6,5},{7,0},{8,15},{9,10},{10,... | collective-permute-start | bytes 1244168 | tf_op jit(solution)/shard_map/ppermute | solution.py:38
  32.7 14.0 %collective-permute-done.edge = bf16[2,3,24,1440]{3,2,1,0:T(8,128)(2,1)S(1)} collective-permute-done((bf16[2,3,24,1440]{3,2,1,0:T(8,128)(2,1)S(1)}, bf16[2,3,24,1440]{3,2,1,0:T(8,128)(2,1)S(1)}, u32[]{:S(2)}, u32[]{:S(2)}) %collective-permute-start) | collective-permute-done | bytes 414752 | tf_op jit(solution)/shard_map/ppermute | solution.py:38
  47.5 5.6 %shard_map.97 = (bf16[4,8,24,128]{3,2,1,0:T(8,128)(2,1)}, bf16[3,48,1440]{2,1,0:T(8,128)(2,1)}) custom-call(s32[2]{0:T(128)} %pad_add_fusion.flags, bf16[2,3,24,1440]{3,2,1,0:T(8,128)(2,1)} %copy-done.8, f32[6,48,1440]{2,1,0:T(8,128)} %get-tuple-element.13.partial, bf16[49,48,128]{2,1,0:T(8,128)(2,1)} %get-tuple-element.14.taps, ...), custom_call_target="tpu_custom_call" | custom-call | flops 20321280 | bytes 3317760 | tf_op jit(solution)/shard_map/pallas_call | solution.py:443
  53.1 2.7 %all-to-all-start = ((bf16[32,24,128]{2,1,0:T(8,128)(2,1)}), bf16[32,24,128]{2,1,0:T(8,128)(2,1)S(1)}, u32[]{:S(2)}, u32[]{:S(2)}) async-start(bf16[32,24,128]{2,1,0:T(8,128)(2,1)} %bitcast.37), calls=%async_computation | async-start | bytes 393216 | tf_op jit(solution)/shard_map/all_to_all | solution.py:456
  55.8 1.0 constant_dynamic-slice_fusion
  59.1 4.9 %all-to-all-done = bf16[32,24,128]{2,1,0:T(8,128)(2,1)S(1)} async-done(((bf16[32,24,128]{2,1,0:T(8,128)(2,1)}), bf16[32,24,128]{2,1,0:T(8,128)(2,1)S(1)}, u32[]{:S(2)}, u32[]{:S(2)}) %all-to-all-start) | async-done | bytes 196640 | tf_op jit(solution)/shard_map/all_to_all | solution.py:456
  64.7 6.5 %shard_map.98 = (bf16[4,8,24,256]{3,2,1,0:T(8,128)(2,1)}, f32[2,2560,128]{2,1,0:T(8,128)}) custom-call(bf16[4,8,24,128]{3,2,1,0:T(8,128)(2,1)} %bitcast.34, bf16[20,48,160]{2,1,0:T(8,128)(2,1)} %bitcast.30, bf16[20,16,160]{2,1,0:T(8,128)(2,1)} %pad.4.target, s32[1,160]{1,0:T(1,128)} %bitcast.40), custom_call_target="tpu_custom_call" | custom-call | flops 40642560 | bytes 3317760 | tf_op jit(solution)/shard_map/pallas_call | solution.py:443
  71.2 3.3 %all-to-all-start.2 = ((bf16[32,24,256]{2,1,0:T(8,128)(2,1)}), bf16[32,24,256]{2,1,0:T(8,128)(2,1)S(1)}, u32[]{:S(2)}, u32[]{:S(2)}) async-start(bf16[32,24,256]{2,1,0:T(8,128)(2,1)} %bitcast.36), calls=%async_computation.2 | async-start | bytes 786432 | tf_op jit(solution)/shard_map/all_to_all | solution.py:456
  74.6 4.2 %shard_map.101 = bf16[4,8,40,256]{3,2,1,0:T(8,128)(2,1)} custom-call(f32[2,2560,128]{2,1,0:T(8,128)} %get-tuple-element.23.grads), custom_call_target="tpu_custom_call" | custom-call | flops 40642560 | bytes 3317760 | tf_op jit(solution)/shard_map/pallas_call | solution.py:443
  78.7 9.2 %all-to-all-done.2 = bf16[32,24,256]{2,1,0:T(8,128)(2,1)S(1)} async-done(((bf16[32,24,256]{2,1,0:T(8,128)(2,1)}), bf16[32,24,256]{2,1,0:T(8,128)(2,1)S(1)}, u32[]{:S(2)}, u32[]{:S(2)}) %all-to-all-start.2) | async-done | bytes 393248 | tf_op jit(solution)/shard_map/all_to_all | solution.py:456
  88.0 2.8 %all-to-all-start.3 = ((bf16[32,40,256]{2,1,0:T(8,128)(2,1)}), bf16[32,40,256]{2,1,0:T(8,128)(2,1)S(1)}, u32[]{:S(2)}, u32[]{:S(2)}) async-start(bf16[32,40,256]{2,1,0:T(8,128)(2,1)} %bitcast.28), calls=%async_computation.3 | async-start | bytes 1310720 | tf_op jit(solution)/shard_map/all_to_all | solution.py:456
  90.8 4.4 %collective-permute-start.3 = (bf16[3,48,1440]{2,1,0:T(8,128)(2,1)S(1)}, bf16[3,48,1440]{2,1,0:T(8,128)(2,1)S(1)}, u32[]{:S(2)}, u32[]{:S(2)}) collective-permute-start(bf16[3,48,1440]{2,1,0:T(8,128)(2,1)S(1)} %copy-done.4), channel_id=1, source_target_pairs={{0,7},{1,2},{2,1},{3,4},{4,3},{5,6},{6,5},{7,0},{8,15},{9,10},{10,... | collective-permute-start | bytes 1244168 | tf_op jit(solution)/shard_map/ppermute | solution.py:38
  95.3 1.9 %shard_map.99.taps = bf16[49,48,128]{2,1,0:T(8,128)(2,1)} custom-call(f32[7,7,24]{2,1,0:T(8,128)} %bitcast.39), custom_call_target="tpu_custom_call" | custom-call | flops 5080320 | bytes 3317760 | tf_op jit(solution)/shard_map/pallas_call | solution.py:443
  97.1 19.2 %collective-permute-done.3.far = bf16[3,48,1440]{2,1,0:T(8,128)(2,1)S(1)} collective-permute-done((bf16[3,48,1440]{2,1,0:T(8,128)(2,1)S(1)}, bf16[3,48,1440]{2,1,0:T(8,128)(2,1)S(1)}, u32[]{:S(2)}, u32[]{:S(2)}) %collective-permute-start.3) | collective-permute-done | bytes 414752 | tf_op jit(solution)/shard_map/ppermute | solution.py:38
  116.4 4.4 %collective-permute-done.2.near = bf16[3,48,1440]{2,1,0:T(8,128)(2,1)S(1)} collective-permute-done((bf16[3,48,1440]{2,1,0:T(8,128)(2,1)S(1)}, bf16[3,48,1440]{2,1,0:T(8,128)(2,1)S(1)}, u32[]{:S(2)}, u32[]{:S(2)}) %collective-permute-start.2) | collective-permute-done | bytes 414752 | tf_op jit(solution)/shard_map/ppermute | solution.py:37
  121.5 9.9 %shard_map.100 = bf16[2,6,24,1440]{3,2,1,0:T(8,128)(2,1)} custom-call(s32[2]{0:T(128)} %pad_add_fusion.flags, bf16[4,8,24,256]{3,2,1,0:T(8,128)(2,1)} %bitcast.31, bf16[3,48,1440]{2,1,0:T(8,128)(2,1)} %copy-done.6, bf16[3,48,1440]{2,1,0:T(8,128)(2,1)} %copy-done.5, bf16[3,48,1440]{2,1,0:T(8,128)(2,1)} %get-tuple-element.21.inner, ...), custom_call_target="tpu_custom_call" | custom-call | flops 40642560 | bytes 3317760 | tf_op jit(solution)/shard_map/pallas_call | solution.py:443
  132.2 3.7 %shard_map.102 = f32[2,24,20,2,160]{4,3,2,1,0:T(2,128)} custom-call(bf16[4,8,40,256]{3,2,1,0:T(8,128)(2,1)} %bitcast.27), custom_call_target="tpu_custom_call" | custom-call | flops 40642560 | bytes 3317760 | tf_op jit(solution)/shard_map/pallas_call | solution.py:443
  (28 shorter events, 7.5 us)
Async XLA Ops:
  1.9 13.2 %collective-permute-start.1 = (bf16[2,3,24,1440]{3,2,1,0:T(8,128)(2,1)S(1)}, bf16[2,3,24,1440]{3,2,1,0:T(8,128)(2,1)S(1)}, u32[]{:S(2)}, u32[]{:S(2)}) collective-permute-start(bf16[2,3,24,1440]{3,2,1,0:T(8,128)(2,1)S(1)} %get-tuple-element.24), channel_id=1, source_target_pairs={{0,1},{1,0},{2,3},{3,2},{4,5},{5,4},{6,7},{7,6},{8,9},{9,8},{10,11... | collective-permute-start | bytes 1244168 | tf_op jit(solution)/shard_map/ppermute | solution.py:37
  15.1 0.8 copy-start.7
  22.0 31.1 %all-to-all-start.1 = ((bf16[8,150,128]{2,1,0:T(8,128)(2,1)}), bf16[8,150,128]{2,1,0:T(8,128)(2,1)S(1)}, u32[]{:S(2)}, u32[]{:S(2)}) async-start(bf16[8,150,128]{2,1,0:T(8,128)(2,1)} %copy.15), calls=%async_computation.1 | async-start | bytes 622592 | tf_op jit(solution)/shard_map/all_to_all | solution.py:497
  28.0 18.7 %collective-permute-start = (bf16[2,3,24,1440]{3,2,1,0:T(8,128)(2,1)S(1)}, bf16[2,3,24,1440]{3,2,1,0:T(8,128)(2,1)S(1)}, u32[]{:S(2)}, u32[]{:S(2)}) collective-permute-start(bf16[2,3,24,1440]{3,2,1,0:T(8,128)(2,1)S(1)} %get-tuple-element.25), channel_id=1, source_target_pairs={{0,7},{1,2},{2,1},{3,4},{4,3},{5,6},{6,5},{7,0},{8,15},{9,10},{10,... | collective-permute-start | bytes 1244168 | tf_op jit(solution)/shard_map/ppermute | solution.py:38
  46.7 0.8 copy-start.8
  53.1 11.0 %all-to-all-start = ((bf16[32,24,128]{2,1,0:T(8,128)(2,1)}), bf16[32,24,128]{2,1,0:T(8,128)(2,1)S(1)}, u32[]{:S(2)}, u32[]{:S(2)}) async-start(bf16[32,24,128]{2,1,0:T(8,128)(2,1)} %bitcast.37), calls=%async_computation | async-start | bytes 393216 | tf_op jit(solution)/shard_map/all_to_all | solution.py:456
  64.0 0.7 copy-start.2
  71.2 19.6 %copy-start.4 = (bf16[3,48,1440]{2,1,0:T(8,128)(2,1)S(1)}, bf16[3,48,1440]{2,1,0:T(8,128)(2,1)}, u32[]{:S(2)}) copy-start(bf16[3,48,1440]{2,1,0:T(8,128)(2,1)} %get-tuple-element.22.outer) | copy-start | bytes 1244164
  71.2 24.0 %copy-start.3 = (bf16[3,48,1440]{2,1,0:T(8,128)(2,1)S(1)}, bf16[3,48,1440]{2,1,0:T(8,128)(2,1)}, u32[]{:S(2)}) copy-start(bf16[3,48,1440]{2,1,0:T(8,128)(2,1)} %get-tuple-element.21.inner) | copy-start | bytes 1244164
  71.2 16.8 %all-to-all-start.2 = ((bf16[32,24,256]{2,1,0:T(8,128)(2,1)}), bf16[32,24,256]{2,1,0:T(8,128)(2,1)S(1)}, u32[]{:S(2)}, u32[]{:S(2)}) async-start(bf16[32,24,256]{2,1,0:T(8,128)(2,1)} %bitcast.36), calls=%async_computation.2 | async-start | bytes 786432 | tf_op jit(solution)/shard_map/all_to_all | solution.py:456
  88.0 32.7 %copy-start.1 = (bf16[32,24,256]{2,1,0:T(8,128)(2,1)}, bf16[32,24,256]{2,1,0:T(8,128)(2,1)S(1)}, u32[]{:S(2)}) copy-start(bf16[32,24,256]{2,1,0:T(8,128)(2,1)S(1)} %all-to-all-done.2) | copy-start | bytes 1179652
  88.0 43.4 %all-to-all-start.3 = ((bf16[32,40,256]{2,1,0:T(8,128)(2,1)}), bf16[32,40,256]{2,1,0:T(8,128)(2,1)S(1)}, u32[]{:S(2)}, u32[]{:S(2)}) async-start(bf16[32,40,256]{2,1,0:T(8,128)(2,1)} %bitcast.28), calls=%async_computation.3 | async-start | bytes 1310720 | tf_op jit(solution)/shard_map/all_to_all | solution.py:456
  90.8 25.6 %collective-permute-start.3 = (bf16[3,48,1440]{2,1,0:T(8,128)(2,1)S(1)}, bf16[3,48,1440]{2,1,0:T(8,128)(2,1)S(1)}, u32[]{:S(2)}, u32[]{:S(2)}) collective-permute-start(bf16[3,48,1440]{2,1,0:T(8,128)(2,1)S(1)} %copy-done.4), channel_id=1, source_target_pairs={{0,7},{1,2},{2,1},{3,4},{4,3},{5,6},{6,5},{7,0},{8,15},{9,10},{10,... | collective-permute-start | bytes 1244168 | tf_op jit(solution)/shard_map/ppermute | solution.py:38
  95.2 25.5 %collective-permute-start.2 = (bf16[3,48,1440]{2,1,0:T(8,128)(2,1)S(1)}, bf16[3,48,1440]{2,1,0:T(8,128)(2,1)S(1)}, u32[]{:S(2)}, u32[]{:S(2)}) collective-permute-start(bf16[3,48,1440]{2,1,0:T(8,128)(2,1)S(1)} %copy-done.3), channel_id=1, source_target_pairs={{0,1},{1,0},{2,3},{3,2},{4,5},{5,4},{6,7},{7,6},{8,9},{9,8},{10,11... | collective-permute-start | bytes 1244168 | tf_op jit(solution)/shard_map/ppermute | solution.py:37
  116.4 4.4 %copy-start.5 = (bf16[3,48,1440]{2,1,0:T(8,128)(2,1)}, bf16[3,48,1440]{2,1,0:T(8,128)(2,1)S(1)}, u32[]{:S(2)}) copy-start(bf16[3,48,1440]{2,1,0:T(8,128)(2,1)S(1)} %collective-permute-done.3.far) | copy-start | bytes 1244164
  120.7 0.8 copy-start.6
  131.4 0.9 copy-start

commit v10 on v9

--- a/solution.py
+++ b/solution.py
@@ -430,7 +430,7 @@
                 pick[r, b, o // chan_share, at, o] = 1.0
     pick = jnp.asarray(pick.reshape(2, members, ens_parts * height, chans).astype(jnp.bfloat16))
 
-    vmem = pltpu.CompilerParams(vmem_limit_bytes=60 * 1024 * 1024)
+    vmem = pltpu.CompilerParams(vmem_limit_bytes=28 * 1024 * 1024)
     scalars = pl.BlockSpec(memory_space=pltpu.SMEM)
     whole = pl.BlockSpec(memory_space=pltpu.VMEM)
     grid_shape = (members, rows, chans, nlon)
@@ -510,7 +510,8 @@
         mixed,
     )
     got = swap(sent)
-    near, far = partners(inner, outer)
+    got, held = lax.optimization_barrier((got, outer))
+    near, far = partners(inner, held)
     back, grads = call(
         functools.partial(score_kernel, members, used, rows, halo),
         (

time: 137 us -> 133 us (0.971)
  Pallas kernels: 43.6 us -> 29.6 us
  waiting for transfers between devices: 53.1 us -> 59 us
  local copies, waits for them, and re-layouts: 10.7 us -> 15 us
    ppermute x2, waiting for transfers between devices: 33.2 us -> 0.01 us  [partners(): other = lax.ppermute(outer, 'lat', far)]
    ppermute x2, waiting for transfers between devices: 5.74 us -> 32.7 us  [partners(): one = lax.ppermute(inner, 'lat', near)]
    pallas_call x8, Pallas kernels: 43.6 us -> 29.6 us  [call(): pl.pallas_call(body, out_shape=outs, in_specs=specs, scratch_shapes=scrat...]
    all_to_all x1, waiting for transfers between devices: 0.01 us -> 9.64 us  [local(): slab = lax.all_to_all(slab, 'lat', split_axis=0, concat_axis=0, tiled=True)]
    all_to_all x3, starting transfers between devices: 8.85 us -> 12.5 us  [swap(): lax.all_to_all(flat, ('ens', 'lat'), split_axis=0, concat_axis=0, tiled=T...]
    unnamed x19 -> x27, local copies, waits for them, and re-layouts: 3.86 us -> 6.84 us
    all_to_all x3, waiting for transfers between devices: 14.2 us -> 16.6 us  [swap(): lax.all_to_all(flat, ('ens', 'lat'), split_axis=0, concat_axis=0, tiled=T...]
    ppermute x2, starting transfers between devices: 9.17 us -> 6.97 us  [partners(): other = lax.ppermute(outer, 'lat', far)]
  transfers between devices with their start and end apart: 8 -> 8, of which waited for: 6 -> 5; matrix products, arithmetic and copies ran while one was open for 4% -> 3% of each run, Pallas kernels for 21% -> 14%
where the time goes in v10:
time: 133 us
  waiting for transfers between devices  59 us (44%)
  Pallas kernels  29.6 us (22%)
  starting transfers between devices  28.2 us (21%)
  local copies, waits for them, and re-layouts  15 us (11%)
    ppermute x2, waiting for transfers between devices, partners(): one = lax.ppermute(inner, 'lat', near)  32.7 us
    pallas_call x8, Pallas kernels, call(): pl.pallas_call(body, out_shape=outs, in_specs=specs, scratch_shapes=scrat...  29.6 us
    all_to_all x3, waiting for transfers between devices, swap(): lax.all_to_all(flat, ('ens', 'lat'), split_axis=0, concat_axis=0, tiled=T...  16.6 us
    all_to_all x3, starting transfers between devices, swap(): lax.all_to_all(flat, ('ens', 'lat'), split_axis=0, concat_axis=0, tiled=T...  12.5 us
    all_to_all x1, waiting for transfers between devices, local(): slab = lax.all_to_all(slab, 'lat', split_axis=0, concat_axis=0, tiled=True)  9.64 us
    ppermute x2, starting transfers between devices, partners(): other = lax.ppermute(outer, 'lat', far)  6.97 us
    unnamed x27, local copies, waits for them, and re-layouts  6.84 us
    ppermute x2, starting transfers between devices, partners(): one = lax.ppermute(inner, 'lat', near)  4.54 us
  transfers between devices with their start and end apart: 8, of which 5 were waited for; matrix products, arithmetic and copies ran while one was open for 3% of the time, Pallas kernels for 14%

profile of v10, /device:TPU:0, one launch (start us, length us, event | category | flops | bytes accessed | tf_op | source)
XLA Modules:
  0.0 132.7 jit_solution(14295922041930214942)
XLA Ops:
  0.7 2.3 %dynamic-slice_bitcast_fusion = (bf16[2,3,24,1440]{3,2,1,0:T(8,128)(2,1)}, bf16[2,3,24,1440]{3,2,1,0:T(8,128)(2,1)}) fusion(bf16[2,24,6,1440]{3,1,2,0:T(8,128)(2,1)} %param.8, s32[]{:T(128)S(6)} %select_n.23, s32[]{:T(128)S(6)} %select_n.22), kind=kLoop, calls=%fused_computation.1 | loop fusion | bytes 1658888 | tf_op jit(solution)/shard_map/dynamic_slice | solution.py:421
  3.0 3.0 %collective-permute-start.1 = (bf16[2,3,24,1440]{3,2,1,0:T(8,128)(2,1)}, bf16[2,3,24,1440]{3,2,1,0:T(8,128)(2,1)S(1)}, u32[]{:S(2)}, u32[]{:S(2)}) collective-permute-start(bf16[2,3,24,1440]{3,2,1,0:T(8,128)(2,1)} %get-tuple-element.28), channel_id=1, source_target_pairs={{0,1},{1,0},{2,3},{3,2},{4,5},{5,4},{6,7},{7,6},{8,9},{9,8},{10,11... | collective-permute-start | bytes 1244168 | tf_op jit(solution)/shard_map/ppermute | solution.py:37
  6.0 3.5 %collective-permute-start = (bf16[2,3,24,1440]{3,2,1,0:T(8,128)(2,1)}, bf16[2,3,24,1440]{3,2,1,0:T(8,128)(2,1)S(1)}, u32[]{:S(2)}, u32[]{:S(2)}) collective-permute-start(bf16[2,3,24,1440]{3,2,1,0:T(8,128)(2,1)} %get-tuple-element.29), channel_id=1, source_target_pairs={{0,7},{1,2},{2,1},{3,4},{4,3},{5,6},{6,5},{7,0},{8,15},{9,10},{10,... | collective-permute-start | bytes 1244168 | tf_op jit(solution)/shard_map/ppermute | solution.py:38
  9.5 2.4 %reshape.37 = bf16[6,8,3200]{2,1,0:T(8,128)(2,1)} reshape(bf16[6,160,160]{2,1,0:T(8,128)(2,1)} %param.11) | data formatting | bytes 614400 | tf_op jit(solution)/shard_map/reshape | solution.py:476
  11.9 4.4 %shard_map.95 = (f32[6,48,1440]{2,1,0:T(8,128)S(1)}, bf16[49,48,128]{2,1,0:T(8,128)(2,1)S(1)}, bf16[2,96,48]{2,1,0:T(8,128)(2,1)S(1)}) custom-call(bf16[2,6,24,1440]{3,2,1,0:T(8,128)(2,1)S(1)} %bitcast.26, f32[7,7,24]{2,1,0:T(8,128)S(1)} %bitcast.31, bf16[24,24]{1,0:T(8,128)(2,1)S(1)} %copy-done.10, bf16[2,2,96,24]{3,2,1,0:T(8,128)(2,1)S(1)} %copy-done.9), custom_call_target="tpu_custom_call" | custom-call | flops 40642560 | bytes 3317760 | tf_op jit(solution)/shard_map/pallas_call | solution.py:443
  16.4 9.4 %collective-permute-done.1.edge = bf16[2,3,24,1440]{3,2,1,0:T(8,128)(2,1)S(1)} collective-permute-done((bf16[2,3,24,1440]{3,2,1,0:T(8,128)(2,1)}, bf16[2,3,24,1440]{3,2,1,0:T(8,128)(2,1)S(1)}, u32[]{:S(2)}, u32[]{:S(2)}) %collective-permute-start.1) | collective-permute-done | bytes 414752 | tf_op jit(solution)/shard_map/ppermute | solution.py:37
  27.6 3.0 %shard_map.96 = (f32[3,96,256]{2,1,0:T(8,128)S(1)}, bf16[3,48,1440]{2,1,0:T(8,128)(2,1)S(1)}) custom-call(s32[2]{0:T(128)S(1)} %pad_add_fusion.flags, bf16[2,3,24,1440]{3,2,1,0:T(8,128)(2,1)S(1)} %copy-done.7, f32[6,48,1440]{2,1,0:T(8,128)S(1)} %get-tuple-element.15.partial, bf16[49,48,128]{2,1,0:T(8,128)(2,1)S(1)} %get-tuple-element.16.taps, ...), custom_call_target="tpu_custom_call" | custom-call | flops 20321280 | bytes 3317760 | tf_op jit(solution)/shard_map/pallas_call | solution.py:443
  32.4 3.9 %shard_map.97 = (bf16[4,8,24,128]{3,2,1,0:T(8,128)(2,1)}, bf16[3,48,1440]{2,1,0:T(8,128)(2,1)S(1)}) custom-call(s32[2]{0:T(128)S(1)} %pad_add_fusion.flags, bf16[2,3,24,1440]{3,2,1,0:T(8,128)(2,1)S(1)} %copy-done.5, f32[6,48,1440]{2,1,0:T(8,128)S(1)} %get-tuple-element.15.partial, bf16[49,48,128]{2,1,0:T(8,128)(2,1)S(1)} %get-tuple-element.16.taps, ...), custom_call_target="tpu_custom_call" | custom-call | flops 20321280 | bytes 3317760 | tf_op jit(solution)/shard_map/pallas_call | solution.py:443
  36.3 6.1 %all-to-all-start = ((bf16[32,24,128]{2,1,0:T(8,128)(2,1)}), bf16[32,24,128]{2,1,0:T(8,128)(2,1)S(1)}, u32[]{:S(2)}, u32[]{:S(2)}) async-start(bf16[32,24,128]{2,1,0:T(8,128)(2,1)} %bitcast.8), calls=%async_computation | async-start | bytes 393216 | tf_op jit(solution)/shard_map/all_to_all | solution.py:456
  43.1 7.5 %all-to-all-done = bf16[32,24,128]{2,1,0:T(8,128)(2,1)S(1)} async-done(((bf16[32,24,128]{2,1,0:T(8,128)(2,1)}), bf16[32,24,128]{2,1,0:T(8,128)(2,1)S(1)}, u32[]{:S(2)}, u32[]{:S(2)}) %all-to-all-start) | async-done | bytes 196640 | tf_op jit(solution)/shard_map/all_to_all | solution.py:456
  50.6 4.2 %all-to-all-start.1 = ((bf16[8,150,128]{2,1,0:T(8,128)(2,1)}), bf16[8,150,128]{2,1,0:T(8,128)(2,1)}, u32[]{:S(2)}, u32[]{:S(2)}) async-start(bf16[8,150,128]{2,1,0:T(8,128)(2,1)} %copy.15), calls=%async_computation.1 | async-start | bytes 622592 | tf_op jit(solution)/shard_map/all_to_all | solution.py:497
  55.8 9.6 %all-to-all-done.1 = bf16[8,150,128]{2,1,0:T(8,128)(2,1)} async-done(((bf16[8,150,128]{2,1,0:T(8,128)(2,1)}), bf16[8,150,128]{2,1,0:T(8,128)(2,1)}, u32[]{:S(2)}, u32[]{:S(2)}) %all-to-all-start.1) | async-done | bytes 307232 | tf_op jit(solution)/shard_map/all_to_all | solution.py:497
  65.5 1.6 %reshape.41 = bf16[48,20,160]{2,1,0:T(8,128)(2,1)S(1)} reshape(bf16[8,150,128]{2,1,0:T(8,128)(2,1)} %all-to-all-done.1) | data formatting | bytes 614400 | tf_op jit(solution)/shard_map/reshape | solution.py:498
  67.3 4.6 %shard_map.98 = (bf16[4,8,24,256]{3,2,1,0:T(8,128)(2,1)}, f32[2,2560,128]{2,1,0:T(8,128)S(1)}) custom-call(bf16[4,8,24,128]{3,2,1,0:T(8,128)(2,1)S(1)} %bitcast.30, bf16[20,48,160]{2,1,0:T(8,128)(2,1)S(1)} %bitcast.28, bf16[20,16,160]{2,1,0:T(8,128)(2,1)S(1)} %pad.4.target, s32[1,160]{1,0:T(1,128)S(1)} %bitcast.33), custom_call_target="tpu_custom_call" | custom-call | flops 40642560 | bytes 3317760 | tf_op jit(solution)/shard_map/pallas_call | solution.py:443
  73.4 3.6 %all-to-all-start.2 = ((bf16[32,24,256]{2,1,0:T(8,128)(2,1)}), bf16[32,24,256]{2,1,0:T(8,128)(2,1)S(1)}, u32[]{:S(2)}, u32[]{:S(2)}) async-start(bf16[32,24,256]{2,1,0:T(8,128)(2,1)} %bitcast.14), calls=%async_computation.2 | async-start | bytes 786432 | tf_op jit(solution)/shard_map/all_to_all | solution.py:456
  77.1 1.7 %copy-done.3 = f32[2,2560,128]{2,1,0:T(8,128)S(1)} copy-done((f32[2,2560,128]{2,1,0:T(8,128)S(1)}, f32[2,2560,128]{2,1,0:T(8,128)}, u32[]{:S(2)}) %copy-start.3) | copy-done | bytes 2621464
  78.8 2.5 %shard_map.101 = bf16[4,8,40,256]{3,2,1,0:T(8,128)(2,1)} custom-call(f32[2,2560,128]{2,1,0:T(8,128)S(1)} %copy-done.3), custom_call_target="tpu_custom_call" | custom-call | flops 40642560 | bytes 3317760 | tf_op jit(solution)/shard_map/pallas_call | solution.py:443
  81.3 9.1 %all-to-all-done.2 = bf16[32,24,256]{2,1,0:T(8,128)(2,1)S(1)} async-done(((bf16[32,24,256]{2,1,0:T(8,128)(2,1)}), bf16[32,24,256]{2,1,0:T(8,128)(2,1)S(1)}, u32[]{:S(2)}, u32[]{:S(2)}) %all-to-all-start.2) | async-done | bytes 393248 | tf_op jit(solution)/shard_map/all_to_all | solution.py:456
  90.5 2.8 %all-to-all-start.3 = ((bf16[32,40,256]{2,1,0:T(8,128)(2,1)}), bf16[32,40,256]{2,1,0:T(8,128)(2,1)S(1)}, u32[]{:S(2)}, u32[]{:S(2)}) async-start(bf16[32,40,256]{2,1,0:T(8,128)(2,1)} %bitcast.17), calls=%async_computation.3 | async-start | bytes 1310720 | tf_op jit(solution)/shard_map/all_to_all | solution.py:456
  93.3 1.5 %collective-permute-start.2 = (bf16[3,48,1440]{2,1,0:T(8,128)(2,1)S(1)}, bf16[3,48,1440]{2,1,0:T(8,128)(2,1)S(1)}, u32[]{:S(2)}, u32[]{:S(2)}) collective-permute-start(bf16[3,48,1440]{2,1,0:T(8,128)(2,1)S(1)} %get-tuple-element.25.inner), channel_id=1, source_target_pairs={{0,1},{1,0},{2,3},{3,2},{4,5},{5,4},{6,7},{7,6},{8,9},{9,8},{10,11... | collective-permute-start | bytes 1244168 | tf_op jit(solution)/shard_map/ppermute | solution.py:37
  94.8 3.4 %collective-permute-start.3 = (bf16[3,48,1440]{2,1,0:T(8,128)(2,1)S(1)}, bf16[3,48,1440]{2,1,0:T(8,128)(2,1)S(1)}, u32[]{:S(2)}, u32[]{:S(2)}) collective-permute-start(bf16[3,48,1440]{2,1,0:T(8,128)(2,1)S(1)} %get-tuple-element.26.outer), channel_id=1, source_target_pairs={{0,7},{1,2},{2,1},{3,4},{4,3},{5,6},{6,5},{7,0},{8,15},{9,10},{10,... | collective-permute-start | bytes 1244168 | tf_op jit(solution)/shard_map/ppermute | solution.py:38
  98.5 23.3 %collective-permute-done.2.near = bf16[3,48,1440]{2,1,0:T(8,128)(2,1)S(1)} collective-permute-done((bf16[3,48,1440]{2,1,0:T(8,128)(2,1)S(1)}, bf16[3,48,1440]{2,1,0:T(8,128)(2,1)S(1)}, u32[]{:S(2)}, u32[]{:S(2)}) %collective-permute-start.2) | collective-permute-done | bytes 414752 | tf_op jit(solution)/shard_map/ppermute | solution.py:37
  121.9 8.2 %shard_map.100 = bf16[2,6,24,1440]{3,2,1,0:T(8,128)(2,1)} custom-call(s32[2]{0:T(128)S(1)} %pad_add_fusion.flags, bf16[4,8,24,256]{3,2,1,0:T(8,128)(2,1)S(1)} %bitcast.29, bf16[3,48,1440]{2,1,0:T(8,128)(2,1)S(1)} %collective-permute-done.2.near, bf16[3,48,1440]{2,1,0:T(8,128)(2,1)S(1)} %collective-permute-done.3.far, ...), custom_call_target="tpu_custom_call" | custom-call | flops 40642560 | bytes 3317760 | tf_op jit(solution)/shard_map/pallas_call | solution.py:443
  130.1 2.6 %shard_map.102 = f32[2,24,20,2,160]{4,3,2,1,0:T(2,128)} custom-call(bf16[4,8,40,256]{3,2,1,0:T(8,128)(2,1)S(1)} %bitcast.27), custom_call_target="tpu_custom_call" | custom-call | flops 40642560 | bytes 3317760 | tf_op jit(solution)/shard_map/pallas_call | solution.py:443
  (36 shorter events, 7.4 us)
Async XLA Ops:
  0.6 11.3 %copy-start.9 = (bf16[2,2,96,24]{3,2,1,0:T(8,128)(2,1)S(1)}, bf16[2,2,96,24]{3,2,1,0:T(8,128)(2,1)}, u32[]{:S(2)}) copy-start(bf16[2,2,96,24]{3,2,1,0:T(8,128)(2,1)} %constant.44.clone.pick) | copy-start | bytes 55300
  0.6 26.0 %copy-start = (bf16[1440,512]{1,0:T(8,128)(2,1)S(1)}, bf16[1440,512]{1,0:T(8,128)(2,1)}, u32[]{:S(2)}) copy-start(bf16[1440,512]{1,0:T(8,128)(2,1)} %constant.43.clone.table) | copy-start | bytes 4423684
  0.7 11.2 %copy-start.1 = (bf16[2,24,6,1440]{3,1,2,0:T(8,128)(2,1)S(1)}, bf16[2,24,6,1440]{3,1,2,0:T(8,128)(2,1)}, u32[]{:S(2)}) copy-start(bf16[2,24,6,1440]{3,1,2,0:T(8,128)(2,1)} %param.8) | copy-start | bytes 2488324
  0.7 11.2 %copy-start.8 = (f32[24,7,7]{0,2,1:T(8,128)S(1)}, f32[24,7,7]{0,2,1:T(8,128)}, u32[]{:S(2)}) copy-start(f32[24,7,7]{0,2,1:T(8,128)} %param.9) | copy-start | bytes 14116
  0.7 11.2 %copy-start.10 = (bf16[24,24]{1,0:T(8,128)(2,1)S(1)}, bf16[24,24]{1,0:T(8,128)(2,1)}, u32[]{:S(2)}) copy-start(bf16[24,24]{1,0:T(8,128)(2,1)} %weight.1) | copy-start | bytes 3460
  3.0 22.9 %collective-permute-start.1 = (bf16[2,3,24,1440]{3,2,1,0:T(8,128)(2,1)}, bf16[2,3,24,1440]{3,2,1,0:T(8,128)(2,1)S(1)}, u32[]{:S(2)}, u32[]{:S(2)}) collective-permute-start(bf16[2,3,24,1440]{3,2,1,0:T(8,128)(2,1)} %get-tuple-element.28), channel_id=1, source_target_pairs={{0,1},{1,0},{2,3},{3,2},{4,5},{5,4},{6,7},{7,6},{8,9},{9,8},{10,11... | collective-permute-start | bytes 1244168 | tf_op jit(solution)/shard_map/ppermute | solution.py:37
  6.0 24.6 %collective-permute-start = (bf16[2,3,24,1440]{3,2,1,0:T(8,128)(2,1)}, bf16[2,3,24,1440]{3,2,1,0:T(8,128)(2,1)S(1)}, u32[]{:S(2)}, u32[]{:S(2)}) collective-permute-start(bf16[2,3,24,1440]{3,2,1,0:T(8,128)(2,1)} %get-tuple-element.29), channel_id=1, source_target_pairs={{0,7},{1,2},{2,1},{3,4},{4,3},{5,6},{6,5},{7,0},{8,15},{9,10},{10,... | collective-permute-start | bytes 1244168 | tf_op jit(solution)/shard_map/ppermute | solution.py:38
  25.8 0.8 copy-start.6
  26.6 1.0 copy-start.7
  27.6 14.8 %copy-start.12 = (bf16[6,8,3200]{2,1,0:T(8,128)(2,1)S(1)}, bf16[6,8,3200]{2,1,0:T(8,128)(2,1)}, u32[]{:S(2)}) copy-start(bf16[6,8,3200]{2,1,0:T(8,128)(2,1)} %reshape.37) | copy-start | bytes 921604
  30.6 0.8 copy-start.4
  31.4 1.0 copy-start.5
  36.3 31.0 %copy-start.11 = (s32[160]{0:T(256)S(1)}, s32[160]{0:T(256)}, u32[]{:S(2)}) copy-start(s32[160]{0:T(256)} %param.13) | copy-start | bytes 1924
  36.3 14.3 %all-to-all-start = ((bf16[32,24,128]{2,1,0:T(8,128)(2,1)}), bf16[32,24,128]{2,1,0:T(8,128)(2,1)S(1)}, u32[]{:S(2)}, u32[]{:S(2)}) async-start(bf16[32,24,128]{2,1,0:T(8,128)(2,1)} %bitcast.8), calls=%async_computation | async-start | bytes 393216 | tf_op jit(solution)/shard_map/all_to_all | solution.py:456
  50.6 14.9 %all-to-all-start.1 = ((bf16[8,150,128]{2,1,0:T(8,128)(2,1)}), bf16[8,150,128]{2,1,0:T(8,128)(2,1)}, u32[]{:S(2)}, u32[]{:S(2)}) async-start(bf16[8,150,128]{2,1,0:T(8,128)(2,1)} %copy.15), calls=%async_computation.1 | async-start | bytes 622592 | tf_op jit(solution)/shard_map/all_to_all | solution.py:497
  71.9 1.5 %copy-start.2 = (f32[2,2560,128]{2,1,0:T(8,128)}, f32[2,2560,128]{2,1,0:T(8,128)S(1)}, u32[]{:S(2)}) copy-start(f32[2,2560,128]{2,1,0:T(8,128)S(1)} %get-tuple-element.27.grads) | copy-start | bytes 7864324
  73.4 17.1 %all-to-all-start.2 = ((bf16[32,24,256]{2,1,0:T(8,128)(2,1)}), bf16[32,24,256]{2,1,0:T(8,128)(2,1)S(1)}, u32[]{:S(2)}, u32[]{:S(2)}) async-start(bf16[32,24,256]{2,1,0:T(8,128)(2,1)} %bitcast.14), calls=%async_computation.2 | async-start | bytes 786432 | tf_op jit(solution)/shard_map/all_to_all | solution.py:456
  77.1 1.7 %copy-start.3 = (f32[2,2560,128]{2,1,0:T(8,128)S(1)}, f32[2,2560,128]{2,1,0:T(8,128)}, u32[]{:S(2)}) copy-start(f32[2,2560,128]{2,1,0:T(8,128)} %copy-done.2) | copy-start | bytes 7864324
  90.5 39.6 %all-to-all-start.3 = ((bf16[32,40,256]{2,1,0:T(8,128)(2,1)}), bf16[32,40,256]{2,1,0:T(8,128)(2,1)S(1)}, u32[]{:S(2)}, u32[]{:S(2)}) async-start(bf16[32,40,256]{2,1,0:T(8,128)(2,1)} %bitcast.17), calls=%async_computation.3 | async-start | bytes 1310720 | tf_op jit(solution)/shard_map/all_to_all | solution.py:456
  93.3 28.6 %collective-permute-start.2 = (bf16[3,48,1440]{2,1,0:T(8,128)(2,1)S(1)}, bf16[3,48,1440]{2,1,0:T(8,128)(2,1)S(1)}, u32[]{:S(2)}, u32[]{:S(2)}) collective-permute-start(bf16[3,48,1440]{2,1,0:T(8,128)(2,1)S(1)} %get-tuple-element.25.inner), channel_id=1, source_target_pairs={{0,1},{1,0},{2,3},{3,2},{4,5},{5,4},{6,7},{7,6},{8,9},{9,8},{10,11... | collective-permute-start | bytes 1244168 | tf_op jit(solution)/shard_map/ppermute | solution.py:37
  94.8 27.0 %collective-permute-start.3 = (bf16[3,48,1440]{2,1,0:T(8,128)(2,1)S(1)}, bf16[3,48,1440]{2,1,0:T(8,128)(2,1)S(1)}, u32[]{:S(2)}, u32[]{:S(2)}) collective-permute-start(bf16[3,48,1440]{2,1,0:T(8,128)(2,1)S(1)} %get-tuple-element.26.outer), channel_id=1, source_target_pairs={{0,7},{1,2},{2,1},{3,4},{4,3},{5,6},{6,5},{7,0},{8,15},{9,10},{10,... | collective-permute-start | bytes 1244168 | tf_op jit(solution)/shard_map/ppermute | solution.py:38
